TPU v7x, 32 devices: a whole 2x2x4 slice. The times are simulated.
32 devices in a mesh: groups: 2 (over x), dev: 16 (over z, y, core).
Axes of the slice: x: 2, y: 2, z: 4, core: 2. Of those that a mesh axis runs over, the one named last changes fastest.
Arguments:
- hidden_in: bfloat16 [512, 4096], P(('groups', 'dev')), parts along dimension 0, may hold values from -2 to 2
- queries: bfloat16 [512, 4096], P(('groups', 'dev')), parts along dimension 0, may hold values from -80 to 80
- fresh_key_value: bfloat16 [512, 2, 256], P(('groups', 'dev')), parts along dimension 0, may hold values from -6 to 6
- segment_key_cache: bfloat16 [4096, 16, 256], P(('groups', 'dev')), parts along dimension 0, may hold values from -6 to 6
- segment_value_cache: bfloat16 [4096, 16, 256], P(('groups', 'dev')), parts along dimension 0, may hold values from -6 to 6
- segment_owner_row: int32 [4096], P(('groups', 'dev')), parts along dimension 0, may hold values from 0 to 255, as said below
- segment_length: int32 [4096], P(('groups', 'dev')), parts along dimension 0, may hold values from 1 to 16
- expert_ids: int32 [512, 8], P(('groups', 'dev')), parts along dimension 0, may hold values from 0 to 15, all different within a row; in each aligned block of 16 rows (0 to 15, 16 to 31, ...) at most 8 rows name the same one
- gate_score: int32 [512, 8], P(('groups', 'dev')), parts along dimension 0, may hold values from 0 to 11
- out_proj: bfloat16 [4096, 4096], P('dev'), may hold values from -0.09375 to 0.09375
- norm_gain: bfloat16 [4096], replicated, may hold values from 0.099609375 to 1.8984375
- w_gate: bfloat16 [16, 4096, 768], P('dev'), may hold values from -0.09375 to 0.09375
- w_up: bfloat16 [16, 4096, 768], P('dev'), may hold values from -0.09375 to 0.09375
- w_down: bfloat16 [16, 768, 4096], P('dev'), may hold values from -0.21875 to 0.21875
Outputs:
- layer_out: bfloat16 [512, 4096], P(('groups', 'dev')), parts along dimension 0
There are 2 independent parts, one for each index of `groups`. A program takes and returns all parts, laid end to end along the dimension named above; an argument that names none is the same for every part. Nothing has to cross between parts.
Inputs may be any that keep to these rules, and one draw needn't show every extreme that they name: `segment_owner_row`: segment rows never fall along the segments, and every row owns at least one segment. `expert_ids`: each row names 8 different experts; among the rows of one device no expert is named by more than 8 rows.
All inputs are finite; a program needn't handle non-finite values.
Results may differ from a plain program's by a relative error of at most 0.024.
Values may be sent and summed in bfloat16 or wider, within the bound.
No kernel may reach another device: no remote copies, remote signals or barrier semaphores. Data moves between devices by JAX's collectives and lax.ppermute only.
A program may use at most 128 MiB of HBM per device.

v0:
```python
import jax
import jax.numpy as jnp
from jax import lax
from jax.sharding import PartitionSpec as P

HEAD_SIZE = 128
TOP = 8
HQ = 32


def segment_terms(query_rows, key_cache, value_cache, seg_lengths):
    seg_count = key_cache.shape[0]
    seg_width = key_cache.shape[1]
    kv_heads = key_cache.shape[2] // HEAD_SIZE
    group_size = HQ // kv_heads
    query_blocks = query_rows.reshape(seg_count, kv_heads, group_size, HEAD_SIZE)
    key_blocks = key_cache.reshape(seg_count, seg_width, kv_heads, HEAD_SIZE)
    value_blocks = value_cache.reshape(seg_count, seg_width, kv_heads, HEAD_SIZE)
    scores = jnp.einsum(
        "skgd,stkd->skgt", query_blocks, key_blocks, preferred_element_type=jnp.float32
    ) * HEAD_SIZE ** (-0.5)
    live_slots = (
        jnp.arange(seg_width, dtype=jnp.int32)[None, None, None, :]
        < seg_lengths[:, None, None, None]
    )
    scores = jnp.where(live_slots, scores, -jnp.inf)
    seg_max = jnp.max(scores, axis=3)
    prob_rows = jnp.exp(scores - seg_max[..., None])
    seg_sum = jnp.sum(prob_rows, axis=3)
    seg_out = jnp.einsum(
        "skgt,stkd->skgd",
        prob_rows.astype(jnp.bfloat16),
        value_blocks,
        preferred_element_type=jnp.float32,
    )
    return (
        seg_max.reshape(seg_count, HQ),
        seg_sum.reshape(seg_count, HQ),
        seg_out.reshape(seg_count, HQ, HEAD_SIZE),
    )


def reduce_rows(seg_max, seg_sum, seg_out, row_ids, row_count):
    row_max = jax.ops.segment_max(seg_max, row_ids, num_segments=row_count)
    weight = jnp.exp(seg_max - jnp.take(row_max, row_ids, axis=0))
    row_sum = jax.ops.segment_sum(seg_sum * weight, row_ids, num_segments=row_count)
    row_out = jax.ops.segment_sum(seg_out * weight[..., None], row_ids, num_segments=row_count)
    return (row_max, row_sum, row_out)


def fold_own(row_max, row_sum, row_out, query_own, kv_own):
    row_count = query_own.shape[0]
    kv_heads = kv_own.shape[2] // HEAD_SIZE
    group_size = HQ // kv_heads
    query_blocks = query_own.reshape(row_count, kv_heads, group_size, HEAD_SIZE).astype(jnp.float32)
    new_key = kv_own[:, 0].reshape(row_count, kv_heads, 1, HEAD_SIZE).astype(jnp.float32)
    new_value = kv_own[:, 1].reshape(row_count, kv_heads, 1, HEAD_SIZE).astype(jnp.float32)
    own_score = jnp.sum(query_blocks * new_key, axis=3).reshape(row_count, HQ) * HEAD_SIZE ** (-0.5)
    merged = jnp.maximum(row_max, own_score)
    old_weight = jnp.exp(row_max - merged)
    new_weight = jnp.exp(own_score - merged)
    total_sum = row_sum * old_weight + new_weight
    value_term = jnp.broadcast_to(new_value, (row_count, kv_heads, group_size, HEAD_SIZE)).reshape(
        row_count, HQ, HEAD_SIZE
    )
    merged_out = row_out * old_weight[..., None] + value_term * new_weight[..., None]
    return (merged, total_sum, merged_out)


def finish(row_max, row_sum, row_out):
    floored = jnp.maximum(row_sum, 1.0)
    block_lse = row_max + jnp.log(floored)
    block_share = (row_out / floored[..., None]).astype(jnp.bfloat16)
    return (block_lse, block_share)


def on_device(
    hidden_in,
    queries,
    fresh_key_value,
    segment_key_cache,
    segment_value_cache,
    segment_owner_row,
    segment_length,
    expert_ids,
    gate_score,
    out_proj,
    norm_gain,
    w_gate,
    w_up,
    w_down,
):
    devices = lax.axis_size("dev")
    my_index = lax.axis_index("dev")
    row_dev = hidden_in.shape[0]
    row_total = row_dev * devices
    per_device = HQ // devices
    own_first = my_index * row_dev
    query_all = lax.all_gather(queries, "dev", axis=0, tiled=True)
    query_rows = jnp.take(query_all, segment_owner_row, axis=0)
    seg_max, seg_sum, seg_out = segment_terms(
        query_rows, segment_key_cache, segment_value_cache, segment_length
    )
    row_max, row_sum, row_out = reduce_rows(seg_max, seg_sum, seg_out, segment_owner_row, row_total)
    own_max, own_sum, own_out = fold_own(
        lax.dynamic_slice_in_dim(row_max, own_first, row_dev, 0),
        lax.dynamic_slice_in_dim(row_sum, own_first, row_dev, 0),
        lax.dynamic_slice_in_dim(row_out, own_first, row_dev, 0),
        queries,
        fresh_key_value,
    )
    row_max = lax.dynamic_update_slice_in_dim(row_max, own_max, own_first, 0)
    row_sum = lax.dynamic_update_slice_in_dim(row_sum, own_sum, own_first, 0)
    row_out = lax.dynamic_update_slice_in_dim(row_out, own_out, own_first, 0)
    table_lse, table_share = finish(row_max, row_sum, row_out)
    got_lse = lax.all_to_all(table_lse[None], "dev", split_axis=2, concat_axis=0, tiled=True)
    got_share = lax.all_to_all(table_share[None], "dev", split_axis=2, concat_axis=0, tiled=True)
    best_lse = jnp.max(got_lse, axis=0)
    weight = jnp.exp(got_lse - best_lse[None])
    denominator = jnp.sum(weight, axis=0)
    numerator = jnp.sum(weight[..., None] * got_share.astype(jnp.float32), axis=0)
    attn_local = (
        (numerator / denominator[..., None])
        .astype(jnp.bfloat16)
        .reshape(row_total, per_device * HEAD_SIZE)
    )
    projected = lax.psum_scatter(
        jnp.dot(attn_local, out_proj, preferred_element_type=jnp.float32).astype(jnp.bfloat16),
        "dev",
        scatter_dimension=0,
        tiled=True,
    ).astype(jnp.float32)
    mixed_f32 = (hidden_in.astype(jnp.float32) + projected).astype(jnp.bfloat16).astype(jnp.float32)
    normed = (
        mixed_f32
        * lax.rsqrt(jnp.mean(mixed_f32 * mixed_f32, axis=1, keepdims=True) + 1e-06)
        * norm_gain.astype(jnp.float32)
    ).astype(jnp.bfloat16)
    gate_probs = jnp.exp(gate_score.astype(jnp.float32) / 4.0)
    gate_probs = gate_probs / jnp.sum(gate_probs, axis=1, keepdims=True)
    capacity = row_dev // 2
    slot_total = devices * capacity
    flat_ids = expert_ids.reshape(-1)
    one_hot = (flat_ids[:, None] == jnp.arange(devices, dtype=jnp.int32)[None, :]).astype(jnp.int32)
    slot_rank = jnp.sum((jnp.cumsum(one_hot, axis=0) - one_hot) * one_hot, axis=1)
    slot_index = (flat_ids * capacity + slot_rank).reshape(row_dev, TOP)
    slot_iota = jnp.arange(slot_total, dtype=jnp.int32)
    combine_weights = jnp.sum(
        jnp.where(slot_index[:, :, None] == slot_iota[None, None, :], gate_probs[:, :, None], 0.0),
        axis=1,
    )
    dispatch = jnp.any(slot_index[None, :, :] == slot_iota[:, None, None], axis=2).astype(
        jnp.bfloat16
    )
    outgoing = (
        jnp.dot(dispatch, normed, preferred_element_type=jnp.float32)
        .astype(jnp.bfloat16)
        .reshape(devices, capacity, normed.shape[1])
    )
    arrived = lax.all_to_all(outgoing, "dev", split_axis=0, concat_axis=0, tiled=True)
    sources = arrived.shape[0]
    slot_count = arrived.shape[1]
    flat_tokens = arrived.reshape(sources * slot_count, arrived.shape[2])
    gate_proj = jnp.dot(flat_tokens, w_gate[0], preferred_element_type=jnp.float32)
    up_proj = jnp.dot(flat_tokens, w_up[0], preferred_element_type=jnp.float32)
    activated = (jax.nn.silu(gate_proj) * up_proj).astype(jnp.bfloat16)
    result = jnp.dot(activated, w_down[0], preferred_element_type=jnp.float32).astype(jnp.bfloat16)
    returned = lax.all_to_all(
        result.reshape(sources, slot_count, result.shape[1]),
        "dev",
        split_axis=0,
        concat_axis=0,
        tiled=True,
    )
    moe_sum = jnp.dot(
        combine_weights,
        returned.reshape(slot_total, returned.shape[2]).astype(jnp.float32),
        precision=lax.Precision.HIGHEST,
        preferred_element_type=jnp.float32,
    )
    return (mixed_f32 + moe_sum).astype(jnp.bfloat16)


def solution(mesh):
    placed = (
        P(("groups", "dev"), None),
        P(("groups", "dev"), None),
        P(("groups", "dev"), None, None),
        P(("groups", "dev"), None, None),
        P(("groups", "dev"), None, None),
        P(("groups", "dev")),
        P(("groups", "dev")),
        P(("groups", "dev"), None),
        P(("groups", "dev"), None),
        P("dev", None),
        P(),
        P("dev", None, None),
        P("dev", None, None),
        P("dev", None, None),
    )
    return jax.shard_map(
        on_device, mesh=mesh, in_specs=placed, out_specs=P(("groups", "dev"), None), check_vma=False
    )
```

profile of v0, /device:TPU:0, one launch (start us, length us, event | category | flops | bytes accessed | tf_op | source)
XLA Modules:
  0.0 307.8 jit_solution(7378402143327455642)
XLA Ops:
  6.5 0.7 all-gather.2.cloned.1.call-update
  7.3 0.9 convert_bitcast_fusion
  8.2 0.1 copy.140
  8.2 0.8 slice_convert_fusion
  9.1 0.2 multiply_reduce_fusion
  9.3 0.1 mul.110
  9.3 0.7 compare_select_fusion
  10.0 0.7 compare_and_fusion
  10.7 0.7 iota_compare_fusion.3
  11.3 42.4 %all-gather.2.cloned.1.call-done = bf16[256,4096]{1,0:T(8,128)(2,1)} async-done(((bf16[16,4096]{1,0:T(8,128)(2,1)}), bf16[256,4096]{1,0:T(8,128)(2,1)}) %all-gather.2.cloned.1.call-update) | async-done | bytes 2097168 | tf_op jit(solution)/shard_map/all_gather | solution.py:99
  53.7 4.1 %gather_fusion = bf16[128,4096]{1,0:T(8,128)(2,1)S(1)} fusion(bf16[256,4096]{1,0:T(8,128)(2,1)} %all-gather.2.cloned.1.call-done, s32[1024]{0:T(1024)S(1)} %pad_clamp_fusion), kind=kCustom, calls=%fused_computation | custom fusion | bytes 2097664 | tf_op jit(solution)/shard_map/jit(_take)/gather | solution.py:100
  57.8 0.2 copy.139
  58.0 3.3 %fusion.25 = f32[128,2,16,16]{2,3,1,0:T(8,128)} fusion(bf16[128,2,16,128]{3,2,1,0:T(8,128)(2,1)S(1)} %bitcast.96, pred[128]{0:T(512)(128)(4,1)S(1)} %compare_and_fusion, bf16[128,16,256]{2,1,0:T(8,128)(2,1)} %param.17), kind=kOutput, calls=%fused_computation.28 | convolution fusion | flops 17301504 | bytes 2359424 | tf_op jit(solution)/shard_map/skgd,stkd->skgt/dot_general | solution.py:19
  61.4 2.7 copy.115
  64.1 0.1 fusion.47
  64.2 0.1 fusion.49
  64.3 1.4 copy.125
  65.7 0.1 copy.118
  65.8 1.6 scatter_custom_fusion
  67.4 0.6 gather_fusion.1
  68.1 0.1 copy.122
  68.2 0.7 copy.127
  68.9 0.1 copy.123
  69.0 1.6 scatter_custom_fusion.1
  70.6 0.6 add_dynamic-update-slice_fusion
  71.2 0.7 add_bitcast_fusion
  71.9 1.6 copy.124
  73.5 3.5 %all-to-all-start = ((f32[1,256,32]{1,0,2:T(1,128)}), f32[1,256,32]{1,0,2:T(1,128)S(1)}, u32[]{:S(2)}, u32[]{:S(2)}) async-start(f32[1,256,32]{1,0,2:T(1,128)} %copy.124), calls=%async_computation | async-start | bytes 65536 | tf_op jit(solution)/shard_map/all_to_all | solution.py:116
  77.0 1.9 fusion.22
  78.9 0.0 copy-start.8
  79.0 2.0 bitcast_multiply_fusion.1
  81.0 2.5 broadcast_in_dim.99
  83.4 19.0 %scatter_fusion = f32[256,32,128]{2,1,0:T(8,128)} fusion(f32[256,32,128]{2,1,0:T(8,128)} %broadcast_in_dim.99, s32[128]{0:T(128)S(1)} %copy-done.8, f32[128,32,128]{2,1,0:T(8,128)} %bitcast_multiply_fusion.1), kind=kCustom, calls=%fused_computation.4 | custom fusion | flops 524288 | bytes 6291968 | tf_op jit(solution)/shard_map/scatter-add | solution.py:47
  102.4 1.8 constant_dynamic-update-slice_fusion
  104.3 2.9 fusion.15
  107.1 2.2 copy.128
  109.3 4.7 %all-to-all-start.1 = ((bf16[1,256,32,128]{3,1,0,2:T(8,128)(2,1)}), bf16[1,256,32,128]{3,1,0,2:T(8,128)(2,1)}, u32[]{:S(2)}, u32[]{:S(2)}) async-start(bf16[1,256,32,128]{3,1,0,2:T(8,128)(2,1)} %copy.128), calls=%async_computation.1 | async-start | bytes 4194304 | tf_op jit(solution)/shard_map/all_to_all | solution.py:117
  114.0 0.2 reduce-scatter.2.cloned.1.call-start
  114.3 40.7 %all-to-all-done.1 = bf16[1,256,32,128]{3,1,0,2:T(8,128)(2,1)} async-done(((bf16[1,256,32,128]{3,1,0,2:T(8,128)(2,1)}), bf16[1,256,32,128]{3,1,0,2:T(8,128)(2,1)}, u32[]{:S(2)}, u32[]{:S(2)}) %all-to-all-start.1) | async-done | bytes 2097184 | tf_op jit(solution)/shard_map/all_to_all | solution.py:117
  155.1 2.5 fusion.14
  157.6 0.0 copy-start.6
  157.6 0.1 divide_convert_fusion.1
  157.7 0.1 copy.130
  157.9 2.1 convolution_convert_fusion
  159.9 0.0 reduce-scatter.2.cloned.1.call-update
  160.0 0.1 copy.131
  160.1 0.1 eq.20
  160.1 0.1 fusion.54
  160.2 0.2 reduce_window_sum.11
  160.4 0.2 select_reduce_fusion.1
  160.6 0.1 reduce_sum.79
  160.7 0.0 copy-done.6
  160.7 0.1 fusion.59
  160.8 67.6 %reduce-scatter.2.cloned.1.call-done = bf16[16,4096]{1,0:T(8,128)(2,1)} async-done(((bf16[256,4096]{1,0:T(8,128)(2,1)}), bf16[16,4096]{1,0:T(8,128)(2,1)}) %reduce-scatter.2.cloned.1.call-update) | async-done | bytes 131088 | tf_op jit(solution)/shard_map/reduce_scatter | solution.py:127
  228.5 1.1 fusion.43
  229.5 1.4 fusion.9
  230.9 28.1 %all_to_all.37 = bf16[16,8,4096]{2,1,0:T(8,128)(2,1)S(1)} all-to-all(bf16[16,8,4096]{2,1,0:T(8,128)(2,1)S(1)} %fusion.9), channel_id=1, replica_groups=mesh['groups'=2,'dev'=16] {'dev'}, dimensions={0} | all-to-all | bytes 2097152 | tf_op jit(solution)/shard_map/all_to_all | solution.py:160
  259.0 3.8 %fusion.4 = f32[128,768]{1,0:T(8,128)S(1)} fusion(bf16[1,4096,768]{2,1,0:T(8,128)(2,1)} %param.25, bf16[16,8,4096]{2,1,0:T(8,128)(2,1)S(1)} %all_to_all.37), kind=kOutput, calls=%fused_computation.9 | convolution fusion | flops 805306368 | bytes 7733248 | tf_op jit(solution)/shard_map/dot_general | solution.py:164
  262.8 8.1 %fusion.10 = bf16[16,8,4096]{2,1,0:T(8,128)(2,1)} fusion(bf16[1,768,4096]{2,1,0:T(8,128)(2,1)} %param.27, bf16[1,4096,768]{2,1,0:T(8,128)(2,1)} %param.26, bf16[16,8,4096]{2,1,0:T(8,128)(2,1)S(1)} %all_to_all.37, f32[128,768]{1,0:T(8,128)S(1)} %fusion.4), kind=kOutput, calls=%fused_computation.15 | convolution fusion | flops 1611726848 | bytes 15073280 | tf_op jit(solution)/shard_map/dot_general | solution.py:167
  270.9 5.0 %all-to-all-start.3 = ((bf16[16,8,4096]{2,1,0:T(8,128)(2,1)}), bf16[16,8,4096]{2,1,0:T(8,128)(2,1)S(1)}, u32[]{:S(2)}, u32[]{:S(2)}) async-start(bf16[16,8,4096]{2,1,0:T(8,128)(2,1)} %fusion.10), calls=%async_computation.4 | async-start | bytes 2097152 | tf_op jit(solution)/shard_map/all_to_all | solution.py:168
  276.0 0.1 copy.133
  276.0 0.1 select_reduce_fusion
  276.2 22.6 %all-to-all-done.3 = bf16[16,8,4096]{2,1,0:T(8,128)(2,1)S(1)} async-done(((bf16[16,8,4096]{2,1,0:T(8,128)(2,1)}), bf16[16,8,4096]{2,1,0:T(8,128)(2,1)S(1)}, u32[]{:S(2)}, u32[]{:S(2)}) %all-to-all-start.3) | async-done | bytes 1048608 | tf_op jit(solution)/shard_map/all_to_all | solution.py:168
  298.8 2.1 fusion.13
  (27 shorter events, 0.2 us)
Async XLA Ops:
  6.5 151.3 %copy-start = (bf16[256,4096]{1,0:T(8,128)(2,1)S(1)}, bf16[256,4096]{1,0:T(8,128)(2,1)}, u32[]{:S(2)}) copy-start(bf16[256,4096]{1,0:T(8,128)(2,1)} %param.23) | copy-start | bytes 6291460
  6.5 47.2 %all-gather.2.cloned.1.call-start = ((), (), s32[]{:S(2)}) async-start(), calls=%async_computation.5 | async-start | bytes 2228224 | tf_op jit(solution)/shard_map/all_gather | solution.py:99
  71.9 7.0 %copy-start.2 = (f32[128,32]{1,0:T(8,128)S(1)}, f32[128,32]{1,0:T(8,128)}, u32[]{:S(2)}) copy-start(f32[128,32]{1,0:T(8,128)} %copy.127) | copy-start | bytes 49156
  73.5 35.8 %all-to-all-start = ((f32[1,256,32]{1,0,2:T(1,128)}), f32[1,256,32]{1,0,2:T(1,128)S(1)}, u32[]{:S(2)}, u32[]{:S(2)}) async-start(f32[1,256,32]{1,0,2:T(1,128)} %copy.124), calls=%async_computation | async-start | bytes 65536 | tf_op jit(solution)/shard_map/all_to_all | solution.py:116
  78.9 4.5 %copy-start.8 = (s32[128]{0:T(128)S(1)}, s32[128]{0:T(128)}, u32[]{:S(2)}) copy-start(s32[128]{0:T(128)} %param.19) | copy-start | bytes 1540
  83.4 19.0 %copy-start.3 = (f32[16,32]{1,0:T(8,128)S(1)}, f32[16,32]{1,0:T(8,128)}, u32[]{:S(2)}) copy-start(f32[16,32]{1,0:T(8,128)} %get-tuple-element.8) | copy-start | bytes 6148
  83.4 19.0 %copy-start.4 = (f32[16,32]{1,0:T(8,128)S(1)}, f32[16,32]{1,0:T(8,128)}, u32[]{:S(2)}) copy-start(f32[16,32]{1,0:T(8,128)} %get-tuple-element.9) | copy-start | bytes 6148
  109.3 45.7 %all-to-all-start.1 = ((bf16[1,256,32,128]{3,1,0,2:T(8,128)(2,1)}), bf16[1,256,32,128]{3,1,0,2:T(8,128)(2,1)}, u32[]{:S(2)}, u32[]{:S(2)}) async-start(bf16[1,256,32,128]{3,1,0,2:T(8,128)(2,1)} %copy.128), calls=%async_computation.1 | async-start | bytes 4194304 | tf_op jit(solution)/shard_map/all_to_all | solution.py:117
  114.0 114.4 %reduce-scatter.2.cloned.1.call-start = ((), (), s32[]{:S(2)}) async-start(), calls=%async_computation.6 | async-start | bytes 2228224 | tf_op jit(solution)/shard_map/reduce_scatter | solution.py:127
  155.1 4.9 %copy-start.7 = (s32[16,8]{0,1:T(8,128)S(1)}, s32[16,8]{0,1:T(8,128)}, u32[]{:S(2)}) copy-start(s32[16,8]{0,1:T(8,128)} %param.21) | copy-start | bytes 1540
  157.6 3.1 %copy-start.6 = (bf16[4096]{0:T(1024)(128)(2,1)S(1)}, bf16[4096]{0:T(1024)(128)(2,1)}, u32[]{:S(2)}) copy-start(bf16[4096]{0:T(1024)(128)(2,1)} %param.24) | copy-start | bytes 24580
  157.6 70.9 %copy-start.1 = (bf16[16,4096]{1,0:T(8,128)(2,1)S(1)}, bf16[16,4096]{1,0:T(8,128)(2,1)}, u32[]{:S(2)}) copy-start(bf16[16,4096]{1,0:T(8,128)(2,1)} %param.14) | copy-start | bytes 393220
  262.8 13.1 %copy-start.5 = (s32[16,8]{0,1:T(8,128)S(1)}, s32[16,8]{0,1:T(8,128)}, u32[]{:S(2)}) copy-start(s32[16,8]{0,1:T(8,128)} %param.22) | copy-start | bytes 1540
  270.9 27.9 %all-to-all-start.3 = ((bf16[16,8,4096]{2,1,0:T(8,128)(2,1)}), bf16[16,8,4096]{2,1,0:T(8,128)(2,1)S(1)}, u32[]{:S(2)}, u32[]{:S(2)}) async-start(bf16[16,8,4096]{2,1,0:T(8,128)(2,1)} %fusion.10), calls=%async_computation.4 | async-start | bytes 2097152 | tf_op jit(solution)/shard_map/all_to_all | solution.py:168
Sparse Core Ops, SparseCore 0:
  9.5 44.1 all-gather.1
  160.1 68.3 reduce-scatter.1
where the time goes:
time: 310 us; the launch traced here: 308 us
  waiting for transfers between devices  174 us (56%)
  other arithmetic  38.8 us (13%)
  blocking collectives  28.1 us (9%)
  matrix products  22.7 us (7%)
  local copies, waits for them, and re-layouts  16.9 us (5%)
  between operations  13.7 us (4%)
  starting transfers between devices  13.4 us (4%)
    reduce_scatter x1, waiting for transfers between devices, on_device(): lax.psum_scatter(jnp.dot(attn_local, out_proj, preferred_element_type=jnp...  67.6 us
    all_gather x1, waiting for transfers between devices, on_device(): query_all = lax.all_gather(queries, 'dev', axis=0, tiled=True)  42.4 us
    all_to_all x1, waiting for transfers between devices, on_device(): lax.all_to_all(table_share[None], 'dev', split_axis=2, concat_axis=0, til...  40.7 us
    all_to_all x1, blocking collectives, on_device(): lax.all_to_all(outgoing, 'dev', split_axis=0, concat_axis=0, tiled=True)  28.1 us
    all_to_all x1, waiting for transfers between devices, on_device(): lax.all_to_all(result.reshape(sources, slot_count, result.shape[1]), 'dev...  22.6 us
    scatter-add x1, other arithmetic, reduce_rows(): jax.ops.segment_sum(seg_out * weight[..., None], row_ids, num_segments=ro...  19 us
    dot_general x1, matrix products, on_device(): jnp.dot(activated, w_down[0], preferred_element_type=jnp.float32)  8.06 us
  transfers between devices with their start and end apart: 5, of which 4 were waited for; matrix products, arithmetic and copies ran while one was open for 12% of the time, Pallas kernels for 0%

commit v1 on v0

v1 whole, which is shorter than its diff:
```python
import functools

import jax
import jax.numpy as jnp
from jax import lax
from jax.experimental import pallas as pl
from jax.experimental.pallas import tpu as pltpu
from jax.sharding import PartitionSpec as P

HEAD_SIZE = 128
LANES = 128
NEG = -1e30
BF = jnp.bfloat16
F32 = jnp.float32


def xor_masks(devices):
    far = devices // 4
    return [c + 2 * y + 4 * z for c in range(2) for y in range(2) for z in range(far)]


def swap(x, mask, devices):
    return lax.ppermute(x, "dev", [(i, i ^ mask) for i in range(devices)])


def gather_blocks(x, devices):
    far = devices // 4
    z_order = sorted(range(1, far), reverse=True)
    z_parts = {0: x}
    for i in z_order:
        z_parts[i] = swap(x, 4 * i, devices)
    near = [z_parts[i] for i in range(far)]
    near = near + [swap(b, 2, devices) for b in near]
    return near + [swap(b, 1, devices) for b in near]


def scatter_blocks(x, devices):
    far = devices // 4
    parts = x.reshape((2, 2, far) + x.shape[1:])
    pieces = []
    for i in range(far - 1, -1, -1):
        pair = parts[0, :, i] + swap(parts[1, :, i], 1, devices)
        mine = pair[0] + swap(pair[1], 2, devices)
        pieces.append(swap(mine, 4 * i, devices) if i else mine)
    return pieces


def lane_pick(vec, lane_iota, index):
    return jnp.sum(jnp.where(lane_iota == index, vec, 0.0), axis=1, keepdims=True)


def attend_kernel(
    me_ref, owner_row_ref, owner_col_ref, bias_ref, k_ref, v_ref, *rest,
    devices, row_dev, width, q_heads, kv_heads, slots, seg_width,
):
    pieces = rest[:devices]
    out_ref, q_scr, o_scr, m_scr = rest[devices:]
    me = me_ref[0]
    masks = xor_masks(devices)
    rows = devices * row_dev
    segs = owner_row_ref.shape[1]
    hp = q_heads // devices
    per_kv = q_heads // kv_heads
    qk = q_heads * HEAD_SIZE
    ext = qk + 2 * kv_heads * HEAD_SIZE
    hots = []
    per_lane = LANES // row_dev
    lane = lax.broadcasted_iota(jnp.int32, (1, LANES), 1)
    for c in range(rows // LANES):
        gid = jnp.zeros((1, LANES), jnp.int32)
        for i in range(per_lane):
            base = (me ^ masks[c * per_lane + i]) * row_dev - i * row_dev
            gid = jnp.where(lane // row_dev == i, lane + base, gid)
        hots.append((owner_col_ref[...] == gid).astype(F32).astype(BF))
    hot = jnp.concatenate(hots, axis=1)
    step = 512
    for c in range(qk // step):
        block = jnp.concatenate([p[:, c * step : (c + 1) * step] for p in pieces], axis=0)
        q_scr[:, c * step : (c + 1) * step] = jnp.dot(
            hot, block, preferred_element_type=F32
        ).astype(BF)
    group = 16
    wide = group * seg_width
    r_i = lax.broadcasted_iota(jnp.int32, (group, wide), 0)
    c_i = lax.broadcasted_iota(jnp.int32, (group, wide), 1)
    eye_bias = jnp.where(r_i == c_i // seg_width, 0.0, NEG)
    ones = jnp.ones((wide, HEAD_SIZE), BF)
    stat_lanes = m_scr.shape[1]
    m_lane = lax.broadcasted_iota(jnp.int32, (group, stat_lanes), 1)
    for g in range(segs // group):
        bias = eye_bias + bias_ref[g : g + 1, :]
        m_acc = jnp.zeros((group, stat_lanes), F32)
        for kv in range(kv_heads):
            lo = kv * per_kv
            q_tile = jnp.concatenate(
                [
                    q_scr[g * group : (g + 1) * group, (lo + h) * HEAD_SIZE : (lo + h + 1) * HEAD_SIZE]
                    for h in range(per_kv)
                ],
                axis=0,
            )
            k_tile = k_ref[g * wide : (g + 1) * wide, kv * HEAD_SIZE : (kv + 1) * HEAD_SIZE]
            v_tile = v_ref[g * wide : (g + 1) * wide, kv * HEAD_SIZE : (kv + 1) * HEAD_SIZE]
            s = lax.dot_general(
                q_tile, k_tile, (((1,), (1,)), ((), ())), preferred_element_type=F32
            ) * HEAD_SIZE ** (-0.5)
            s = s.reshape(per_kv, group, wide) + bias[None]
            m = jnp.max(s, axis=2, keepdims=True)
            prob = jnp.exp(s - m).reshape(per_kv * group, wide).astype(BF)
            o = jnp.dot(prob, jnp.concatenate([v_tile, ones], axis=1), preferred_element_type=F32)
            o_scr[lo : lo + per_kv, g * group : (g + 1) * group, :] = o.reshape(
                per_kv, group, 2 * HEAD_SIZE
            ).astype(BF)
            for h in range(per_kv):
                m_acc = jnp.where(m_lane == lo + h, m[h], m_acc)
        m_scr[g * group : (g + 1) * group, :] = m_acc
    m_t = m_scr[...].T
    ext_sum = jnp.zeros((1, LANES), F32)
    for p in range(devices):
        vec = pieces[p][0:1, ext : ext + LANES].astype(F32)
        ext_sum = ext_sum + jnp.where((me ^ masks[p]) == me - 1, vec, 0.0)
    prev_last = 16.0 * lane_pick(ext_sum, lane, 18) + lane_pick(ext_sum, lane, 19)
    owner = owner_row_ref[...]
    first = jnp.min(owner.astype(F32), axis=1, keepdims=True)
    repeated = jnp.logical_and(first == prev_last, me > 0)
    slot = jnp.where(
        jnp.logical_and(owner.astype(F32) == first, repeated), rows + me, owner
    )
    mask = lax.broadcasted_iota(jnp.int32, (slots, segs), 0) == slot
    stats = devices * 8
    st_lane = lax.broadcasted_iota(jnp.int32, (slots, stats), 1)
    max_acc = jnp.zeros((slots, stats), F32)
    sum_acc = jnp.ones((slots, stats), F32)
    for d in range(devices):
        pos_mask = me ^ d
        far = devices // 4
        pos = (pos_mask & 1) * (2 * far) + ((pos_mask >> 1) & 1) * far + (pos_mask >> 2)
        for hh in range(hp):
            h = d * hp + hh
            m_row = m_t[h : h + 1, :]
            mm = jnp.where(mask, m_row, NEG)
            r_max = jnp.maximum(jnp.max(mm, axis=1, keepdims=True), 0.1 * NEG)
            weight = jnp.exp(mm - r_max).astype(BF)
            r = jnp.dot(weight, o_scr[h], preferred_element_type=F32)
            r_sum = jnp.maximum(r[:, HEAD_SIZE:], 1.0)
            out_ref[pos, 0:slots, hh * HEAD_SIZE : (hh + 1) * HEAD_SIZE] = (
                r[:, :HEAD_SIZE] / r_sum
            ).astype(BF)
            here = jnp.zeros((slots, stats), jnp.bool_)
            for part in range(3):
                here = jnp.logical_or(here, st_lane == d * 8 + part * hp + hh)
            max_acc = jnp.where(here, r_max, max_acc)
            sum_acc = jnp.where(here, r_sum[:, 0:1], sum_acc)
    owned = jnp.max(jnp.where(mask, 1.0, 0.0), axis=1, keepdims=True)
    lse = jnp.where(owned > 0.0, max_acc + jnp.log(sum_acc), 0.0)
    hi = lse.astype(BF).astype(F32)
    rest1 = lse - hi
    mid = rest1.astype(BF).astype(F32)
    low = rest1 - mid
    part = (st_lane % 8) // hp
    lse = jnp.where(part == 0, hi, jnp.where(part == 1, mid, low))
    pad = -(-slots // width) * width - slots
    pad_t = -(-slots // LANES) * LANES - slots
    if pad_t:
        lse = jnp.concatenate([lse, jnp.zeros((pad_t, stats), F32)], axis=0)
    lse_t = lse.T
    if pad > pad_t:
        lse_t = jnp.concatenate([lse_t, jnp.zeros((stats, pad - pad_t), F32)], axis=1)
    tail = out_ref.shape[1] - slots
    for d in range(devices):
        pos_mask = me ^ d
        far = devices // 4
        pos = (pos_mask & 1) * (2 * far) + ((pos_mask >> 1) & 1) * far + (pos_mask >> 2)
        strips = [
            lse_t[d * 8 : (d + 1) * 8, b * width : (b + 1) * width]
            for b in range((slots + pad) // width)
        ]
        if len(strips) * 8 < tail:
            strips.append(jnp.zeros((tail - len(strips) * 8, width), F32))
        out_ref[pos, slots:, :] = jnp.concatenate(strips, axis=0).astype(BF)


def combine_kernel(
    me_ref, w_ref, *rest, devices, row_dev, width, q_heads, kv_heads, slots,
):
    pieces = rest[:devices]
    far = devices // 4
    shares = rest[devices : devices + far]
    out_ref, x_scr, l_scr = rest[devices + far :]
    me = me_ref[0]
    masks = xor_masks(devices)
    rows = devices * row_dev
    hp = q_heads // devices
    qk = q_heads * HEAD_SIZE
    ext = qk + 2 * kv_heads * HEAD_SIZE
    total = shares[0][...].astype(F32)
    for s in shares[1:]:
        total = total + s[...].astype(F32)
    x_scr[...] = total
    strips = -(-slots // width)
    lse8 = jnp.concatenate(
        [total[slots + 8 * b : slots + 8 * (b + 1), :] for b in range(strips)], axis=1
    )
    lse_rows = [
        lse8[hh : hh + 1, :] + lse8[hp + hh : hp + hh + 1, :] + lse8[2 * hp + hh : 2 * hp + hh + 1, :]
        for hh in range(hp)
    ]
    head_pos = lax.broadcasted_iota(jnp.int32, (LANES, rows), 0)
    spread = jnp.zeros((LANES, rows), F32)
    for hh in range(hp):
        spread = jnp.where(head_pos == hh, lse_rows[hh][:, :rows], spread)
    l_scr[...] = spread.T
    lane = lax.broadcasted_iota(jnp.int32, (1, LANES), 1)
    first = jnp.full((1, LANES), -1.0, F32)
    before = jnp.full((1, LANES), -2.0, F32)
    for p in range(devices):
        vec = pieces[p][0:1, ext : ext + LANES].astype(F32)
        dev = me ^ masks[p]
        first = jnp.where(
            lane == dev, 16.0 * lane_pick(vec, lane, 16) + lane_pick(vec, lane, 17), first
        )
        before = jnp.where(
            lane == dev + 1, 16.0 * lane_pick(vec, lane, 18) + lane_pick(vec, lane, 19), before
        )
    again = jnp.where(jnp.logical_and(first == before, lane < devices), first, -1.0).astype(jnp.int32)
    row_id = jnp.concatenate(
        [
            lax.broadcasted_iota(jnp.int32, (row_dev, LANES), 0) + (me ^ masks[p]) * row_dev
            for p in range(devices)
        ],
        axis=0,
    )
    share = jnp.concatenate(
        [x_scr[pl.ds((me ^ masks[p]) * row_dev, row_dev), :] for p in range(devices)], axis=0
    )
    lse_col = jnp.concatenate(
        [l_scr[pl.ds((me ^ masks[p]) * row_dev, row_dev), :] for p in range(devices)], axis=0
    )
    kv = (me * hp) // (q_heads // kv_heads)
    q_at = pl.multiple_of(me * width, LANES)
    k_at = pl.multiple_of(qk + kv * HEAD_SIZE, LANES)
    v_at = pl.multiple_of(qk + (kv_heads + kv) * HEAD_SIZE, LANES)
    q = jnp.concatenate([p[:, pl.ds(q_at, width)] for p in pieces], axis=0).astype(F32)
    key = jnp.concatenate([p[:, pl.ds(k_at, HEAD_SIZE)] for p in pieces], axis=0).astype(F32)
    val = jnp.concatenate([p[:, pl.ds(v_at, HEAD_SIZE)] for p in pieces], axis=0).astype(F32)
    chosen = row_id == again
    heads = []
    for hh in range(hp):
        cut = slice(hh * HEAD_SIZE, (hh + 1) * HEAD_SIZE)
        own = jnp.sum(q[:, cut] * key, axis=1, keepdims=True) * HEAD_SIZE ** (-0.5)
        lse_p = lse_col[:, hh : hh + 1]
        extra = jnp.where(chosen, lse_rows[hh][:, rows : rows + LANES], NEG)
        top = jnp.maximum(jnp.maximum(lse_p, own), jnp.max(extra, axis=1, keepdims=True))
        w_p = jnp.exp(lse_p - top)
        w_o = jnp.exp(own - top)
        w_e = jnp.exp(extra - top)
        more = jnp.concatenate(
            [x_scr[rows:slots, cut], jnp.zeros((LANES - devices, HEAD_SIZE), F32)], axis=0
        )
        num = w_p * share[:, cut] + w_o * val + jnp.dot(
            w_e, more, precision=lax.Precision.HIGHEST, preferred_element_type=F32
        )
        den = w_p + w_o + jnp.sum(w_e, axis=1, keepdims=True)
        heads.append((num / den).astype(BF))
    attn = heads[0] if hp == 1 else jnp.concatenate(heads, axis=1)
    step = 1024
    for c in range(w_ref.shape[1] // step):
        cut = slice(c * step, (c + 1) * step)
        r = jnp.dot(attn, w_ref[:, cut], preferred_element_type=F32).astype(BF)
        for p in range(devices):
            out_ref[p, :, cut] = r[p * row_dev : (p + 1) * row_dev]


def expert_kernel(me_ref, *rest, devices, row_dev, top):
    pieces = rest[:devices]
    ext = rest[devices : 2 * devices]
    gate_ref, up_ref, down_ref, out_ref, x_scr, acc = rest[2 * devices :]
    i = pl.program_id(0)

    @pl.when(i == 0)
    def _():
        for p in range(devices):
            x_scr[p * row_dev : (p + 1) * row_dev, :] = pieces[p][...]
        acc[...] = jnp.zeros(acc.shape, F32)

    x = x_scr[...]
    a = jnp.dot(x, gate_ref[...], preferred_element_type=F32)
    b = jnp.dot(x, up_ref[...], preferred_element_type=F32)
    h = (a / (1.0 + jnp.exp(-a)) * b).astype(BF)
    acc[...] += jnp.dot(h, down_ref[...], preferred_element_type=F32)

    @pl.when(i == pl.num_programs(0) - 1)
    def _():
        me = me_ref[0]
        lane = lax.broadcasted_iota(jnp.int32, (row_dev, LANES), 1)
        for p in range(devices):
            e = ext[p][...].astype(F32)
            score = jnp.where(jnp.logical_and(lane >= top, lane < 2 * top), jnp.exp(e * 0.25), 0.0)
            total = jnp.sum(score, axis=1, keepdims=True)
            weight = jnp.zeros((row_dev, 1), F32)
            for k in range(top):
                weight = weight + jnp.where(
                    e[:, k : k + 1] == me.astype(F32), score[:, top + k : top + k + 1], 0.0
                )
            weight = weight / total
            y = acc[p * row_dev : (p + 1) * row_dev, :].astype(BF).astype(F32)
            out_ref[p] = (y * weight).astype(BF)


def on_device(
    hidden_in, queries, fresh_key_value, segment_key_cache, segment_value_cache,
    segment_owner_row, segment_length, expert_ids, gate_score, out_proj, norm_gain,
    w_gate, w_up, w_down,
):
    devices = lax.axis_size("dev")
    me = lax.axis_index("dev").astype(jnp.int32).reshape(1)
    row_dev, d_model = hidden_in.shape
    rows = row_dev * devices
    q_heads = queries.shape[1] // HEAD_SIZE
    kv_heads = fresh_key_value.shape[2] // HEAD_SIZE
    segs, seg_width = segment_key_cache.shape[:2]
    top = expert_ids.shape[1]
    width = out_proj.shape[0]
    slots = rows + devices
    strips = -(-slots // width)
    tall = slots + -(-strips // 2) * 16
    first = segment_owner_row[0]
    last = segment_owner_row[segs - 1]
    ends = jnp.stack([first // 16, first % 16, last // 16, last % 16]).astype(BF)
    extra = jnp.concatenate(
        [
            expert_ids.astype(BF),
            gate_score.astype(BF),
            jnp.broadcast_to(ends[None], (row_dev, 4)),
            jnp.zeros((row_dev, LANES - 2 * top - 4), BF),
        ],
        axis=1,
    )
    payload = jnp.concatenate(
        [queries, fresh_key_value.reshape(row_dev, -1), extra], axis=1
    )
    group = 16
    slot_ids = jnp.arange(seg_width, dtype=jnp.int32)
    bias = jnp.where(slot_ids[None] < segment_length[:, None], 0.0, NEG).astype(F32)
    bias = bias.reshape(segs // group, group * seg_width)
    owner_row = segment_owner_row.reshape(1, segs)
    owner_col = jnp.broadcast_to(segment_owner_row[:, None], (segs, LANES))
    pieces = gather_blocks(payload, devices)
    smem = pl.BlockSpec(memory_space=pltpu.SMEM)
    vmem = pl.BlockSpec(memory_space=pltpu.VMEM)
    stat_lanes = LANES
    params = pltpu.CompilerParams(vmem_limit_bytes=56 * 1024 * 1024)
    table = pl.pallas_call(
        functools.partial(
            attend_kernel, devices=devices, row_dev=row_dev, width=width, q_heads=q_heads,
            kv_heads=kv_heads, slots=slots, seg_width=seg_width,
        ),
        out_shape=jax.ShapeDtypeStruct((devices, tall, width), BF),
        in_specs=[smem] + [vmem] * (5 + devices),
        out_specs=vmem,
        scratch_shapes=[
            pltpu.VMEM((segs, q_heads * HEAD_SIZE), BF),
            pltpu.VMEM((q_heads, segs, 2 * HEAD_SIZE), BF),
            pltpu.VMEM((segs, stat_lanes), F32),
        ],
        compiler_params=params,
        name="attend",
    )(
        me, owner_row, owner_col, bias,
        segment_key_cache.reshape(segs * seg_width, -1),
        segment_value_cache.reshape(segs * seg_width, -1),
        *pieces,
    )
    shares = scatter_blocks(table, devices)
    part = pl.pallas_call(
        functools.partial(
            combine_kernel, devices=devices, row_dev=row_dev, width=width, q_heads=q_heads,
            kv_heads=kv_heads, slots=slots,
        ),
        out_shape=jax.ShapeDtypeStruct((devices, row_dev, d_model), BF),
        in_specs=[smem] + [vmem] * (1 + devices + devices // 4),
        out_specs=vmem,
        scratch_shapes=[pltpu.VMEM((tall, width), F32), pltpu.VMEM((rows, LANES), F32)],
        compiler_params=params,
        name="combine",
    )(me, out_proj, *pieces, *shares)
    projected = sum(p.astype(F32) for p in scatter_blocks(part, devices))
    mixed = (hidden_in.astype(F32) + projected).astype(BF).astype(F32)
    normed = (
        mixed
        * lax.rsqrt(jnp.mean(mixed * mixed, axis=1, keepdims=True) + 1e-06)
        * norm_gain.astype(F32)
    ).astype(BF)
    tokens = gather_blocks(normed, devices)
    ff = w_gate.shape[2]
    tile = 256
    ext_at = (q_heads + 2 * kv_heads) * HEAD_SIZE // LANES
    moe = pl.pallas_call(
        functools.partial(expert_kernel, devices=devices, row_dev=row_dev, top=top),
        grid=(ff // tile,),
        out_shape=jax.ShapeDtypeStruct((devices, row_dev, d_model), BF),
        in_specs=[smem]
        + [pl.BlockSpec((row_dev, d_model), lambda i: (0, 0))] * devices
        + [pl.BlockSpec((row_dev, LANES), lambda i: (0, ext_at))] * devices
        + [
            pl.BlockSpec((None, d_model, tile), lambda i: (0, 0, i)),
            pl.BlockSpec((None, d_model, tile), lambda i: (0, 0, i)),
            pl.BlockSpec((None, tile, d_model), lambda i: (0, i, 0)),
        ],
        out_specs=pl.BlockSpec((devices, row_dev, d_model), lambda i: (0, 0, 0)),
        scratch_shapes=[pltpu.VMEM((rows, d_model), BF), pltpu.VMEM((rows, d_model), F32)],
        compiler_params=params,
        name="experts",
    )(me, *tokens, *pieces, w_gate, w_up, w_down)
    summed = sum(p.astype(F32) for p in scatter_blocks(moe, devices))
    return (mixed + summed).astype(BF)


def solution(mesh):
    both = ("groups", "dev")
    placed = (
        P(both, None), P(both, None), P(both, None, None), P(both, None, None),
        P(both, None, None), P(both), P(both), P(both, None), P(both, None),
        P("dev", None), P(), P("dev", None, None), P("dev", None, None), P("dev", None, None),
    )
    return jax.shard_map(
        on_device, mesh=mesh, in_specs=placed, out_specs=P(both, None), check_vma=False
    )
```

time: 310 us -> 169 us (0.55)
  waiting for transfers between devices: 174 us -> 62.2 us
  starting transfers between devices: 13.4 us -> 56 us
  other arithmetic: 38.8 us -> 4.32 us
  Pallas kernels: 0 us -> 28.4 us
  blocking collectives: 28.1 us -> 0 us
  matrix products: 22.7 us -> 0 us
  between operations: 13.7 us -> 5.63 us
  local copies, waits for them, and re-layouts: 16.9 us -> 12.4 us
    reduce_scatter x1 -> x0, waiting for transfers between devices: 67.6 us -> none  [on_device(): lax.psum_scatter(jnp.dot(attn_local, out_proj, preferred_element_type=jnp...]
    all_to_all x3 -> x0, waiting for transfers between devices: 63.4 us -> none  [the longest x1 40.7 us: on_device(): lax.all_to_all(table_share[None], 'dev', split_axis=2, concat_axis=0, til...]
    ppermute x0 -> x63, waiting for transfers between devices: none -> 62.2 us  [swap(): return lax.ppermute(x, 'dev', [(i, i ^ mask) for i in range(devices)])]
    ppermute x0 -> x63, starting transfers between devices: none -> 56 us  [swap(): return lax.ppermute(x, 'dev', [(i, i ^ mask) for i in range(devices)])]
    all_gather x1 -> x0, waiting for transfers between devices: 42.4 us -> none  [on_device(): query_all = lax.all_gather(queries, 'dev', axis=0, tiled=True)]
    pallas_call x0 -> x3, Pallas kernels: none -> 28.4 us  [the longest x1 13.9 us: on_device(): pl.pallas_call(functools.partial(expert_kernel, devices=devices, row_dev=...]
    all_to_all x1 -> x0, blocking collectives: 28.1 us -> none  [on_device(): lax.all_to_all(outgoing, 'dev', split_axis=0, concat_axis=0, tiled=True)]
    dot_general x7 -> x0, matrix products: 22.7 us -> none  [the longest x1 8.06 us: on_device(): jnp.dot(activated, w_down[0], preferred_element_type=jnp.float32)]
  transfers between devices with their start and end apart: 5 -> 63, of which waited for: 4 -> 41; matrix products, arithmetic and copies ran while one was open for 12% -> 1% of each run, Pallas kernels for 0% -> 0%
where the time goes in v1:
time: 169 us
  waiting for transfers between devices  62.2 us (37%)
  starting transfers between devices  56 us (33%)
  Pallas kernels  28.4 us (17%)
  local copies, waits for them, and re-layouts  12.4 us (7%)
  between operations  5.63 us (3%)
  other arithmetic  4.32 us (3%)
    ppermute x63, waiting for transfers between devices, swap(): return lax.ppermute(x, 'dev', [(i, i ^ mask) for i in range(devices)])  62.2 us
    ppermute x63, starting transfers between devices, swap(): return lax.ppermute(x, 'dev', [(i, i ^ mask) for i in range(devices)])  56 us
    pallas_call x1, Pallas kernels, on_device(): pl.pallas_call(functools.partial(expert_kernel, devices=devices, row_dev=...  13.9 us
    pallas_call x1, Pallas kernels, on_device(): pl.pallas_call(functools.partial(attend_kernel, devices=devices, row_dev=...  8.9 us
    pallas_call x1, Pallas kernels, on_device(): pl.pallas_call(functools.partial(combine_kernel, devices=devices, row_dev...  5.56 us
    squeeze x3, local copies, waits for them, and re-layouts, scatter_blocks(): pair = parts[0, :, i] + swap(parts[1, :, i], 1, devices)  4.31 us
  transfers between devices with their start and end apart: 63, of which 41 were waited for; matrix products, arithmetic and copies ran while one was open for 1% of the time, Pallas kernels for 0%

profile of v1, /device:TPU:0, one launch (start us, length us, event | category | flops | bytes accessed | tf_op | source)
XLA Modules:
  0.0 168.9 jit_solution(264762396939398240)
XLA Ops:
  0.0 1.3 fusion.28
  6.4 0.7 copy.93
  7.2 0.7 convert_element_type.54
  7.9 0.7 convert_element_type.55
  8.8 1.0 concatenate.8.rest_0_.rest_16_
  9.8 3.1 %collective-permute-start = (bf16[16,4736]{1,0:T(8,128)(2,1)S(1)}, bf16[16,4736]{1,0:T(8,128)(2,1)S(1)}, u32[]{:S(2)}, u32[]{:S(2)}) collective-permute-start(bf16[16,4736]{1,0:T(8,128)(2,1)S(1)} %concatenate.8.rest_0_.rest_16_), channel_id=1, source_target_pairs={{0,4},{1,5},{2,6},{3,7},{4,0},{5,1},{6,2},{7,3},{8,12},{9,13},{10,... | collective-permute-start | bytes 454664 | tf_op jit(solution)/shard_map/ppermute | solution.py:23
  12.9 2.6 %collective-permute-start.1 = (bf16[16,4736]{1,0:T(8,128)(2,1)S(1)}, bf16[16,4736]{1,0:T(8,128)(2,1)S(1)}, u32[]{:S(2)}, u32[]{:S(2)}) collective-permute-start(bf16[16,4736]{1,0:T(8,128)(2,1)S(1)} %concatenate.8.rest_0_.rest_16_), channel_id=1, source_target_pairs={{0,8},{1,9},{2,10},{3,11},{4,12},{5,13},{6,14},{7,15},{8,0},{9,1},... | collective-permute-start | bytes 454664 | tf_op jit(solution)/shard_map/ppermute | solution.py:23
  15.5 1.7 %collective-permute-start.3 = (bf16[16,4736]{1,0:T(8,128)(2,1)S(1)}, bf16[16,4736]{1,0:T(8,128)(2,1)S(1)}, u32[]{:S(2)}, u32[]{:S(2)}) collective-permute-start(bf16[16,4736]{1,0:T(8,128)(2,1)S(1)} %concatenate.8.rest_0_.rest_16_), channel_id=1, source_target_pairs={{0,2},{1,3},{2,0},{3,1},{4,6},{5,7},{6,4},{7,5},{8,10},{9,11},{10,... | collective-permute-start | bytes 454664 | tf_op jit(solution)/shard_map/ppermute | solution.py:23
  17.3 1.8 %collective-permute-done.rest_1_.rest_17_ = bf16[16,4736]{1,0:T(8,128)(2,1)S(1)} collective-permute-done((bf16[16,4736]{1,0:T(8,128)(2,1)S(1)}, bf16[16,4736]{1,0:T(8,128)(2,1)S(1)}, u32[]{:S(2)}, u32[]{:S(2)}) %collective-permute-start) | collective-permute-done | bytes 151584 | tf_op jit(solution)/shard_map/ppermute | solution.py:23
  19.0 1.7 %collective-permute-start.4 = (bf16[16,4736]{1,0:T(8,128)(2,1)S(1)}, bf16[16,4736]{1,0:T(8,128)(2,1)S(1)}, u32[]{:S(2)}, u32[]{:S(2)}) collective-permute-start(bf16[16,4736]{1,0:T(8,128)(2,1)S(1)} %collective-permute-done.rest_1_.rest_17_), channel_id=1, source_target_pairs={{0,2},{1,3},{2,0},{3,1},{4,6},{5,7},{6,4},{7,5},{8,10},{9,11},{10,... | collective-permute-start | bytes 454664 | tf_op jit(solution)/shard_map/ppermute | solution.py:23
  20.8 6.4 %collective-permute-done.1.rest_2_.rest_18_ = bf16[16,4736]{1,0:T(8,128)(2,1)S(1)} collective-permute-done((bf16[16,4736]{1,0:T(8,128)(2,1)S(1)}, bf16[16,4736]{1,0:T(8,128)(2,1)S(1)}, u32[]{:S(2)}, u32[]{:S(2)}) %collective-permute-start.1) | collective-permute-done | bytes 151584 | tf_op jit(solution)/shard_map/ppermute | solution.py:23
  27.1 1.5 collective-permute-start.5
  29.7 0.7 lt.37
  30.8 1.5 collective-permute-done.5.rest_6_.rest_22_
  32.3 1.6 collective-permute-done.6.rest_7_.rest_23_
  34.6 0.6 compare_select_fusion.bias_ref
  35.8 1.4 broadcast_in_dim.16.owner_col_ref
  37.4 8.9 %attend.1 = bf16[16,288,256]{2,1,0:T(8,128)(2,1)} custom-call(s32[1]{0:T(128)} %bitcast.me_ref, s32[1,128]{1,0:T(1,128)} %bitcast.222, s32[128,128]{1,0:T(8,128)} %broadcast_in_dim.16.owner_col_ref, f32[8,256]{1,0:T(8,128)} %compare_select_fusion.bias_ref, bf16[2048,256]{1,0:T(8,128)(2,1)} %bitcast.218, bf16[2048,256]{1,0:T(8,128)(2,1)} %bitcast.219, ...), custom_call_target="tpu_custom_call" | custom-call | tf_op jit(solution)/shard_map/attend/pallas_call | solution.py:353
  46.3 1.5 slice_bitcast_fusion
  50.8 1.6 collective-permute-start.25
  53.0 1.6 collective-permute-start.19
  55.1 5.6 %collective-permute-done.22 = bf16[288,256]{1,0:T(8,128)(2,1)S(1)} collective-permute-done((bf16[288,256]{1,0:T(8,128)(2,1)S(1)}, bf16[288,256]{1,0:T(8,128)(2,1)S(1)}, u32[]{:S(2)}, u32[]{:S(2)}) %collective-permute-start.22) | collective-permute-done | bytes 147488 | tf_op jit(solution)/shard_map/ppermute | solution.py:23
  60.7 1.1 collective-permute-start.23
  61.9 2.0 %collective-permute-done.19 = bf16[288,256]{1,0:T(8,128)(2,1)S(1)} collective-permute-done((bf16[288,256]{1,0:T(8,128)(2,1)S(1)}, bf16[288,256]{1,0:T(8,128)(2,1)S(1)}, u32[]{:S(2)}, u32[]{:S(2)}) %collective-permute-start.19) | collective-permute-done | bytes 147488 | tf_op jit(solution)/shard_map/ppermute | solution.py:23
  63.9 1.9 %collective-permute-start.20 = (bf16[288,256]{1,0:T(8,128)(2,1)S(1)}, bf16[288,256]{1,0:T(8,128)(2,1)S(1)}, u32[]{:S(2)}, u32[]{:S(2)}) collective-permute-start(bf16[288,256]{1,0:T(8,128)(2,1)S(1)} %fusion.18), channel_id=1, source_target_pairs={{0,8},{1,9},{2,10},{3,11},{4,12},{5,13},{6,14},{7,15},{8,0},{9,1},... | collective-permute-start | bytes 442376 | tf_op jit(solution)/shard_map/ppermute | solution.py:23
  66.3 2.4 %collective-permute-start.17 = (bf16[288,256]{1,0:T(8,128)(2,1)S(1)}, bf16[288,256]{1,0:T(8,128)(2,1)S(1)}, u32[]{:S(2)}, u32[]{:S(2)}) collective-permute-start(bf16[288,256]{1,0:T(8,128)(2,1)S(1)} %fusion.19), channel_id=1, source_target_pairs={{0,12},{1,13},{2,14},{3,15},{4,8},{5,9},{6,10},{7,11},{8,4},{9,5},... | collective-permute-start | bytes 442376 | tf_op jit(solution)/shard_map/ppermute | solution.py:23
  68.7 0.7 fusion.16.rest_19_
  69.4 7.4 %collective-permute-done.20.rest_17_ = bf16[288,256]{1,0:T(8,128)(2,1)S(1)} collective-permute-done((bf16[288,256]{1,0:T(8,128)(2,1)S(1)}, bf16[288,256]{1,0:T(8,128)(2,1)S(1)}, u32[]{:S(2)}, u32[]{:S(2)}) %collective-permute-start.20) | collective-permute-done | bytes 147488 | tf_op jit(solution)/shard_map/ppermute | solution.py:23
  76.8 0.6 copy-done.21
  77.5 0.6 copy-done.22
  78.1 5.6 %combine.1 = bf16[16,16,4096]{2,1,0:T(8,128)(2,1)} custom-call(s32[1]{0:T(128)} %bitcast.me_ref, bf16[256,4096]{1,0:T(8,128)(2,1)} %w_ref.1, bf16[16,4736]{1,0:T(8,128)(2,1)} %copy-done.3, bf16[16,4736]{1,0:T(8,128)(2,1)} %copy-done.4, bf16[16,4736]{1,0:T(8,128)(2,1)} %copy-done.5, bf16[16,4736]{1,0:T(8,128)(2,1)} %copy-done.6, bf16[16,4736]{1,0:T(8,128)(2,1)} %copy-done.7, ...), custom_call_target="tpu_custom_call" | custom-call | tf_op jit(solution)/shard_map/combine/pallas_call | solution.py:375
  83.7 1.4 slice_bitcast_fusion.22
  88.0 1.6 collective-permute-start.27
  90.1 1.6 collective-permute-start.33
  92.3 2.1 %collective-permute-done.27 = bf16[16,4096]{1,0:T(8,128)(2,1)S(1)} collective-permute-done((bf16[16,4096]{1,0:T(8,128)(2,1)S(1)}, bf16[16,4096]{1,0:T(8,128)(2,1)S(1)}, u32[]{:S(2)}, u32[]{:S(2)}) %collective-permute-start.27) | collective-permute-done | bytes 131104 | tf_op jit(solution)/shard_map/ppermute | solution.py:23
  94.4 1.9 %collective-permute-start.28 = (bf16[16,4096]{1,0:T(8,128)(2,1)S(1)}, bf16[16,4096]{1,0:T(8,128)(2,1)S(1)}, u32[]{:S(2)}, u32[]{:S(2)}) collective-permute-start(bf16[16,4096]{1,0:T(8,128)(2,1)S(1)} %fusion.27), channel_id=1, source_target_pairs={{0,12},{1,13},{2,14},{3,15},{4,8},{5,9},{6,10},{7,11},{8,4},{9,5},... | collective-permute-start | bytes 393224 | tf_op jit(solution)/shard_map/ppermute | solution.py:23
  96.3 0.9 collective-permute-done.30
  97.2 2.7 %collective-permute-start.31 = (bf16[16,4096]{1,0:T(8,128)(2,1)S(1)}, bf16[16,4096]{1,0:T(8,128)(2,1)S(1)}, u32[]{:S(2)}, u32[]{:S(2)}) collective-permute-start(bf16[16,4096]{1,0:T(8,128)(2,1)S(1)} %fusion.26), channel_id=1, source_target_pairs={{0,8},{1,9},{2,10},{3,11},{4,12},{5,13},{6,14},{7,15},{8,0},{9,1},... | collective-permute-start | bytes 393224 | tf_op jit(solution)/shard_map/ppermute | solution.py:23
  100.0 1.9 %collective-permute-start.34 = (bf16[16,4096]{1,0:T(8,128)(2,1)S(1)}, bf16[16,4096]{1,0:T(8,128)(2,1)S(1)}, u32[]{:S(2)}, u32[]{:S(2)}) collective-permute-start(bf16[16,4096]{1,0:T(8,128)(2,1)S(1)} %fusion.25), channel_id=1, source_target_pairs={{0,4},{1,5},{2,6},{3,7},{4,0},{5,1},{6,2},{7,3},{8,12},{9,13},{10,... | collective-permute-start | bytes 393224 | tf_op jit(solution)/shard_map/ppermute | solution.py:23
  102.1 5.9 %collective-permute-done.31 = bf16[16,4096]{1,0:T(8,128)(2,1)S(1)} collective-permute-done((bf16[16,4096]{1,0:T(8,128)(2,1)S(1)}, bf16[16,4096]{1,0:T(8,128)(2,1)S(1)}, u32[]{:S(2)}, u32[]{:S(2)}) %collective-permute-start.31) | collective-permute-done | bytes 131104 | tf_op jit(solution)/shard_map/ppermute | solution.py:23
  108.5 2.9 %collective-permute-start.38 = (bf16[16,4096]{1,0:T(8,128)(2,1)S(1)}, bf16[16,4096]{1,0:T(8,128)(2,1)S(1)}, u32[]{:S(2)}, u32[]{:S(2)}) collective-permute-start(bf16[16,4096]{1,0:T(8,128)(2,1)S(1)} %fusion.6.rest_0_), channel_id=1, source_target_pairs={{0,8},{1,9},{2,10},{3,11},{4,12},{5,13},{6,14},{7,15},{8,0},{9,1},... | collective-permute-start | bytes 393224 | tf_op jit(solution)/shard_map/ppermute | solution.py:23
  111.3 1.5 collective-permute-start.39
  112.8 1.5 collective-permute-start.40
  114.7 1.5 collective-permute-start.41
  116.2 4.7 %collective-permute-done.38.rest_2_ = bf16[16,4096]{1,0:T(8,128)(2,1)S(1)} collective-permute-done((bf16[16,4096]{1,0:T(8,128)(2,1)S(1)}, bf16[16,4096]{1,0:T(8,128)(2,1)S(1)}, u32[]{:S(2)}, u32[]{:S(2)}) %collective-permute-start.38) | collective-permute-done | bytes 131104 | tf_op jit(solution)/shard_map/ppermute | solution.py:23
  120.9 1.5 collective-permute-start.42
  123.5 2.3 %collective-permute-done.42.rest_6_ = bf16[16,4096]{1,0:T(8,128)(2,1)S(1)} collective-permute-done((bf16[16,4096]{1,0:T(8,128)(2,1)S(1)}, bf16[16,4096]{1,0:T(8,128)(2,1)S(1)}, u32[]{:S(2)}, u32[]{:S(2)}) %collective-permute-start.42) | collective-permute-done | bytes 131104 | tf_op jit(solution)/shard_map/ppermute | solution.py:23
  125.9 1.5 collective-permute-done.43.rest_7_
  128.0 0.7 collective-permute-done.49.rest_13_
  129.6 0.7 copy-done.37
  130.3 13.9 %experts.1 = bf16[16,16,4096]{2,1,0:T(8,128)(2,1)} custom-call(s32[1]{0:T(128)} %bitcast.me_ref, bf16[16,4096]{1,0:T(8,128)(2,1)} %copy-done.19, bf16[16,4096]{1,0:T(8,128)(2,1)} %copy-done.23, bf16[16,4096]{1,0:T(8,128)(2,1)} %copy-done.24, bf16[16,4096]{1,0:T(8,128)(2,1)} %copy-done.25, bf16[16,4096]{1,0:T(8,128)(2,1)} %copy-done.26, ...), custom_call_target="tpu_custom_call" | custom-call | tf_op jit(solution)/shard_map/experts/pallas_call | solution.py:398
  144.2 1.4 slice_bitcast_fusion.8
  148.5 1.5 collective-permute-start.53
  150.0 0.7 collective-permute-start.56
  150.7 1.5 collective-permute-start.59
  152.1 0.7 collective-permute-start.62
  152.8 2.1 %collective-permute-done.53 = bf16[16,4096]{1,0:T(8,128)(2,1)S(1)} collective-permute-done((bf16[16,4096]{1,0:T(8,128)(2,1)S(1)}, bf16[16,4096]{1,0:T(8,128)(2,1)S(1)}, u32[]{:S(2)}, u32[]{:S(2)}) %collective-permute-start.53) | collective-permute-done | bytes 131104 | tf_op jit(solution)/shard_map/ppermute | solution.py:23
  154.9 2.4 %collective-permute-start.54 = (bf16[16,4096]{1,0:T(8,128)(2,1)S(1)}, bf16[16,4096]{1,0:T(8,128)(2,1)S(1)}, u32[]{:S(2)}, u32[]{:S(2)}) collective-permute-start(bf16[16,4096]{1,0:T(8,128)(2,1)S(1)} %fusion.23), channel_id=1, source_target_pairs={{0,12},{1,13},{2,14},{3,15},{4,8},{5,9},{6,10},{7,11},{8,4},{9,5},... | collective-permute-start | bytes 393224 | tf_op jit(solution)/shard_map/ppermute | solution.py:23
  157.7 1.4 collective-permute-start.57
  159.1 1.4 collective-permute-done.59
  160.6 0.9 collective-permute-start.60
  161.4 1.3 collective-permute-done.62
  163.2 4.9 %collective-permute-done.57 = bf16[16,4096]{1,0:T(8,128)(2,1)S(1)} collective-permute-done((bf16[16,4096]{1,0:T(8,128)(2,1)S(1)}, bf16[16,4096]{1,0:T(8,128)(2,1)S(1)}, u32[]{:S(2)}, u32[]{:S(2)}) %collective-permute-start.57) | collective-permute-done | bytes 131104 | tf_op jit(solution)/shard_map/ppermute | solution.py:23
  168.1 0.8 fusion.7
  (195 shorter events, 19.2 us)
Async XLA Ops:
  9.8 27.4 %copy-start.3 = (bf16[16,4736]{1,0:T(8,128)(2,1)}, bf16[16,4736]{1,0:T(8,128)(2,1)S(1)}, u32[]{:S(2)}) copy-start(bf16[16,4736]{1,0:T(8,128)(2,1)S(1)} %concatenate.8.rest_0_.rest_16_) | copy-start | bytes 454660
  9.8 9.2 %collective-permute-start = (bf16[16,4736]{1,0:T(8,128)(2,1)S(1)}, bf16[16,4736]{1,0:T(8,128)(2,1)S(1)}, u32[]{:S(2)}, u32[]{:S(2)}) collective-permute-start(bf16[16,4736]{1,0:T(8,128)(2,1)S(1)} %concatenate.8.rest_0_.rest_16_), channel_id=1, source_target_pairs={{0,4},{1,5},{2,6},{3,7},{4,0},{5,1},{6,2},{7,3},{8,12},{9,13},{10,... | collective-permute-start | bytes 454664 | tf_op jit(solution)/shard_map/ppermute | solution.py:23
  12.9 14.2 %collective-permute-start.1 = (bf16[16,4736]{1,0:T(8,128)(2,1)S(1)}, bf16[16,4736]{1,0:T(8,128)(2,1)S(1)}, u32[]{:S(2)}, u32[]{:S(2)}) collective-permute-start(bf16[16,4736]{1,0:T(8,128)(2,1)S(1)} %concatenate.8.rest_0_.rest_16_), channel_id=1, source_target_pairs={{0,8},{1,9},{2,10},{3,11},{4,12},{5,13},{6,14},{7,15},{8,0},{9,1},... | collective-permute-start | bytes 454664 | tf_op jit(solution)/shard_map/ppermute | solution.py:23
  15.5 13.1 %collective-permute-start.2 = (bf16[16,4736]{1,0:T(8,128)(2,1)S(1)}, bf16[16,4736]{1,0:T(8,128)(2,1)S(1)}, u32[]{:S(2)}, u32[]{:S(2)}) collective-permute-start(bf16[16,4736]{1,0:T(8,128)(2,1)S(1)} %concatenate.8.rest_0_.rest_16_), channel_id=1, source_target_pairs={{0,12},{1,13},{2,14},{3,15},{4,8},{5,9},{6,10},{7,11},{8,4},{9,5},... | collective-permute-start | bytes 454664 | tf_op jit(solution)/shard_map/ppermute | solution.py:23
  15.5 13.6 %collective-permute-start.3 = (bf16[16,4736]{1,0:T(8,128)(2,1)S(1)}, bf16[16,4736]{1,0:T(8,128)(2,1)S(1)}, u32[]{:S(2)}, u32[]{:S(2)}) collective-permute-start(bf16[16,4736]{1,0:T(8,128)(2,1)S(1)} %concatenate.8.rest_0_.rest_16_), channel_id=1, source_target_pairs={{0,2},{1,3},{2,0},{3,1},{4,6},{5,7},{6,4},{7,5},{8,10},{9,11},{10,... | collective-permute-start | bytes 454664 | tf_op jit(solution)/shard_map/ppermute | solution.py:23
  17.3 11.9 %collective-permute-start.7 = (bf16[16,4736]{1,0:T(8,128)(2,1)S(1)}, bf16[16,4736]{1,0:T(8,128)(2,1)S(1)}, u32[]{:S(2)}, u32[]{:S(2)}) collective-permute-start(bf16[16,4736]{1,0:T(8,128)(2,1)S(1)} %concatenate.8.rest_0_.rest_16_), channel_id=1, source_target_pairs={{0,1},{1,0},{2,3},{3,2},{4,5},{5,4},{6,7},{7,6},{8,9},{9,8},{10,11... | collective-permute-start | bytes 454664 | tf_op jit(solution)/shard_map/ppermute | solution.py:23
  19.0 11.7 %collective-permute-start.4 = (bf16[16,4736]{1,0:T(8,128)(2,1)S(1)}, bf16[16,4736]{1,0:T(8,128)(2,1)S(1)}, u32[]{:S(2)}, u32[]{:S(2)}) collective-permute-start(bf16[16,4736]{1,0:T(8,128)(2,1)S(1)} %collective-permute-done.rest_1_.rest_17_), channel_id=1, source_target_pairs={{0,2},{1,3},{2,0},{3,1},{4,6},{5,7},{6,4},{7,5},{8,10},{9,11},{10,... | collective-permute-start | bytes 454664 | tf_op jit(solution)/shard_map/ppermute | solution.py:23
  27.1 5.2 %collective-permute-start.5 = (bf16[16,4736]{1,0:T(8,128)(2,1)S(1)}, bf16[16,4736]{1,0:T(8,128)(2,1)S(1)}, u32[]{:S(2)}, u32[]{:S(2)}) collective-permute-start(bf16[16,4736]{1,0:T(8,128)(2,1)S(1)} %collective-permute-done.1.rest_2_.rest_18_), channel_id=1, source_target_pairs={{0,2},{1,3},{2,0},{3,1},{4,6},{5,7},{6,4},{7,5},{8,10},{9,11},{10,... | collective-permute-start | bytes 454664 | tf_op jit(solution)/shard_map/ppermute | solution.py:23
  28.7 5.3 %collective-permute-start.6 = (bf16[16,4736]{1,0:T(8,128)(2,1)S(1)}, bf16[16,4736]{1,0:T(8,128)(2,1)S(1)}, u32[]{:S(2)}, u32[]{:S(2)}) collective-permute-start(bf16[16,4736]{1,0:T(8,128)(2,1)S(1)} %collective-permute-done.2.rest_3_.rest_19_), channel_id=1, source_target_pairs={{0,2},{1,3},{2,0},{3,1},{4,6},{5,7},{6,4},{7,5},{8,10},{9,11},{10,... | collective-permute-start | bytes 454664 | tf_op jit(solution)/shard_map/ppermute | solution.py:23
  29.2 4.8 %collective-permute-start.10 = (bf16[16,4736]{1,0:T(8,128)(2,1)S(1)}, bf16[16,4736]{1,0:T(8,128)(2,1)S(1)}, u32[]{:S(2)}, u32[]{:S(2)}) collective-permute-start(bf16[16,4736]{1,0:T(8,128)(2,1)S(1)} %collective-permute-done.2.rest_3_.rest_19_), channel_id=1, source_target_pairs={{0,1},{1,0},{2,3},{3,2},{4,5},{5,4},{6,7},{7,6},{8,9},{9,8},{10,11... | collective-permute-start | bytes 454664 | tf_op jit(solution)/shard_map/ppermute | solution.py:23
  29.2 5.3 %collective-permute-start.11 = (bf16[16,4736]{1,0:T(8,128)(2,1)S(1)}, bf16[16,4736]{1,0:T(8,128)(2,1)S(1)}, u32[]{:S(2)}, u32[]{:S(2)}) collective-permute-start(bf16[16,4736]{1,0:T(8,128)(2,1)S(1)} %collective-permute-done.3.rest_4_.rest_20_), channel_id=1, source_target_pairs={{0,1},{1,0},{2,3},{3,2},{4,5},{5,4},{6,7},{7,6},{8,9},{9,8},{10,11... | collective-permute-start | bytes 454664 | tf_op jit(solution)/shard_map/ppermute | solution.py:23
  30.7 4.5 %collective-permute-start.8 = (bf16[16,4736]{1,0:T(8,128)(2,1)S(1)}, bf16[16,4736]{1,0:T(8,128)(2,1)S(1)}, u32[]{:S(2)}, u32[]{:S(2)}) collective-permute-start(bf16[16,4736]{1,0:T(8,128)(2,1)S(1)} %collective-permute-done.rest_1_.rest_17_), channel_id=1, source_target_pairs={{0,1},{1,0},{2,3},{3,2},{4,5},{5,4},{6,7},{7,6},{8,9},{9,8},{10,11... | collective-permute-start | bytes 454664 | tf_op jit(solution)/shard_map/ppermute | solution.py:23
  32.3 2.8 %collective-permute-start.9 = (bf16[16,4736]{1,0:T(8,128)(2,1)S(1)}, bf16[16,4736]{1,0:T(8,128)(2,1)S(1)}, u32[]{:S(2)}, u32[]{:S(2)}) collective-permute-start(bf16[16,4736]{1,0:T(8,128)(2,1)S(1)} %collective-permute-done.1.rest_2_.rest_18_), channel_id=1, source_target_pairs={{0,1},{1,0},{2,3},{3,2},{4,5},{5,4},{6,7},{7,6},{8,9},{9,8},{10,11... | collective-permute-start | bytes 454664 | tf_op jit(solution)/shard_map/ppermute | solution.py:23
  33.9 1.4 collective-permute-start.12
  34.0 1.6 collective-permute-start.13
  34.5 1.4 collective-permute-start.14
  47.7 1.6 collective-permute-start.15
  48.0 1.8 %collective-permute-start.18 = (bf16[2,288,256]{2,1,0:T(8,128)(2,1)S(1)}, bf16[2,288,256]{2,1,0:T(8,128)(2,1)S(1)}, u32[]{:S(2)}, u32[]{:S(2)}) collective-permute-start(bf16[2,288,256]{2,1,0:T(8,128)(2,1)S(1)} %get-tuple-element.13), channel_id=1, source_target_pairs={{0,1},{1,0},{2,3},{3,2},{4,5},{5,4},{6,7},{7,6},{8,9},{9,8},{10,11... | collective-permute-start | bytes 884744 | tf_op jit(solution)/shard_map/ppermute | solution.py:23
  48.3 1.9 %collective-permute-start.21 = (bf16[2,288,256]{2,1,0:T(8,128)(2,1)S(1)}, bf16[2,288,256]{2,1,0:T(8,128)(2,1)S(1)}, u32[]{:S(2)}, u32[]{:S(2)}) collective-permute-start(bf16[2,288,256]{2,1,0:T(8,128)(2,1)S(1)} %get-tuple-element.12), channel_id=1, source_target_pairs={{0,1},{1,0},{2,3},{3,2},{4,5},{5,4},{6,7},{7,6},{8,9},{9,8},{10,11... | collective-permute-start | bytes 884744 | tf_op jit(solution)/shard_map/ppermute | solution.py:23
  48.5 2.1 %collective-permute-start.24 = (bf16[2,288,256]{2,1,0:T(8,128)(2,1)S(1)}, bf16[2,288,256]{2,1,0:T(8,128)(2,1)S(1)}, u32[]{:S(2)}, u32[]{:S(2)}) collective-permute-start(bf16[2,288,256]{2,1,0:T(8,128)(2,1)S(1)} %get-tuple-element.11), channel_id=1, source_target_pairs={{0,1},{1,0},{2,3},{3,2},{4,5},{5,4},{6,7},{7,6},{8,9},{9,8},{10,11... | collective-permute-start | bytes 884744 | tf_op jit(solution)/shard_map/ppermute | solution.py:23
  50.8 17.9 %collective-permute-start.25 = (bf16[288,256]{1,0:T(8,128)(2,1)S(1)}, bf16[288,256]{1,0:T(8,128)(2,1)S(1)}, u32[]{:S(2)}, u32[]{:S(2)}) collective-permute-start(bf16[288,256]{1,0:T(8,128)(2,1)S(1)} %slice_bitcast_fusion.24), channel_id=1, source_target_pairs={{0,2},{1,3},{2,0},{3,1},{4,6},{5,7},{6,4},{7,5},{8,10},{9,11},{10,... | collective-permute-start | bytes 442376 | tf_op jit(solution)/shard_map/ppermute | solution.py:23
  52.4 8.3 %collective-permute-start.22 = (bf16[288,256]{1,0:T(8,128)(2,1)S(1)}, bf16[288,256]{1,0:T(8,128)(2,1)S(1)}, u32[]{:S(2)}, u32[]{:S(2)}) collective-permute-start(bf16[288,256]{1,0:T(8,128)(2,1)S(1)} %slice_bitcast_fusion.26), channel_id=1, source_target_pairs={{0,2},{1,3},{2,0},{3,1},{4,6},{5,7},{6,4},{7,5},{8,10},{9,11},{10,... | collective-permute-start | bytes 442376 | tf_op jit(solution)/shard_map/ppermute | solution.py:23
  53.0 10.9 %collective-permute-start.19 = (bf16[288,256]{1,0:T(8,128)(2,1)S(1)}, bf16[288,256]{1,0:T(8,128)(2,1)S(1)}, u32[]{:S(2)}, u32[]{:S(2)}) collective-permute-start(bf16[288,256]{1,0:T(8,128)(2,1)S(1)} %slice_bitcast_fusion.28), channel_id=1, source_target_pairs={{0,2},{1,3},{2,0},{3,1},{4,6},{5,7},{6,4},{7,5},{8,10},{9,11},{10,... | collective-permute-start | bytes 442376 | tf_op jit(solution)/shard_map/ppermute | solution.py:23
  54.6 11.7 %collective-permute-start.16 = (bf16[288,256]{1,0:T(8,128)(2,1)S(1)}, bf16[288,256]{1,0:T(8,128)(2,1)S(1)}, u32[]{:S(2)}, u32[]{:S(2)}) collective-permute-start(bf16[288,256]{1,0:T(8,128)(2,1)S(1)} %slice_bitcast_fusion.30), channel_id=1, source_target_pairs={{0,2},{1,3},{2,0},{3,1},{4,6},{5,7},{6,4},{7,5},{8,10},{9,11},{10,... | collective-permute-start | bytes 442376 | tf_op jit(solution)/shard_map/ppermute | solution.py:23
  60.7 8.6 %collective-permute-start.23 = (bf16[288,256]{1,0:T(8,128)(2,1)S(1)}, bf16[288,256]{1,0:T(8,128)(2,1)S(1)}, u32[]{:S(2)}, u32[]{:S(2)}) collective-permute-start(bf16[288,256]{1,0:T(8,128)(2,1)S(1)} %fusion.17), channel_id=1, source_target_pairs={{0,4},{1,5},{2,6},{3,7},{4,0},{5,1},{6,2},{7,3},{8,12},{9,13},{10,... | collective-permute-start | bytes 442376 | tf_op jit(solution)/shard_map/ppermute | solution.py:23
  63.9 12.9 %collective-permute-start.20 = (bf16[288,256]{1,0:T(8,128)(2,1)S(1)}, bf16[288,256]{1,0:T(8,128)(2,1)S(1)}, u32[]{:S(2)}, u32[]{:S(2)}) collective-permute-start(bf16[288,256]{1,0:T(8,128)(2,1)S(1)} %fusion.18), channel_id=1, source_target_pairs={{0,8},{1,9},{2,10},{3,11},{4,12},{5,13},{6,14},{7,15},{8,0},{9,1},... | collective-permute-start | bytes 442376 | tf_op jit(solution)/shard_map/ppermute | solution.py:23
  66.3 10.5 %collective-permute-start.17 = (bf16[288,256]{1,0:T(8,128)(2,1)S(1)}, bf16[288,256]{1,0:T(8,128)(2,1)S(1)}, u32[]{:S(2)}, u32[]{:S(2)}) collective-permute-start(bf16[288,256]{1,0:T(8,128)(2,1)S(1)} %fusion.19), channel_id=1, source_target_pairs={{0,12},{1,13},{2,14},{3,15},{4,8},{5,9},{6,10},{7,11},{8,4},{9,5},... | collective-permute-start | bytes 442376 | tf_op jit(solution)/shard_map/ppermute | solution.py:23
  85.1 1.6 collective-permute-start.26
  85.2 1.9 %collective-permute-start.29 = (bf16[2,16,4096]{2,1,0:T(8,128)(2,1)S(1)}, bf16[2,16,4096]{2,1,0:T(8,128)(2,1)S(1)}, u32[]{:S(2)}, u32[]{:S(2)}) collective-permute-start(bf16[2,16,4096]{2,1,0:T(8,128)(2,1)S(1)} %get-tuple-element.29), channel_id=1, source_target_pairs={{0,1},{1,0},{2,3},{3,2},{4,5},{5,4},{6,7},{7,6},{8,9},{9,8},{10,11... | collective-permute-start | bytes 786440 | tf_op jit(solution)/shard_map/ppermute | solution.py:23
  85.7 1.8 %collective-permute-start.32 = (bf16[2,16,4096]{2,1,0:T(8,128)(2,1)S(1)}, bf16[2,16,4096]{2,1,0:T(8,128)(2,1)S(1)}, u32[]{:S(2)}, u32[]{:S(2)}) collective-permute-start(bf16[2,16,4096]{2,1,0:T(8,128)(2,1)S(1)} %get-tuple-element.28), channel_id=1, source_target_pairs={{0,1},{1,0},{2,3},{3,2},{4,5},{5,4},{6,7},{7,6},{8,9},{9,8},{10,11... | collective-permute-start | bytes 786440 | tf_op jit(solution)/shard_map/ppermute | solution.py:23
  85.8 2.1 %collective-permute-start.35 = (bf16[2,16,4096]{2,1,0:T(8,128)(2,1)S(1)}, bf16[2,16,4096]{2,1,0:T(8,128)(2,1)S(1)}, u32[]{:S(2)}, u32[]{:S(2)}) collective-permute-start(bf16[2,16,4096]{2,1,0:T(8,128)(2,1)S(1)} %get-tuple-element.30), channel_id=1, source_target_pairs={{0,1},{1,0},{2,3},{3,2},{4,5},{5,4},{6,7},{7,6},{8,9},{9,8},{10,11... | collective-permute-start | bytes 786440 | tf_op jit(solution)/shard_map/ppermute | solution.py:23
  88.0 6.4 %collective-permute-start.27 = (bf16[16,4096]{1,0:T(8,128)(2,1)S(1)}, bf16[16,4096]{1,0:T(8,128)(2,1)S(1)}, u32[]{:S(2)}, u32[]{:S(2)}) collective-permute-start(bf16[16,4096]{1,0:T(8,128)(2,1)S(1)} %slice_bitcast_fusion.46), channel_id=1, source_target_pairs={{0,2},{1,3},{2,0},{3,1},{4,6},{5,7},{6,4},{7,5},{8,10},{9,11},{10,... | collective-permute-start | bytes 393224 | tf_op jit(solution)/shard_map/ppermute | solution.py:23
  89.6 7.6 %collective-permute-start.30 = (bf16[16,4096]{1,0:T(8,128)(2,1)S(1)}, bf16[16,4096]{1,0:T(8,128)(2,1)S(1)}, u32[]{:S(2)}, u32[]{:S(2)}) collective-permute-start(bf16[16,4096]{1,0:T(8,128)(2,1)S(1)} %slice_bitcast_fusion.44), channel_id=1, source_target_pairs={{0,2},{1,3},{2,0},{3,1},{4,6},{5,7},{6,4},{7,5},{8,10},{9,11},{10,... | collective-permute-start | bytes 393224 | tf_op jit(solution)/shard_map/ppermute | solution.py:23
  90.1 9.9 %collective-permute-start.33 = (bf16[16,4096]{1,0:T(8,128)(2,1)S(1)}, bf16[16,4096]{1,0:T(8,128)(2,1)S(1)}, u32[]{:S(2)}, u32[]{:S(2)}) collective-permute-start(bf16[16,4096]{1,0:T(8,128)(2,1)S(1)} %slice_bitcast_fusion.42), channel_id=1, source_target_pairs={{0,2},{1,3},{2,0},{3,1},{4,6},{5,7},{6,4},{7,5},{8,10},{9,11},{10,... | collective-permute-start | bytes 393224 | tf_op jit(solution)/shard_map/ppermute | solution.py:23
  91.7 10.3 %collective-permute-start.36 = (bf16[16,4096]{1,0:T(8,128)(2,1)S(1)}, bf16[16,4096]{1,0:T(8,128)(2,1)S(1)}, u32[]{:S(2)}, u32[]{:S(2)}) collective-permute-start(bf16[16,4096]{1,0:T(8,128)(2,1)S(1)} %slice_bitcast_fusion.40), channel_id=1, source_target_pairs={{0,2},{1,3},{2,0},{3,1},{4,6},{5,7},{6,4},{7,5},{8,10},{9,11},{10,... | collective-permute-start | bytes 393224 | tf_op jit(solution)/shard_map/ppermute | solution.py:23
  94.4 7.7 %collective-permute-start.28 = (bf16[16,4096]{1,0:T(8,128)(2,1)S(1)}, bf16[16,4096]{1,0:T(8,128)(2,1)S(1)}, u32[]{:S(2)}, u32[]{:S(2)}) collective-permute-start(bf16[16,4096]{1,0:T(8,128)(2,1)S(1)} %fusion.27), channel_id=1, source_target_pairs={{0,12},{1,13},{2,14},{3,15},{4,8},{5,9},{6,10},{7,11},{8,4},{9,5},... | collective-permute-start | bytes 393224 | tf_op jit(solution)/shard_map/ppermute | solution.py:23
  97.2 10.8 %collective-permute-start.31 = (bf16[16,4096]{1,0:T(8,128)(2,1)S(1)}, bf16[16,4096]{1,0:T(8,128)(2,1)S(1)}, u32[]{:S(2)}, u32[]{:S(2)}) collective-permute-start(bf16[16,4096]{1,0:T(8,128)(2,1)S(1)} %fusion.26), channel_id=1, source_target_pairs={{0,8},{1,9},{2,10},{3,11},{4,12},{5,13},{6,14},{7,15},{8,0},{9,1},... | collective-permute-start | bytes 393224 | tf_op jit(solution)/shard_map/ppermute | solution.py:23
  100.0 8.0 %collective-permute-start.34 = (bf16[16,4096]{1,0:T(8,128)(2,1)S(1)}, bf16[16,4096]{1,0:T(8,128)(2,1)S(1)}, u32[]{:S(2)}, u32[]{:S(2)}) collective-permute-start(bf16[16,4096]{1,0:T(8,128)(2,1)S(1)} %fusion.25), channel_id=1, source_target_pairs={{0,4},{1,5},{2,6},{3,7},{4,0},{5,1},{6,2},{7,3},{8,12},{9,13},{10,... | collective-permute-start | bytes 393224 | tf_op jit(solution)/shard_map/ppermute | solution.py:23
  108.4 6.3 %collective-permute-start.37 = (bf16[16,4096]{1,0:T(8,128)(2,1)S(1)}, bf16[16,4096]{1,0:T(8,128)(2,1)S(1)}, u32[]{:S(2)}, u32[]{:S(2)}) collective-permute-start(bf16[16,4096]{1,0:T(8,128)(2,1)S(1)} %fusion.6.rest_0_), channel_id=1, source_target_pairs={{0,4},{1,5},{2,6},{3,7},{4,0},{5,1},{6,2},{7,3},{8,12},{9,13},{10,... | collective-permute-start | bytes 393224 | tf_op jit(solution)/shard_map/ppermute | solution.py:23
  108.5 12.4 %collective-permute-start.38 = (bf16[16,4096]{1,0:T(8,128)(2,1)S(1)}, bf16[16,4096]{1,0:T(8,128)(2,1)S(1)}, u32[]{:S(2)}, u32[]{:S(2)}) collective-permute-start(bf16[16,4096]{1,0:T(8,128)(2,1)S(1)} %fusion.6.rest_0_), channel_id=1, source_target_pairs={{0,8},{1,9},{2,10},{3,11},{4,12},{5,13},{6,14},{7,15},{8,0},{9,1},... | collective-permute-start | bytes 393224 | tf_op jit(solution)/shard_map/ppermute | solution.py:23
  111.3 11.1 %collective-permute-start.39 = (bf16[16,4096]{1,0:T(8,128)(2,1)S(1)}, bf16[16,4096]{1,0:T(8,128)(2,1)S(1)}, u32[]{:S(2)}, u32[]{:S(2)}) collective-permute-start(bf16[16,4096]{1,0:T(8,128)(2,1)S(1)} %fusion.6.rest_0_), channel_id=1, source_target_pairs={{0,12},{1,13},{2,14},{3,15},{4,8},{5,9},{6,10},{7,11},{8,4},{9,5},... | collective-permute-start | bytes 393224 | tf_op jit(solution)/shard_map/ppermute | solution.py:23
  112.8 10.1 %collective-permute-start.40 = (bf16[16,4096]{1,0:T(8,128)(2,1)S(1)}, bf16[16,4096]{1,0:T(8,128)(2,1)S(1)}, u32[]{:S(2)}, u32[]{:S(2)}) collective-permute-start(bf16[16,4096]{1,0:T(8,128)(2,1)S(1)} %fusion.6.rest_0_), channel_id=1, source_target_pairs={{0,2},{1,3},{2,0},{3,1},{4,6},{5,7},{6,4},{7,5},{8,10},{9,11},{10,... | collective-permute-start | bytes 393224 | tf_op jit(solution)/shard_map/ppermute | solution.py:23
  114.4 8.6 %collective-permute-start.44 = (bf16[16,4096]{1,0:T(8,128)(2,1)S(1)}, bf16[16,4096]{1,0:T(8,128)(2,1)S(1)}, u32[]{:S(2)}, u32[]{:S(2)}) collective-permute-start(bf16[16,4096]{1,0:T(8,128)(2,1)S(1)} %fusion.6.rest_0_), channel_id=1, source_target_pairs={{0,1},{1,0},{2,3},{3,2},{4,5},{5,4},{6,7},{7,6},{8,9},{9,8},{10,11... | collective-permute-start | bytes 393224 | tf_op jit(solution)/shard_map/ppermute | solution.py:23
  114.7 8.8 %collective-permute-start.41 = (bf16[16,4096]{1,0:T(8,128)(2,1)S(1)}, bf16[16,4096]{1,0:T(8,128)(2,1)S(1)}, u32[]{:S(2)}, u32[]{:S(2)}) collective-permute-start(bf16[16,4096]{1,0:T(8,128)(2,1)S(1)} %collective-permute-done.37.rest_1_), channel_id=1, source_target_pairs={{0,2},{1,3},{2,0},{3,1},{4,6},{5,7},{6,4},{7,5},{8,10},{9,11},{10,... | collective-permute-start | bytes 393224 | tf_op jit(solution)/shard_map/ppermute | solution.py:23
  120.9 5.0 %collective-permute-start.42 = (bf16[16,4096]{1,0:T(8,128)(2,1)S(1)}, bf16[16,4096]{1,0:T(8,128)(2,1)S(1)}, u32[]{:S(2)}, u32[]{:S(2)}) collective-permute-start(bf16[16,4096]{1,0:T(8,128)(2,1)S(1)} %collective-permute-done.38.rest_2_), channel_id=1, source_target_pairs={{0,2},{1,3},{2,0},{3,1},{4,6},{5,7},{6,4},{7,5},{8,10},{9,11},{10,... | collective-permute-start | bytes 393224 | tf_op jit(solution)/shard_map/ppermute | solution.py:23
  122.4 5.0 %collective-permute-start.43 = (bf16[16,4096]{1,0:T(8,128)(2,1)S(1)}, bf16[16,4096]{1,0:T(8,128)(2,1)S(1)}, u32[]{:S(2)}, u32[]{:S(2)}) collective-permute-start(bf16[16,4096]{1,0:T(8,128)(2,1)S(1)} %collective-permute-done.39.rest_3_), channel_id=1, source_target_pairs={{0,2},{1,3},{2,0},{3,1},{4,6},{5,7},{6,4},{7,5},{8,10},{9,11},{10,... | collective-permute-start | bytes 393224 | tf_op jit(solution)/shard_map/ppermute | solution.py:23
  122.9 4.5 %collective-permute-start.45 = (bf16[16,4096]{1,0:T(8,128)(2,1)S(1)}, bf16[16,4096]{1,0:T(8,128)(2,1)S(1)}, u32[]{:S(2)}, u32[]{:S(2)}) collective-permute-start(bf16[16,4096]{1,0:T(8,128)(2,1)S(1)} %collective-permute-done.37.rest_1_), channel_id=1, source_target_pairs={{0,1},{1,0},{2,3},{3,2},{4,5},{5,4},{6,7},{7,6},{8,9},{9,8},{10,11... | collective-permute-start | bytes 393224 | tf_op jit(solution)/shard_map/ppermute | solution.py:23
  123.0 4.9 %collective-permute-start.46 = (bf16[16,4096]{1,0:T(8,128)(2,1)S(1)}, bf16[16,4096]{1,0:T(8,128)(2,1)S(1)}, u32[]{:S(2)}, u32[]{:S(2)}) collective-permute-start(bf16[16,4096]{1,0:T(8,128)(2,1)S(1)} %collective-permute-done.38.rest_2_), channel_id=1, source_target_pairs={{0,1},{1,0},{2,3},{3,2},{4,5},{5,4},{6,7},{7,6},{8,9},{9,8},{10,11... | collective-permute-start | bytes 393224 | tf_op jit(solution)/shard_map/ppermute | solution.py:23
  123.5 4.5 %collective-permute-start.47 = (bf16[16,4096]{1,0:T(8,128)(2,1)S(1)}, bf16[16,4096]{1,0:T(8,128)(2,1)S(1)}, u32[]{:S(2)}, u32[]{:S(2)}) collective-permute-start(bf16[16,4096]{1,0:T(8,128)(2,1)S(1)} %collective-permute-done.39.rest_3_), channel_id=1, source_target_pairs={{0,1},{1,0},{2,3},{3,2},{4,5},{5,4},{6,7},{7,6},{8,9},{9,8},{10,11... | collective-permute-start | bytes 393224 | tf_op jit(solution)/shard_map/ppermute | solution.py:23
  125.9 2.1 %collective-permute-start.48 = (bf16[16,4096]{1,0:T(8,128)(2,1)S(1)}, bf16[16,4096]{1,0:T(8,128)(2,1)S(1)}, u32[]{:S(2)}, u32[]{:S(2)}) collective-permute-start(bf16[16,4096]{1,0:T(8,128)(2,1)S(1)} %collective-permute-done.40.rest_4_), channel_id=1, source_target_pairs={{0,1},{1,0},{2,3},{3,2},{4,5},{5,4},{6,7},{7,6},{8,9},{9,8},{10,11... | collective-permute-start | bytes 393224 | tf_op jit(solution)/shard_map/ppermute | solution.py:23
  127.4 1.3 collective-permute-start.49
  127.4 1.5 collective-permute-start.50
  127.9 1.3 collective-permute-start.51
  145.6 1.6 collective-permute-start.52
  146.0 1.6 collective-permute-start.55
  146.2 1.8 %collective-permute-start.58 = (bf16[2,16,4096]{2,1,0:T(8,128)(2,1)S(1)}, bf16[2,16,4096]{2,1,0:T(8,128)(2,1)S(1)}, u32[]{:S(2)}, u32[]{:S(2)}) collective-permute-start(bf16[2,16,4096]{2,1,0:T(8,128)(2,1)S(1)} %get-tuple-element.20), channel_id=1, source_target_pairs={{0,1},{1,0},{2,3},{3,2},{4,5},{5,4},{6,7},{7,6},{8,9},{9,8},{10,11... | collective-permute-start | bytes 786440 | tf_op jit(solution)/shard_map/ppermute | solution.py:23
  146.5 1.8 %collective-permute-start.61 = (bf16[2,16,4096]{2,1,0:T(8,128)(2,1)S(1)}, bf16[2,16,4096]{2,1,0:T(8,128)(2,1)S(1)}, u32[]{:S(2)}, u32[]{:S(2)}) collective-permute-start(bf16[2,16,4096]{2,1,0:T(8,128)(2,1)S(1)} %get-tuple-element.19), channel_id=1, source_target_pairs={{0,1},{1,0},{2,3},{3,2},{4,5},{5,4},{6,7},{7,6},{8,9},{9,8},{10,11... | collective-permute-start | bytes 786440 | tf_op jit(solution)/shard_map/ppermute | solution.py:23
  148.5 6.4 %collective-permute-start.53 = (bf16[16,4096]{1,0:T(8,128)(2,1)S(1)}, bf16[16,4096]{1,0:T(8,128)(2,1)S(1)}, u32[]{:S(2)}, u32[]{:S(2)}) collective-permute-start(bf16[16,4096]{1,0:T(8,128)(2,1)S(1)} %slice_bitcast_fusion.38), channel_id=1, source_target_pairs={{0,2},{1,3},{2,0},{3,1},{4,6},{5,7},{6,4},{7,5},{8,10},{9,11},{10,... | collective-permute-start | bytes 393224 | tf_op jit(solution)/shard_map/ppermute | solution.py:23
  150.0 7.8 %collective-permute-start.56 = (bf16[16,4096]{1,0:T(8,128)(2,1)S(1)}, bf16[16,4096]{1,0:T(8,128)(2,1)S(1)}, u32[]{:S(2)}, u32[]{:S(2)}) collective-permute-start(bf16[16,4096]{1,0:T(8,128)(2,1)S(1)} %slice_bitcast_fusion.36), channel_id=1, source_target_pairs={{0,2},{1,3},{2,0},{3,1},{4,6},{5,7},{6,4},{7,5},{8,10},{9,11},{10,... | collective-permute-start | bytes 393224 | tf_op jit(solution)/shard_map/ppermute | solution.py:23
  150.7 9.9 %collective-permute-start.59 = (bf16[16,4096]{1,0:T(8,128)(2,1)S(1)}, bf16[16,4096]{1,0:T(8,128)(2,1)S(1)}, u32[]{:S(2)}, u32[]{:S(2)}) collective-permute-start(bf16[16,4096]{1,0:T(8,128)(2,1)S(1)} %slice_bitcast_fusion.34), channel_id=1, source_target_pairs={{0,2},{1,3},{2,0},{3,1},{4,6},{5,7},{6,4},{7,5},{8,10},{9,11},{10,... | collective-permute-start | bytes 393224 | tf_op jit(solution)/shard_map/ppermute | solution.py:23
  152.1 10.6 %collective-permute-start.62 = (bf16[16,4096]{1,0:T(8,128)(2,1)S(1)}, bf16[16,4096]{1,0:T(8,128)(2,1)S(1)}, u32[]{:S(2)}, u32[]{:S(2)}) collective-permute-start(bf16[16,4096]{1,0:T(8,128)(2,1)S(1)} %slice_bitcast_fusion.32), channel_id=1, source_target_pairs={{0,2},{1,3},{2,0},{3,1},{4,6},{5,7},{6,4},{7,5},{8,10},{9,11},{10,... | collective-permute-start | bytes 393224 | tf_op jit(solution)/shard_map/ppermute | solution.py:23
  154.9 8.3 %collective-permute-start.54 = (bf16[16,4096]{1,0:T(8,128)(2,1)S(1)}, bf16[16,4096]{1,0:T(8,128)(2,1)S(1)}, u32[]{:S(2)}, u32[]{:S(2)}) collective-permute-start(bf16[16,4096]{1,0:T(8,128)(2,1)S(1)} %fusion.23), channel_id=1, source_target_pairs={{0,12},{1,13},{2,14},{3,15},{4,8},{5,9},{6,10},{7,11},{8,4},{9,5},... | collective-permute-start | bytes 393224 | tf_op jit(solution)/shard_map/ppermute | solution.py:23
  157.7 10.4 %collective-permute-start.57 = (bf16[16,4096]{1,0:T(8,128)(2,1)S(1)}, bf16[16,4096]{1,0:T(8,128)(2,1)S(1)}, u32[]{:S(2)}, u32[]{:S(2)}) collective-permute-start(bf16[16,4096]{1,0:T(8,128)(2,1)S(1)} %fusion.22), channel_id=1, source_target_pairs={{0,8},{1,9},{2,10},{3,11},{4,12},{5,13},{6,14},{7,15},{8,0},{9,1},... | collective-permute-start | bytes 393224 | tf_op jit(solution)/shard_map/ppermute | solution.py:23
  160.6 7.6 %collective-permute-start.60 = (bf16[16,4096]{1,0:T(8,128)(2,1)S(1)}, bf16[16,4096]{1,0:T(8,128)(2,1)S(1)}, u32[]{:S(2)}, u32[]{:S(2)}) collective-permute-start(bf16[16,4096]{1,0:T(8,128)(2,1)S(1)} %fusion.21), channel_id=1, source_target_pairs={{0,4},{1,5},{2,6},{3,7},{4,0},{5,1},{6,2},{7,3},{8,12},{9,13},{10,... | collective-permute-start | bytes 393224 | tf_op jit(solution)/shard_map/ppermute | solution.py:23
  (39 other events, 226.2 us)

commit v2 on v1

--- a/solution.py
+++ b/solution.py
@@ -34,27 +34,55 @@
     return near + [swap(b, 1, devices) for b in near]
 
 
-def scatter_blocks(x, devices):
-    far = devices // 4
-    parts = x.reshape((2, 2, far) + x.shape[1:])
+def scatter_blocks(keep, send, devices):
     pieces = []
-    for i in range(far - 1, -1, -1):
-        pair = parts[0, :, i] + swap(parts[1, :, i], 1, devices)
+    for i in range(devices // 4 - 1, -1, -1):
+        pair = keep[i] + swap(send[i], 1, devices)
         mine = pair[0] + swap(pair[1], 2, devices)
         pieces.append(swap(mine, 4 * i, devices) if i else mine)
     return pieces
 
 
+def split_shapes(devices, tail):
+    return [jax.ShapeDtypeStruct((2,) + tail, BF)] * (devices // 2)
+
+
+def split_refs(refs, devices):
+    far = devices // 4
+    return [(refs[c * far + z], y) for c in range(2) for y in range(2) for z in range(far)]
+
+
 def lane_pick(vec, lane_iota, index):
     return jnp.sum(jnp.where(lane_iota == index, vec, 0.0), axis=1, keepdims=True)
 
 
+def payload_kernel(q_ref, fresh_ref, ids_ref, score_ref, owner_ref, out_ref, *, top):
+    row_dev, qk = q_ref.shape
+    kv = fresh_ref.shape[2]
+    out_ref[:, :qk] = q_ref[...]
+    out_ref[:, qk : qk + kv] = fresh_ref[:, 0, :]
+    out_ref[:, qk + kv : qk + 2 * kv] = fresh_ref[:, 1, :]
+    segs = owner_ref.shape[1]
+    owner = owner_ref[...]
+    first = jnp.broadcast_to(owner[:, 0:1], (row_dev, LANES))
+    last = jnp.broadcast_to(owner[:, segs - 1 : segs], (row_dev, LANES))
+    lane = lax.broadcasted_iota(jnp.int32, (row_dev, LANES), 1)
+    extra = jnp.zeros((row_dev, LANES), jnp.int32)
+    for k in range(top):
+        extra = jnp.where(lane == k, ids_ref[:, k : k + 1], extra)
+        extra = jnp.where(lane == top + k, score_ref[:, k : k + 1], extra)
+    for k, v in enumerate((first // 16, first % 16, last // 16, last % 16)):
+        extra = jnp.where(lane == 2 * top + k, v, extra)
+    out_ref[:, qk + 2 * kv :] = extra.astype(F32).astype(BF)
+
+
 def attend_kernel(
-    me_ref, owner_row_ref, owner_col_ref, bias_ref, k_ref, v_ref, *rest,
+    me_ref, owner_row_ref, length_ref, k_ref, v_ref, *rest,
     devices, row_dev, width, q_heads, kv_heads, slots, seg_width,
 ):
     pieces = rest[:devices]
-    out_ref, q_scr, o_scr, m_scr = rest[devices:]
+    outs = split_refs(rest[devices : devices + devices // 2], devices)
+    q_scr, o_scr, m_scr, t_scr, l_scr = rest[devices + devices // 2 :]
     me = me_ref[0]
     masks = xor_masks(devices)
     rows = devices * row_dev
@@ -63,6 +91,7 @@
     per_kv = q_heads // kv_heads
     qk = q_heads * HEAD_SIZE
     ext = qk + 2 * kv_heads * HEAD_SIZE
+    owner_col = jnp.broadcast_to(owner_row_ref[...].astype(F32), (LANES, segs)).T.astype(jnp.int32)
     hots = []
     per_lane = LANES // row_dev
     lane = lax.broadcasted_iota(jnp.int32, (1, LANES), 1)
@@ -71,7 +100,7 @@
         for i in range(per_lane):
             base = (me ^ masks[c * per_lane + i]) * row_dev - i * row_dev
             gid = jnp.where(lane // row_dev == i, lane + base, gid)
-        hots.append((owner_col_ref[...] == gid).astype(F32).astype(BF))
+        hots.append((owner_col == gid).astype(F32).astype(BF))
     hot = jnp.concatenate(hots, axis=1)
     step = 512
     for c in range(qk // step):
@@ -85,10 +114,19 @@
     c_i = lax.broadcasted_iota(jnp.int32, (group, wide), 1)
     eye_bias = jnp.where(r_i == c_i // seg_width, 0.0, NEG)
     ones = jnp.ones((wide, HEAD_SIZE), BF)
+    of_group = lax.broadcasted_iota(jnp.int32, (segs // group, segs), 1) // group
+    g_i = lax.broadcasted_iota(jnp.int32, (segs // group, segs), 0)
+    lens = jnp.where(of_group == g_i, length_ref[...], 0).astype(F32).astype(BF)
+    e_i = lax.broadcasted_iota(jnp.int32, (segs, wide), 0) % group
+    e_j = lax.broadcasted_iota(jnp.int32, (segs, wide), 1) // seg_width
+    spread = jnp.where(e_i == e_j, 1.0, 0.0).astype(BF)
+    live = jnp.dot(lens, spread, preferred_element_type=F32)
+    at = (lax.broadcasted_iota(jnp.int32, (segs // group, wide), 1) % seg_width).astype(F32)
+    live_bias = jnp.where(at < live, 0.0, NEG)
     stat_lanes = m_scr.shape[1]
     m_lane = lax.broadcasted_iota(jnp.int32, (group, stat_lanes), 1)
     for g in range(segs // group):
-        bias = eye_bias + bias_ref[g : g + 1, :]
+        bias = eye_bias + live_bias[g : g + 1, :]
         m_acc = jnp.zeros((group, stat_lanes), F32)
         for kv in range(kv_heads):
             lo = kv * per_kv
@@ -114,7 +152,7 @@
             for h in range(per_kv):
                 m_acc = jnp.where(m_lane == lo + h, m[h], m_acc)
         m_scr[g * group : (g + 1) * group, :] = m_acc
-    m_t = m_scr[...].T
+    t_scr[...] = m_scr[...].T
     ext_sum = jnp.zeros((1, LANES), F32)
     for p in range(devices):
         vec = pieces[p][0:1, ext : ext + LANES].astype(F32)
@@ -131,19 +169,18 @@
     st_lane = lax.broadcasted_iota(jnp.int32, (slots, stats), 1)
     max_acc = jnp.zeros((slots, stats), F32)
     sum_acc = jnp.ones((slots, stats), F32)
-    for d in range(devices):
-        pos_mask = me ^ d
-        far = devices // 4
-        pos = (pos_mask & 1) * (2 * far) + ((pos_mask >> 1) & 1) * far + (pos_mask >> 2)
+    for p in range(devices):
+        d = me ^ masks[p]
+        out_ref, y = outs[p]
         for hh in range(hp):
             h = d * hp + hh
-            m_row = m_t[h : h + 1, :]
+            m_row = t_scr[pl.ds(h, 1), :]
             mm = jnp.where(mask, m_row, NEG)
             r_max = jnp.maximum(jnp.max(mm, axis=1, keepdims=True), 0.1 * NEG)
             weight = jnp.exp(mm - r_max).astype(BF)
             r = jnp.dot(weight, o_scr[h], preferred_element_type=F32)
             r_sum = jnp.maximum(r[:, HEAD_SIZE:], 1.0)
-            out_ref[pos, 0:slots, hh * HEAD_SIZE : (hh + 1) * HEAD_SIZE] = (
+            out_ref[y, 0:slots, hh * HEAD_SIZE : (hh + 1) * HEAD_SIZE] = (
                 r[:, :HEAD_SIZE] / r_sum
             ).astype(BF)
             here = jnp.zeros((slots, stats), jnp.bool_)
@@ -166,18 +203,18 @@
     lse_t = lse.T
     if pad > pad_t:
         lse_t = jnp.concatenate([lse_t, jnp.zeros((stats, pad - pad_t), F32)], axis=1)
-    tail = out_ref.shape[1] - slots
-    for d in range(devices):
-        pos_mask = me ^ d
-        far = devices // 4
-        pos = (pos_mask & 1) * (2 * far) + ((pos_mask >> 1) & 1) * far + (pos_mask >> 2)
+    l_scr[...] = lse_t
+    tail = outs[0][0].shape[1] - slots
+    for p in range(devices):
+        at = pl.multiple_of((me ^ masks[p]) * 8, 8)
+        out_ref, y = outs[p]
         strips = [
-            lse_t[d * 8 : (d + 1) * 8, b * width : (b + 1) * width]
+            l_scr[pl.ds(at, 8), b * width : (b + 1) * width]
             for b in range((slots + pad) // width)
         ]
         if len(strips) * 8 < tail:
             strips.append(jnp.zeros((tail - len(strips) * 8, width), F32))
-        out_ref[pos, slots:, :] = jnp.concatenate(strips, axis=0).astype(BF)
+        out_ref[y, slots:, :] = jnp.concatenate(strips, axis=0).astype(BF)
 
 
 def combine_kernel(
@@ -186,7 +223,8 @@
     pieces = rest[:devices]
     far = devices // 4
     shares = rest[devices : devices + far]
-    out_ref, x_scr, l_scr = rest[devices + far :]
+    outs = split_refs(rest[devices + far : devices + far + devices // 2], devices)
+    x_scr, l_scr = rest[devices + far + devices // 2 :]
     me = me_ref[0]
     masks = xor_masks(devices)
     rows = devices * row_dev
@@ -268,43 +306,45 @@
         cut = slice(c * step, (c + 1) * step)
         r = jnp.dot(attn, w_ref[:, cut], preferred_element_type=F32).astype(BF)
         for p in range(devices):
-            out_ref[p, :, cut] = r[p * row_dev : (p + 1) * row_dev]
-
-
-def expert_kernel(me_ref, *rest, devices, row_dev, top):
+            out_ref, y = outs[p]
+            out_ref[y, :, cut] = r[p * row_dev : (p + 1) * row_dev]
+
+
+def expert_kernel(me_ref, gate_ref, up_ref, down_ref, *rest, devices, row_dev, top, ext_at):
     pieces = rest[:devices]
     ext = rest[devices : 2 * devices]
-    gate_ref, up_ref, down_ref, out_ref, x_scr, acc = rest[2 * devices :]
-    i = pl.program_id(0)
-
-    @pl.when(i == 0)
-    def _():
+    outs = split_refs(rest[2 * devices : 2 * devices + devices // 2], devices)
+    x_scr, h_scr = rest[2 * devices + devices // 2 :]
+    for p in range(devices):
+        x_scr[p * row_dev : (p + 1) * row_dev, :] = pieces[p][...]
+    ff = gate_ref.shape[2]
+    d_model = gate_ref.shape[1]
+    tile = 256
+    for c in range(ff // tile):
+        cut = slice(c * tile, (c + 1) * tile)
+        a = jnp.dot(x_scr[...], gate_ref[0, :, cut], preferred_element_type=F32)
+        b = jnp.dot(x_scr[...], up_ref[0, :, cut], preferred_element_type=F32)
+        h_scr[:, cut] = (a / (1.0 + jnp.exp(-a)) * b).astype(BF)
+    me = me_ref[0].astype(F32)
+    lane = lax.broadcasted_iota(jnp.int32, (row_dev, LANES), 1)
+    weights = []
+    for p in range(devices):
+        e = ext[p][:, ext_at : ext_at + LANES].astype(F32)
+        score = jnp.where(jnp.logical_and(lane >= top, lane < 2 * top), jnp.exp(e * 0.25), 0.0)
+        total = jnp.sum(score, axis=1, keepdims=True)
+        weight = jnp.zeros((row_dev, 1), F32)
+        for k in range(top):
+            weight = weight + jnp.where(e[:, k : k + 1] == me, score[:, top + k : top + k + 1], 0.0)
+        weights.append(weight / total)
+    weight = jnp.concatenate(weights, axis=0)
+    step = 512
+    for c in range(d_model // step):
+        cut = slice(c * step, (c + 1) * step)
+        y = jnp.dot(h_scr[...], down_ref[0, :, cut], preferred_element_type=F32)
+        y = (y.astype(BF).astype(F32) * weight).astype(BF)
         for p in range(devices):
-            x_scr[p * row_dev : (p + 1) * row_dev, :] = pieces[p][...]
-        acc[...] = jnp.zeros(acc.shape, F32)
-
-    x = x_scr[...]
-    a = jnp.dot(x, gate_ref[...], preferred_element_type=F32)
-    b = jnp.dot(x, up_ref[...], preferred_element_type=F32)
-    h = (a / (1.0 + jnp.exp(-a)) * b).astype(BF)
-    acc[...] += jnp.dot(h, down_ref[...], preferred_element_type=F32)
-
-    @pl.when(i == pl.num_programs(0) - 1)
-    def _():
-        me = me_ref[0]
-        lane = lax.broadcasted_iota(jnp.int32, (row_dev, LANES), 1)
-        for p in range(devices):
-            e = ext[p][...].astype(F32)
-            score = jnp.where(jnp.logical_and(lane >= top, lane < 2 * top), jnp.exp(e * 0.25), 0.0)
-            total = jnp.sum(score, axis=1, keepdims=True)
-            weight = jnp.zeros((row_dev, 1), F32)
-            for k in range(top):
-                weight = weight + jnp.where(
-                    e[:, k : k + 1] == me.astype(F32), score[:, top + k : top + k + 1], 0.0
-                )
-            weight = weight / total
-            y = acc[p * row_dev : (p + 1) * row_dev, :].astype(BF).astype(F32)
-            out_ref[p] = (y * weight).astype(BF)
+            out_ref, side = outs[p]
+            out_ref[side, :, cut] = y[p * row_dev : (p + 1) * row_dev]
 
 
 def on_device(
@@ -324,67 +364,59 @@
     slots = rows + devices
     strips = -(-slots // width)
     tall = slots + -(-strips // 2) * 16
-    first = segment_owner_row[0]
-    last = segment_owner_row[segs - 1]
-    ends = jnp.stack([first // 16, first % 16, last // 16, last % 16]).astype(BF)
-    extra = jnp.concatenate(
-        [
-            expert_ids.astype(BF),
-            gate_score.astype(BF),
-            jnp.broadcast_to(ends[None], (row_dev, 4)),
-            jnp.zeros((row_dev, LANES - 2 * top - 4), BF),
-        ],
-        axis=1,
-    )
-    payload = jnp.concatenate(
-        [queries, fresh_key_value.reshape(row_dev, -1), extra], axis=1
-    )
-    group = 16
-    slot_ids = jnp.arange(seg_width, dtype=jnp.int32)
-    bias = jnp.where(slot_ids[None] < segment_length[:, None], 0.0, NEG).astype(F32)
-    bias = bias.reshape(segs // group, group * seg_width)
-    owner_row = segment_owner_row.reshape(1, segs)
-    owner_col = jnp.broadcast_to(segment_owner_row[:, None], (segs, LANES))
-    pieces = gather_blocks(payload, devices)
     smem = pl.BlockSpec(memory_space=pltpu.SMEM)
     vmem = pl.BlockSpec(memory_space=pltpu.VMEM)
-    stat_lanes = LANES
-    params = pltpu.CompilerParams(vmem_limit_bytes=56 * 1024 * 1024)
+    half = devices // 2
+    far = devices // 4
+    owner_row = segment_owner_row.reshape(1, segs)
+    ext_at = (q_heads + 2 * kv_heads) * HEAD_SIZE
+    payload = pl.pallas_call(
+        functools.partial(payload_kernel, top=top),
+        out_shape=jax.ShapeDtypeStruct((row_dev, ext_at + LANES), BF),
+        in_specs=[vmem] * 5,
+        out_specs=vmem,
+        name="payload",
+    )(queries, fresh_key_value, expert_ids, gate_score, owner_row)
+    pieces = gather_blocks(payload, devices)
+    params = pltpu.CompilerParams(vmem_limit_bytes=24 * 1024 * 1024)
+    stats = devices * 8
     table = pl.pallas_call(
         functools.partial(
             attend_kernel, devices=devices, row_dev=row_dev, width=width, q_heads=q_heads,
             kv_heads=kv_heads, slots=slots, seg_width=seg_width,
         ),
-        out_shape=jax.ShapeDtypeStruct((devices, tall, width), BF),
-        in_specs=[smem] + [vmem] * (5 + devices),
-        out_specs=vmem,
+        out_shape=split_shapes(devices, (tall, width)),
+        in_specs=[smem] + [vmem] * (4 + devices),
+        out_specs=[vmem] * half,
         scratch_shapes=[
             pltpu.VMEM((segs, q_heads * HEAD_SIZE), BF),
             pltpu.VMEM((q_heads, segs, 2 * HEAD_SIZE), BF),
-            pltpu.VMEM((segs, stat_lanes), F32),
+            pltpu.VMEM((segs, LANES), F32),
+            pltpu.VMEM((LANES, segs), F32),
+            pltpu.VMEM((stats, max(strips * width, -(-slots // LANES) * LANES)), F32),
         ],
         compiler_params=params,
         name="attend",
     )(
-        me, owner_row, owner_col, bias,
+        me, owner_row, segment_length.reshape(1, segs),
         segment_key_cache.reshape(segs * seg_width, -1),
         segment_value_cache.reshape(segs * seg_width, -1),
         *pieces,
     )
-    shares = scatter_blocks(table, devices)
+    shares = scatter_blocks(table[:far], table[far:], devices)
     part = pl.pallas_call(
         functools.partial(
             combine_kernel, devices=devices, row_dev=row_dev, width=width, q_heads=q_heads,
             kv_heads=kv_heads, slots=slots,
         ),
-        out_shape=jax.ShapeDtypeStruct((devices, row_dev, d_model), BF),
-        in_specs=[smem] + [vmem] * (1 + devices + devices // 4),
-        out_specs=vmem,
+        out_shape=split_shapes(devices, (row_dev, d_model)),
+        in_specs=[smem] + [vmem] * (1 + devices + far),
+        out_specs=[vmem] * half,
         scratch_shapes=[pltpu.VMEM((tall, width), F32), pltpu.VMEM((rows, LANES), F32)],
         compiler_params=params,
         name="combine",
     )(me, out_proj, *pieces, *shares)
-    projected = sum(p.astype(F32) for p in scatter_blocks(part, devices))
+    projected = sum(p.astype(F32) for p in scatter_blocks(part[:far], part[far:], devices))
     mixed = (hidden_in.astype(F32) + projected).astype(BF).astype(F32)
     normed = (
         mixed
@@ -393,26 +425,18 @@
     ).astype(BF)
     tokens = gather_blocks(normed, devices)
     ff = w_gate.shape[2]
-    tile = 256
-    ext_at = (q_heads + 2 * kv_heads) * HEAD_SIZE // LANES
     moe = pl.pallas_call(
-        functools.partial(expert_kernel, devices=devices, row_dev=row_dev, top=top),
-        grid=(ff // tile,),
-        out_shape=jax.ShapeDtypeStruct((devices, row_dev, d_model), BF),
-        in_specs=[smem]
-        + [pl.BlockSpec((row_dev, d_model), lambda i: (0, 0))] * devices
-        + [pl.BlockSpec((row_dev, LANES), lambda i: (0, ext_at))] * devices
-        + [
-            pl.BlockSpec((None, d_model, tile), lambda i: (0, 0, i)),
-            pl.BlockSpec((None, d_model, tile), lambda i: (0, 0, i)),
-            pl.BlockSpec((None, tile, d_model), lambda i: (0, i, 0)),
-        ],
-        out_specs=pl.BlockSpec((devices, row_dev, d_model), lambda i: (0, 0, 0)),
-        scratch_shapes=[pltpu.VMEM((rows, d_model), BF), pltpu.VMEM((rows, d_model), F32)],
-        compiler_params=params,
+        functools.partial(
+            expert_kernel, devices=devices, row_dev=row_dev, top=top, ext_at=ext_at
+        ),
+        out_shape=split_shapes(devices, (row_dev, d_model)),
+        in_specs=[smem] + [vmem] * (3 + 2 * devices),
+        out_specs=[vmem] * half,
+        scratch_shapes=[pltpu.VMEM((rows, d_model), BF), pltpu.VMEM((rows, ff), BF)],
+        compiler_params=pltpu.CompilerParams(vmem_limit_bytes=34 * 1024 * 1024),
         name="experts",
-    )(me, *tokens, *pieces, w_gate, w_up, w_down)
-    summed = sum(p.astype(F32) for p in scatter_blocks(moe, devices))
+    )(me, w_gate, w_up, w_down, *tokens, *pieces)
+    summed = sum(p.astype(F32) for p in scatter_blocks(moe[:far], moe[far:], devices))
     return (mixed + summed).astype(BF)
 
 

time: 169 us -> 144 us (0.85)
  Pallas kernels: 28.4 us -> 16.8 us
  starting transfers between devices: 56 us -> 49.3 us
  between operations: 5.63 us -> 0.42 us
  local copies, waits for them, and re-layouts: 12.4 us -> 7.54 us
  waiting for transfers between devices: 62.2 us -> 67 us
  other arithmetic: 4.32 us -> 2.08 us
    ppermute x63, starting transfers between devices: 56 us -> 49.3 us  [swap(): return lax.ppermute(x, 'dev', [(i, i ^ mask) for i in range(devices)])]
    pallas_call x1, Pallas kernels: 13.9 us -> 7.92 us  [on_device(): pl.pallas_call(functools.partial(expert_kernel, devices=devices, row_dev=...]
    ppermute x63, waiting for transfers between devices: 62.2 us -> 67 us  [swap(): return lax.ppermute(x, 'dev', [(i, i ^ mask) for i in range(devices)])]
    unnamed x81 -> x26, local copies, waits for them, and re-layouts: 3.05 us -> 7.41 us
    squeeze x3 -> x0, local copies, waits for them, and re-layouts: 4.31 us -> none  [scatter_blocks(): pair = parts[0, :, i] + swap(parts[1, :, i], 1, devices)]
    pallas_call x1, Pallas kernels: 5.56 us -> 1.75 us  [on_device(): pl.pallas_call(functools.partial(combine_kernel, devices=devices, row_dev...]
    pallas_call x1, Pallas kernels: 8.9 us -> 5.37 us  [on_device(): pl.pallas_call(functools.partial(attend_kernel, devices=devices, row_dev=...]
    pallas_call x0 -> x1, Pallas kernels: none -> 1.71 us  [on_device(): pl.pallas_call(functools.partial(payload_kernel, top=top), out_shape=jax....]
  transfers between devices with their start and end apart: 63 -> 63, of which waited for: 41 -> 29; matrix products, arithmetic and copies ran while one was open for 1% -> 1% of each run, Pallas kernels for 0% -> 0%
where the time goes in v2:
time: 144 us; the launch traced here: 143 us
  waiting for transfers between devices  67 us (47%)
  starting transfers between devices  49.3 us (34%)
  Pallas kernels  16.8 us (12%)
  local copies, waits for them, and re-layouts  7.54 us (5%)
  other arithmetic  2.08 us (1%)
    ppermute x63, waiting for transfers between devices, swap(): return lax.ppermute(x, 'dev', [(i, i ^ mask) for i in range(devices)])  67 us
    ppermute x63, starting transfers between devices, swap(): return lax.ppermute(x, 'dev', [(i, i ^ mask) for i in range(devices)])  49.3 us
    pallas_call x1, Pallas kernels, on_device(): pl.pallas_call(functools.partial(expert_kernel, devices=devices, row_dev=...  7.92 us
    unnamed x26, local copies, waits for them, and re-layouts  7.41 us
    pallas_call x1, Pallas kernels, on_device(): pl.pallas_call(functools.partial(attend_kernel, devices=devices, row_dev=...  5.37 us
  transfers between devices with their start and end apart: 63, of which 29 were waited for; matrix products, arithmetic and copies ran while one was open for 1% of the time, Pallas kernels for 0%

profile of v2, /device:TPU:0, one launch (start us, length us, event | category | flops | bytes accessed | tf_op | source)
XLA Modules:
  0.0 143.2 jit_solution(1962490861779681293)
XLA Ops:
  0.0 1.4 copy.15.ids_ref
  1.4 1.3 copy.16.score_ref
  2.7 1.7 %payload.1.rest_0_.rest_16_ = bf16[16,4736]{1,0:T(8,128)(2,1)} custom-call(bf16[16,4096]{1,0:T(8,128)(2,1)} %q_ref.1, bf16[16,2,256]{2,1,0:T(2,128)(2,1)} %fresh_ref.1, s32[16,8]{1,0:T(8,128)} %copy.15.ids_ref, s32[16,8]{1,0:T(8,128)} %copy.16.score_ref, s32[1,128]{1,0:T(1,128)} %bitcast.86), custom_call_target="tpu_custom_call" | custom-call | tf_op jit(solution)/shard_map/payload/pallas_call | solution.py:373
  4.4 3.0 %collective-permute-start.3 = (bf16[16,4736]{1,0:T(8,128)(2,1)}, bf16[16,4736]{1,0:T(8,128)(2,1)S(1)}, u32[]{:S(2)}, u32[]{:S(2)}) collective-permute-start(bf16[16,4736]{1,0:T(8,128)(2,1)} %payload.1.rest_0_.rest_16_), channel_id=1, source_target_pairs={{0,2},{1,3},{2,0},{3,1},{4,6},{5,7},{6,4},{7,5},{8,10},{9,11},{10,... | collective-permute-start | bytes 454664 | tf_op jit(solution)/shard_map/ppermute | solution.py:23
  7.4 3.6 %collective-permute-start.2 = (bf16[16,4736]{1,0:T(8,128)(2,1)}, bf16[16,4736]{1,0:T(8,128)(2,1)S(1)}, u32[]{:S(2)}, u32[]{:S(2)}) collective-permute-start(bf16[16,4736]{1,0:T(8,128)(2,1)} %payload.1.rest_0_.rest_16_), channel_id=1, source_target_pairs={{0,12},{1,13},{2,14},{3,15},{4,8},{5,9},{6,10},{7,11},{8,4},{9,5},... | collective-permute-start | bytes 454664 | tf_op jit(solution)/shard_map/ppermute | solution.py:23
  11.0 0.8 collective-permute-start
  11.8 3.9 %collective-permute-done.2.rest_3_.rest_19_ = bf16[16,4736]{1,0:T(8,128)(2,1)S(1)} collective-permute-done((bf16[16,4736]{1,0:T(8,128)(2,1)}, bf16[16,4736]{1,0:T(8,128)(2,1)S(1)}, u32[]{:S(2)}, u32[]{:S(2)}) %collective-permute-start.2) | collective-permute-done | bytes 151584 | tf_op jit(solution)/shard_map/ppermute | solution.py:23
  16.3 7.5 %collective-permute-done.1.rest_2_.rest_18_ = bf16[16,4736]{1,0:T(8,128)(2,1)S(1)} collective-permute-done((bf16[16,4736]{1,0:T(8,128)(2,1)}, bf16[16,4736]{1,0:T(8,128)(2,1)S(1)}, u32[]{:S(2)}, u32[]{:S(2)}) %collective-permute-start.1) | collective-permute-done | bytes 151584 | tf_op jit(solution)/shard_map/ppermute | solution.py:23
  24.3 1.5 %collective-permute-start.4 = (bf16[16,4736]{1,0:T(8,128)(2,1)S(1)}, bf16[16,4736]{1,0:T(8,128)(2,1)S(1)}, u32[]{:S(2)}, u32[]{:S(2)}) collective-permute-start(bf16[16,4736]{1,0:T(8,128)(2,1)S(1)} %collective-permute-done.rest_1_.rest_17_), channel_id=1, source_target_pairs={{0,2},{1,3},{2,0},{3,1},{4,6},{5,7},{6,4},{7,5},{8,10},{9,11},{10,... | collective-permute-start | bytes 454664 | tf_op jit(solution)/shard_map/ppermute | solution.py:23
  26.4 4.0 %collective-permute-done.5.rest_6_.rest_22_ = bf16[16,4736]{1,0:T(8,128)(2,1)S(1)} collective-permute-done((bf16[16,4736]{1,0:T(8,128)(2,1)S(1)}, bf16[16,4736]{1,0:T(8,128)(2,1)S(1)}, u32[]{:S(2)}, u32[]{:S(2)}) %collective-permute-start.5) | collective-permute-done | bytes 151584 | tf_op jit(solution)/shard_map/ppermute | solution.py:23
  30.4 1.6 %collective-permute-done.4.rest_5_.rest_21_ = bf16[16,4736]{1,0:T(8,128)(2,1)S(1)} collective-permute-done((bf16[16,4736]{1,0:T(8,128)(2,1)S(1)}, bf16[16,4736]{1,0:T(8,128)(2,1)S(1)}, u32[]{:S(2)}, u32[]{:S(2)}) %collective-permute-start.4) | collective-permute-done | bytes 151584 | tf_op jit(solution)/shard_map/ppermute | solution.py:23
  32.0 1.3 collective-permute-done.12.rest_13_.rest_29_
  33.4 0.9 copy-done.1
  34.3 1.2 copy-done.4
  35.5 1.2 copy-done.5
  36.7 0.7 copy-done.6
  37.4 0.7 copy-done.7
  38.1 5.4 %attend.1 = (bf16[2,288,256]{2,1,0:T(8,128)(2,1)S(1)}, bf16[2,288,256]{2,1,0:T(8,128)(2,1)S(1)}, bf16[2,288,256]{2,1,0:T(8,128)(2,1)S(1)}, bf16[2,288,256]{2,1,0...) custom-call(s32[1]{0:T(128)} %bitcast.me_ref, ...), custom_call_target="tpu_custom_call" | custom-call | tf_op jit(solution)/shard_map/attend/pallas_call | solution.py:383
  44.5 0.6 collective-permute-done.15
  45.2 0.6 collective-permute-start.16
  45.9 1.6 %collective-permute-start.19 = (bf16[288,256]{1,0:T(8,128)(2,1)S(1)}, bf16[288,256]{1,0:T(8,128)(2,1)S(1)}, u32[]{:S(2)}, u32[]{:S(2)}) collective-permute-start(bf16[288,256]{1,0:T(8,128)(2,1)S(1)} %slice_bitcast_fusion.4), channel_id=1, source_target_pairs={{0,2},{1,3},{2,0},{3,1},{4,6},{5,7},{6,4},{7,5},{8,10},{9,11},{10,... | collective-permute-start | bytes 442376 | tf_op jit(solution)/shard_map/ppermute | solution.py:23
  47.5 0.6 collective-permute-start.22
  48.2 1.6 %collective-permute-start.25 = (bf16[288,256]{1,0:T(8,128)(2,1)S(1)}, bf16[288,256]{1,0:T(8,128)(2,1)S(1)}, u32[]{:S(2)}, u32[]{:S(2)}) collective-permute-start(bf16[288,256]{1,0:T(8,128)(2,1)S(1)} %slice_bitcast_fusion), channel_id=1, source_target_pairs={{0,2},{1,3},{2,0},{3,1},{4,6},{5,7},{6,4},{7,5},{8,10},{9,11},{10,... | collective-permute-start | bytes 442376 | tf_op jit(solution)/shard_map/ppermute | solution.py:23
  49.8 2.2 %collective-permute-done.16 = bf16[288,256]{1,0:T(8,128)(2,1)S(1)} collective-permute-done((bf16[288,256]{1,0:T(8,128)(2,1)S(1)}, bf16[288,256]{1,0:T(8,128)(2,1)S(1)}, u32[]{:S(2)}, u32[]{:S(2)}) %collective-permute-start.16) | collective-permute-done | bytes 147488 | tf_op jit(solution)/shard_map/ppermute | solution.py:23
  52.0 2.3 %collective-permute-start.17 = (bf16[288,256]{1,0:T(8,128)(2,1)S(1)}, bf16[288,256]{1,0:T(8,128)(2,1)S(1)}, u32[]{:S(2)}, u32[]{:S(2)}) collective-permute-start(bf16[288,256]{1,0:T(8,128)(2,1)S(1)} %fusion.7), channel_id=1, source_target_pairs={{0,12},{1,13},{2,14},{3,15},{4,8},{5,9},{6,10},{7,11},{8,4},{9,5},... | collective-permute-start | bytes 442376 | tf_op jit(solution)/shard_map/ppermute | solution.py:23
  54.3 0.9 collective-permute-done.19
  55.2 4.3 %collective-permute-start.20 = (bf16[288,256]{1,0:T(8,128)(2,1)S(1)}, bf16[288,256]{1,0:T(8,128)(2,1)S(1)}, u32[]{:S(2)}, u32[]{:S(2)}) collective-permute-start(bf16[288,256]{1,0:T(8,128)(2,1)S(1)} %fusion.6), channel_id=1, source_target_pairs={{0,8},{1,9},{2,10},{3,11},{4,12},{5,13},{6,14},{7,15},{8,0},{9,1},... | collective-permute-start | bytes 442376 | tf_op jit(solution)/shard_map/ppermute | solution.py:23
  59.4 1.8 %collective-permute-start.23 = (bf16[288,256]{1,0:T(8,128)(2,1)S(1)}, bf16[288,256]{1,0:T(8,128)(2,1)S(1)}, u32[]{:S(2)}, u32[]{:S(2)}) collective-permute-start(bf16[288,256]{1,0:T(8,128)(2,1)S(1)} %fusion.5), channel_id=1, source_target_pairs={{0,4},{1,5},{2,6},{3,7},{4,0},{5,1},{6,2},{7,3},{8,12},{9,13},{10,... | collective-permute-start | bytes 442376 | tf_op jit(solution)/shard_map/ppermute | solution.py:23
  61.3 6.3 %collective-permute-done.20.rest_17_ = bf16[288,256]{1,0:T(8,128)(2,1)S(1)} collective-permute-done((bf16[288,256]{1,0:T(8,128)(2,1)S(1)}, bf16[288,256]{1,0:T(8,128)(2,1)S(1)}, u32[]{:S(2)}, u32[]{:S(2)}) %collective-permute-start.20) | collective-permute-done | bytes 147488 | tf_op jit(solution)/shard_map/ppermute | solution.py:23
  67.6 1.8 %combine.1 = (bf16[2,16,4096]{2,1,0:T(8,128)(2,1)S(1)}, bf16[2,16,4096]{2,1,0:T(8,128)(2,1)S(1)}, bf16[2,16,4096]{2,1,0:T(8,128)(2,1)S(1)}, bf16[2,16,4096]{2,1,...) custom-call(s32[1]{0:T(128)} %bitcast.me_ref, ...), custom_call_target="tpu_custom_call" | custom-call | tf_op jit(solution)/shard_map/combine/pallas_call | solution.py:407
  71.1 0.6 collective-permute-start.27
  71.8 1.6 %collective-permute-start.30 = (bf16[16,4096]{1,0:T(8,128)(2,1)S(1)}, bf16[16,4096]{1,0:T(8,128)(2,1)S(1)}, u32[]{:S(2)}, u32[]{:S(2)}) collective-permute-start(bf16[16,4096]{1,0:T(8,128)(2,1)S(1)} %slice_bitcast_fusion.20), channel_id=1, source_target_pairs={{0,2},{1,3},{2,0},{3,1},{4,6},{5,7},{6,4},{7,5},{8,10},{9,11},{10,... | collective-permute-start | bytes 393224 | tf_op jit(solution)/shard_map/ppermute | solution.py:23
  73.4 0.6 collective-permute-start.33
  74.1 1.6 %collective-permute-start.36 = (bf16[16,4096]{1,0:T(8,128)(2,1)S(1)}, bf16[16,4096]{1,0:T(8,128)(2,1)S(1)}, u32[]{:S(2)}, u32[]{:S(2)}) collective-permute-start(bf16[16,4096]{1,0:T(8,128)(2,1)S(1)} %slice_bitcast_fusion.16), channel_id=1, source_target_pairs={{0,2},{1,3},{2,0},{3,1},{4,6},{5,7},{6,4},{7,5},{8,10},{9,11},{10,... | collective-permute-start | bytes 393224 | tf_op jit(solution)/shard_map/ppermute | solution.py:23
  75.7 1.8 %collective-permute-done.27 = bf16[16,4096]{1,0:T(8,128)(2,1)S(1)} collective-permute-done((bf16[16,4096]{1,0:T(8,128)(2,1)S(1)}, bf16[16,4096]{1,0:T(8,128)(2,1)S(1)}, u32[]{:S(2)}, u32[]{:S(2)}) %collective-permute-start.27) | collective-permute-done | bytes 131104 | tf_op jit(solution)/shard_map/ppermute | solution.py:23
  77.5 2.2 %collective-permute-start.28 = (bf16[16,4096]{1,0:T(8,128)(2,1)S(1)}, bf16[16,4096]{1,0:T(8,128)(2,1)S(1)}, u32[]{:S(2)}, u32[]{:S(2)}) collective-permute-start(bf16[16,4096]{1,0:T(8,128)(2,1)S(1)} %fusion.15), channel_id=1, source_target_pairs={{0,12},{1,13},{2,14},{3,15},{4,8},{5,9},{6,10},{7,11},{8,4},{9,5},... | collective-permute-start | bytes 393224 | tf_op jit(solution)/shard_map/ppermute | solution.py:23
  79.8 0.6 collective-permute-done.30
  80.5 2.7 %collective-permute-done.33 = bf16[16,4096]{1,0:T(8,128)(2,1)S(1)} collective-permute-done((bf16[16,4096]{1,0:T(8,128)(2,1)S(1)}, bf16[16,4096]{1,0:T(8,128)(2,1)S(1)}, u32[]{:S(2)}, u32[]{:S(2)}) %collective-permute-start.33) | collective-permute-done | bytes 131104 | tf_op jit(solution)/shard_map/ppermute | solution.py:23
  83.3 1.9 %collective-permute-done.36 = bf16[16,4096]{1,0:T(8,128)(2,1)S(1)} collective-permute-done((bf16[16,4096]{1,0:T(8,128)(2,1)S(1)}, bf16[16,4096]{1,0:T(8,128)(2,1)S(1)}, u32[]{:S(2)}, u32[]{:S(2)}) %collective-permute-start.36) | collective-permute-done | bytes 131104 | tf_op jit(solution)/shard_map/ppermute | solution.py:23
  85.1 4.8 %collective-permute-done.31 = bf16[16,4096]{1,0:T(8,128)(2,1)S(1)} collective-permute-done((bf16[16,4096]{1,0:T(8,128)(2,1)S(1)}, bf16[16,4096]{1,0:T(8,128)(2,1)S(1)}, u32[]{:S(2)}, u32[]{:S(2)}) %collective-permute-start.31) | collective-permute-done | bytes 131104 | tf_op jit(solution)/shard_map/ppermute | solution.py:23
  89.9 0.6 collective-permute-done.34
  90.9 0.6 collective-permute-start.40
  91.4 2.0 %collective-permute-start.39 = (bf16[16,4096]{1,0:T(8,128)(2,1)S(1)}, bf16[16,4096]{1,0:T(8,128)(2,1)S(1)}, u32[]{:S(2)}, u32[]{:S(2)}) collective-permute-start(bf16[16,4096]{1,0:T(8,128)(2,1)S(1)} %fusion.2.rest_0_), channel_id=1, source_target_pairs={{0,12},{1,13},{2,14},{3,15},{4,8},{5,9},{6,10},{7,11},{8,4},{9,5},... | collective-permute-start | bytes 393224 | tf_op jit(solution)/shard_map/ppermute | solution.py:23
  93.4 2.4 %collective-permute-start.37 = (bf16[16,4096]{1,0:T(8,128)(2,1)S(1)}, bf16[16,4096]{1,0:T(8,128)(2,1)S(1)}, u32[]{:S(2)}, u32[]{:S(2)}) collective-permute-start(bf16[16,4096]{1,0:T(8,128)(2,1)S(1)} %fusion.2.rest_0_), channel_id=1, source_target_pairs={{0,4},{1,5},{2,6},{3,7},{4,0},{5,1},{6,2},{7,3},{8,12},{9,13},{10,... | collective-permute-start | bytes 393224 | tf_op jit(solution)/shard_map/ppermute | solution.py:23
  95.9 3.8 %collective-permute-done.39.rest_3_ = bf16[16,4096]{1,0:T(8,128)(2,1)S(1)} collective-permute-done((bf16[16,4096]{1,0:T(8,128)(2,1)S(1)}, bf16[16,4096]{1,0:T(8,128)(2,1)S(1)}, u32[]{:S(2)}, u32[]{:S(2)}) %collective-permute-start.39) | collective-permute-done | bytes 131104 | tf_op jit(solution)/shard_map/ppermute | solution.py:23
  99.7 1.5 %collective-permute-start.43 = (bf16[16,4096]{1,0:T(8,128)(2,1)S(1)}, bf16[16,4096]{1,0:T(8,128)(2,1)S(1)}, u32[]{:S(2)}, u32[]{:S(2)}) collective-permute-start(bf16[16,4096]{1,0:T(8,128)(2,1)S(1)} %collective-permute-done.39.rest_3_), channel_id=1, source_target_pairs={{0,2},{1,3},{2,0},{3,1},{4,6},{5,7},{6,4},{7,5},{8,10},{9,11},{10,... | collective-permute-start | bytes 393224 | tf_op jit(solution)/shard_map/ppermute | solution.py:23
  101.2 2.6 %collective-permute-done.38.rest_2_ = bf16[16,4096]{1,0:T(8,128)(2,1)S(1)} collective-permute-done((bf16[16,4096]{1,0:T(8,128)(2,1)S(1)}, bf16[16,4096]{1,0:T(8,128)(2,1)S(1)}, u32[]{:S(2)}, u32[]{:S(2)}) %collective-permute-start.38) | collective-permute-done | bytes 131104 | tf_op jit(solution)/shard_map/ppermute | solution.py:23
  103.8 1.5 %collective-permute-start.42 = (bf16[16,4096]{1,0:T(8,128)(2,1)S(1)}, bf16[16,4096]{1,0:T(8,128)(2,1)S(1)}, u32[]{:S(2)}, u32[]{:S(2)}) collective-permute-start(bf16[16,4096]{1,0:T(8,128)(2,1)S(1)} %collective-permute-done.38.rest_2_), channel_id=1, source_target_pairs={{0,2},{1,3},{2,0},{3,1},{4,6},{5,7},{6,4},{7,5},{8,10},{9,11},{10,... | collective-permute-start | bytes 393224 | tf_op jit(solution)/shard_map/ppermute | solution.py:23
  105.4 0.5 collective-permute-start.41
  106.6 3.6 %collective-permute-done.42.rest_6_ = bf16[16,4096]{1,0:T(8,128)(2,1)S(1)} collective-permute-done((bf16[16,4096]{1,0:T(8,128)(2,1)S(1)}, bf16[16,4096]{1,0:T(8,128)(2,1)S(1)}, u32[]{:S(2)}, u32[]{:S(2)}) %collective-permute-start.42) | collective-permute-done | bytes 131104 | tf_op jit(solution)/shard_map/ppermute | solution.py:23
  110.2 1.9 %collective-permute-done.41.rest_5_ = bf16[16,4096]{1,0:T(8,128)(2,1)S(1)} collective-permute-done((bf16[16,4096]{1,0:T(8,128)(2,1)S(1)}, bf16[16,4096]{1,0:T(8,128)(2,1)S(1)}, u32[]{:S(2)}, u32[]{:S(2)}) %collective-permute-start.41) | collective-permute-done | bytes 131104 | tf_op jit(solution)/shard_map/ppermute | solution.py:23
  112.1 1.3 collective-permute-done.49.rest_13_
  113.4 7.9 %experts.1 = (bf16[2,16,4096]{2,1,0:T(8,128)(2,1)S(1)}, bf16[2,16,4096]{2,1,0:T(8,128)(2,1)S(1)}, bf16[2,16,4096]{2,1,0:T(8,128)(2,1)S(1)}, bf16[2,16,4096]{2,1,...) custom-call(s32[1]{0:T(128)} %bitcast.me_ref, ...), custom_call_target="tpu_custom_call" | custom-call | tf_op jit(solution)/shard_map/experts/pallas_call | solution.py:428
  123.1 1.6 %collective-permute-start.53 = (bf16[16,4096]{1,0:T(8,128)(2,1)S(1)}, bf16[16,4096]{1,0:T(8,128)(2,1)S(1)}, u32[]{:S(2)}, u32[]{:S(2)}) collective-permute-start(bf16[16,4096]{1,0:T(8,128)(2,1)S(1)} %slice_bitcast_fusion.14), channel_id=1, source_target_pairs={{0,2},{1,3},{2,0},{3,1},{4,6},{5,7},{6,4},{7,5},{8,10},{9,11},{10,... | collective-permute-start | bytes 393224 | tf_op jit(solution)/shard_map/ppermute | solution.py:23
  124.7 0.6 collective-permute-start.56
  125.4 1.6 %collective-permute-start.59 = (bf16[16,4096]{1,0:T(8,128)(2,1)S(1)}, bf16[16,4096]{1,0:T(8,128)(2,1)S(1)}, u32[]{:S(2)}, u32[]{:S(2)}) collective-permute-start(bf16[16,4096]{1,0:T(8,128)(2,1)S(1)} %slice_bitcast_fusion.10), channel_id=1, source_target_pairs={{0,2},{1,3},{2,0},{3,1},{4,6},{5,7},{6,4},{7,5},{8,10},{9,11},{10,... | collective-permute-start | bytes 393224 | tf_op jit(solution)/shard_map/ppermute | solution.py:23
  127.0 0.6 collective-permute-start.62
  127.6 1.9 %collective-permute-done.53 = bf16[16,4096]{1,0:T(8,128)(2,1)S(1)} collective-permute-done((bf16[16,4096]{1,0:T(8,128)(2,1)S(1)}, bf16[16,4096]{1,0:T(8,128)(2,1)S(1)}, u32[]{:S(2)}, u32[]{:S(2)}) %collective-permute-start.53) | collective-permute-done | bytes 131104 | tf_op jit(solution)/shard_map/ppermute | solution.py:23
  129.5 2.1 %collective-permute-start.54 = (bf16[16,4096]{1,0:T(8,128)(2,1)S(1)}, bf16[16,4096]{1,0:T(8,128)(2,1)S(1)}, u32[]{:S(2)}, u32[]{:S(2)}) collective-permute-start(bf16[16,4096]{1,0:T(8,128)(2,1)S(1)} %fusion.11), channel_id=1, source_target_pairs={{0,12},{1,13},{2,14},{3,15},{4,8},{5,9},{6,10},{7,11},{8,4},{9,5},... | collective-permute-start | bytes 393224 | tf_op jit(solution)/shard_map/ppermute | solution.py:23
  131.6 0.7 collective-permute-done.56
  132.8 2.4 %collective-permute-done.59 = bf16[16,4096]{1,0:T(8,128)(2,1)S(1)} collective-permute-done((bf16[16,4096]{1,0:T(8,128)(2,1)S(1)}, bf16[16,4096]{1,0:T(8,128)(2,1)S(1)}, u32[]{:S(2)}, u32[]{:S(2)}) %collective-permute-start.59) | collective-permute-done | bytes 131104 | tf_op jit(solution)/shard_map/ppermute | solution.py:23
  135.2 1.9 %collective-permute-done.62 = bf16[16,4096]{1,0:T(8,128)(2,1)S(1)} collective-permute-done((bf16[16,4096]{1,0:T(8,128)(2,1)S(1)}, bf16[16,4096]{1,0:T(8,128)(2,1)S(1)}, u32[]{:S(2)}, u32[]{:S(2)}) %collective-permute-start.62) | collective-permute-done | bytes 131104 | tf_op jit(solution)/shard_map/ppermute | solution.py:23
  137.1 5.1 %collective-permute-done.57 = bf16[16,4096]{1,0:T(8,128)(2,1)S(1)} collective-permute-done((bf16[16,4096]{1,0:T(8,128)(2,1)S(1)}, bf16[16,4096]{1,0:T(8,128)(2,1)S(1)}, u32[]{:S(2)}, u32[]{:S(2)}) %collective-permute-start.57) | collective-permute-done | bytes 131104 | tf_op jit(solution)/shard_map/ppermute | solution.py:23
  142.4 0.8 fusion.3
  (132 shorter events, 9.2 us)
Async XLA Ops:
  4.4 7.4 %collective-permute-start.3 = (bf16[16,4736]{1,0:T(8,128)(2,1)}, bf16[16,4736]{1,0:T(8,128)(2,1)S(1)}, u32[]{:S(2)}, u32[]{:S(2)}) collective-permute-start(bf16[16,4736]{1,0:T(8,128)(2,1)} %payload.1.rest_0_.rest_16_), channel_id=1, source_target_pairs={{0,2},{1,3},{2,0},{3,1},{4,6},{5,7},{6,4},{7,5},{8,10},{9,11},{10,... | collective-permute-start | bytes 454664 | tf_op jit(solution)/shard_map/ppermute | solution.py:23
  7.4 8.3 %collective-permute-start.2 = (bf16[16,4736]{1,0:T(8,128)(2,1)}, bf16[16,4736]{1,0:T(8,128)(2,1)S(1)}, u32[]{:S(2)}, u32[]{:S(2)}) collective-permute-start(bf16[16,4736]{1,0:T(8,128)(2,1)} %payload.1.rest_0_.rest_16_), channel_id=1, source_target_pairs={{0,12},{1,13},{2,14},{3,15},{4,8},{5,9},{6,10},{7,11},{8,4},{9,5},... | collective-permute-start | bytes 454664 | tf_op jit(solution)/shard_map/ppermute | solution.py:23
  11.0 4.8 %collective-permute-start.7 = (bf16[16,4736]{1,0:T(8,128)(2,1)}, bf16[16,4736]{1,0:T(8,128)(2,1)S(1)}, u32[]{:S(2)}, u32[]{:S(2)}) collective-permute-start(bf16[16,4736]{1,0:T(8,128)(2,1)} %payload.1.rest_0_.rest_16_), channel_id=1, source_target_pairs={{0,1},{1,0},{2,3},{3,2},{4,5},{5,4},{6,7},{7,6},{8,9},{9,8},{10,11... | collective-permute-start | bytes 454664 | tf_op jit(solution)/shard_map/ppermute | solution.py:23
  11.0 12.8 %collective-permute-start.1 = (bf16[16,4736]{1,0:T(8,128)(2,1)}, bf16[16,4736]{1,0:T(8,128)(2,1)S(1)}, u32[]{:S(2)}, u32[]{:S(2)}) collective-permute-start(bf16[16,4736]{1,0:T(8,128)(2,1)} %payload.1.rest_0_.rest_16_), channel_id=1, source_target_pairs={{0,8},{1,9},{2,10},{3,11},{4,12},{5,13},{6,14},{7,15},{8,0},{9,1},... | collective-permute-start | bytes 454664 | tf_op jit(solution)/shard_map/ppermute | solution.py:23
  11.0 13.3 %collective-permute-start = (bf16[16,4736]{1,0:T(8,128)(2,1)}, bf16[16,4736]{1,0:T(8,128)(2,1)S(1)}, u32[]{:S(2)}, u32[]{:S(2)}) collective-permute-start(bf16[16,4736]{1,0:T(8,128)(2,1)} %payload.1.rest_0_.rest_16_), channel_id=1, source_target_pairs={{0,4},{1,5},{2,6},{3,7},{4,0},{5,1},{6,2},{7,3},{8,12},{9,13},{10,... | collective-permute-start | bytes 454664 | tf_op jit(solution)/shard_map/ppermute | solution.py:23
  11.8 14.0 %collective-permute-start.11 = (bf16[16,4736]{1,0:T(8,128)(2,1)S(1)}, bf16[16,4736]{1,0:T(8,128)(2,1)S(1)}, u32[]{:S(2)}, u32[]{:S(2)}) collective-permute-start(bf16[16,4736]{1,0:T(8,128)(2,1)S(1)} %collective-permute-done.3.rest_4_.rest_20_), channel_id=1, source_target_pairs={{0,1},{1,0},{2,3},{3,2},{4,5},{5,4},{6,7},{7,6},{8,9},{9,8},{10,11... | collective-permute-start | bytes 454664 | tf_op jit(solution)/shard_map/ppermute | solution.py:23
  15.8 10.1 %collective-permute-start.10 = (bf16[16,4736]{1,0:T(8,128)(2,1)S(1)}, bf16[16,4736]{1,0:T(8,128)(2,1)S(1)}, u32[]{:S(2)}, u32[]{:S(2)}) collective-permute-start(bf16[16,4736]{1,0:T(8,128)(2,1)S(1)} %collective-permute-done.2.rest_3_.rest_19_), channel_id=1, source_target_pairs={{0,1},{1,0},{2,3},{3,2},{4,5},{5,4},{6,7},{7,6},{8,9},{9,8},{10,11... | collective-permute-start | bytes 454664 | tf_op jit(solution)/shard_map/ppermute | solution.py:23
  15.8 10.6 %collective-permute-start.6 = (bf16[16,4736]{1,0:T(8,128)(2,1)S(1)}, bf16[16,4736]{1,0:T(8,128)(2,1)S(1)}, u32[]{:S(2)}, u32[]{:S(2)}) collective-permute-start(bf16[16,4736]{1,0:T(8,128)(2,1)S(1)} %collective-permute-done.2.rest_3_.rest_19_), channel_id=1, source_target_pairs={{0,2},{1,3},{2,0},{3,1},{4,6},{5,7},{6,4},{7,5},{8,10},{9,11},{10,... | collective-permute-start | bytes 454664 | tf_op jit(solution)/shard_map/ppermute | solution.py:23
  23.8 6.6 %collective-permute-start.5 = (bf16[16,4736]{1,0:T(8,128)(2,1)S(1)}, bf16[16,4736]{1,0:T(8,128)(2,1)S(1)}, u32[]{:S(2)}, u32[]{:S(2)}) collective-permute-start(bf16[16,4736]{1,0:T(8,128)(2,1)S(1)} %collective-permute-done.1.rest_2_.rest_18_), channel_id=1, source_target_pairs={{0,2},{1,3},{2,0},{3,1},{4,6},{5,7},{6,4},{7,5},{8,10},{9,11},{10,... | collective-permute-start | bytes 454664 | tf_op jit(solution)/shard_map/ppermute | solution.py:23
  24.3 7.7 %collective-permute-start.4 = (bf16[16,4736]{1,0:T(8,128)(2,1)S(1)}, bf16[16,4736]{1,0:T(8,128)(2,1)S(1)}, u32[]{:S(2)}, u32[]{:S(2)}) collective-permute-start(bf16[16,4736]{1,0:T(8,128)(2,1)S(1)} %collective-permute-done.rest_1_.rest_17_), channel_id=1, source_target_pairs={{0,2},{1,3},{2,0},{3,1},{4,6},{5,7},{6,4},{7,5},{8,10},{9,11},{10,... | collective-permute-start | bytes 454664 | tf_op jit(solution)/shard_map/ppermute | solution.py:23
  25.8 6.2 %collective-permute-start.9 = (bf16[16,4736]{1,0:T(8,128)(2,1)S(1)}, bf16[16,4736]{1,0:T(8,128)(2,1)S(1)}, u32[]{:S(2)}, u32[]{:S(2)}) collective-permute-start(bf16[16,4736]{1,0:T(8,128)(2,1)S(1)} %collective-permute-done.1.rest_2_.rest_18_), channel_id=1, source_target_pairs={{0,1},{1,0},{2,3},{3,2},{4,5},{5,4},{6,7},{7,6},{8,9},{9,8},{10,11... | collective-permute-start | bytes 454664 | tf_op jit(solution)/shard_map/ppermute | solution.py:23
  25.8 6.2 %collective-permute-start.8 = (bf16[16,4736]{1,0:T(8,128)(2,1)S(1)}, bf16[16,4736]{1,0:T(8,128)(2,1)S(1)}, u32[]{:S(2)}, u32[]{:S(2)}) collective-permute-start(bf16[16,4736]{1,0:T(8,128)(2,1)S(1)} %collective-permute-done.rest_1_.rest_17_), channel_id=1, source_target_pairs={{0,1},{1,0},{2,3},{3,2},{4,5},{5,4},{6,7},{7,6},{8,9},{9,8},{10,11... | collective-permute-start | bytes 454664 | tf_op jit(solution)/shard_map/ppermute | solution.py:23
  26.3 5.7 %collective-permute-start.14 = (bf16[16,4736]{1,0:T(8,128)(2,1)S(1)}, bf16[16,4736]{1,0:T(8,128)(2,1)S(1)}, u32[]{:S(2)}, u32[]{:S(2)}) collective-permute-start(bf16[16,4736]{1,0:T(8,128)(2,1)S(1)} %collective-permute-done.6.rest_7_.rest_23_), channel_id=1, source_target_pairs={{0,1},{1,0},{2,3},{3,2},{4,5},{5,4},{6,7},{7,6},{8,9},{9,8},{10,11... | collective-permute-start | bytes 454664 | tf_op jit(solution)/shard_map/ppermute | solution.py:23
  30.4 1.6 %collective-permute-start.13 = (bf16[16,4736]{1,0:T(8,128)(2,1)S(1)}, bf16[16,4736]{1,0:T(8,128)(2,1)S(1)}, u32[]{:S(2)}, u32[]{:S(2)}) collective-permute-start(bf16[16,4736]{1,0:T(8,128)(2,1)S(1)} %collective-permute-done.5.rest_6_.rest_22_), channel_id=1, source_target_pairs={{0,1},{1,0},{2,3},{3,2},{4,5},{5,4},{6,7},{7,6},{8,9},{9,8},{10,11... | collective-permute-start | bytes 454664 | tf_op jit(solution)/shard_map/ppermute | solution.py:23
  32.0 1.4 collective-permute-start.12
  43.4 1.6 %collective-permute-start.15 = (bf16[2,288,256]{2,1,0:T(8,128)(2,1)S(1)}, bf16[2,288,256]{2,1,0:T(8,128)(2,1)S(1)}, u32[]{:S(2)}, u32[]{:S(2)}) collective-permute-start(bf16[2,288,256]{2,1,0:T(8,128)(2,1)S(1)} %get-tuple-element.30), channel_id=1, source_target_pairs={{0,1},{1,0},{2,3},{3,2},{4,5},{5,4},{6,7},{7,6},{8,9},{9,8},{10,11... | collective-permute-start | bytes 884744 | tf_op jit(solution)/shard_map/ppermute | solution.py:23
  43.6 2.1 %collective-permute-start.18 = (bf16[2,288,256]{2,1,0:T(8,128)(2,1)S(1)}, bf16[2,288,256]{2,1,0:T(8,128)(2,1)S(1)}, u32[]{:S(2)}, u32[]{:S(2)}) collective-permute-start(bf16[2,288,256]{2,1,0:T(8,128)(2,1)S(1)} %get-tuple-element.32), channel_id=1, source_target_pairs={{0,1},{1,0},{2,3},{3,2},{4,5},{5,4},{6,7},{7,6},{8,9},{9,8},{10,11... | collective-permute-start | bytes 884744 | tf_op jit(solution)/shard_map/ppermute | solution.py:23
  44.0 3.4 %collective-permute-start.21 = (bf16[2,288,256]{2,1,0:T(8,128)(2,1)S(1)}, bf16[2,288,256]{2,1,0:T(8,128)(2,1)S(1)}, u32[]{:S(2)}, u32[]{:S(2)}) collective-permute-start(bf16[2,288,256]{2,1,0:T(8,128)(2,1)S(1)} %get-tuple-element.34), channel_id=1, source_target_pairs={{0,1},{1,0},{2,3},{3,2},{4,5},{5,4},{6,7},{7,6},{8,9},{9,8},{10,11... | collective-permute-start | bytes 884744 | tf_op jit(solution)/shard_map/ppermute | solution.py:23
  44.1 4.0 %collective-permute-start.24 = (bf16[2,288,256]{2,1,0:T(8,128)(2,1)S(1)}, bf16[2,288,256]{2,1,0:T(8,128)(2,1)S(1)}, u32[]{:S(2)}, u32[]{:S(2)}) collective-permute-start(bf16[2,288,256]{2,1,0:T(8,128)(2,1)S(1)} %get-tuple-element.36), channel_id=1, source_target_pairs={{0,1},{1,0},{2,3},{3,2},{4,5},{5,4},{6,7},{7,6},{8,9},{9,8},{10,11... | collective-permute-start | bytes 884744 | tf_op jit(solution)/shard_map/ppermute | solution.py:23
  45.2 6.8 %collective-permute-start.16 = (bf16[288,256]{1,0:T(8,128)(2,1)S(1)}, bf16[288,256]{1,0:T(8,128)(2,1)S(1)}, u32[]{:S(2)}, u32[]{:S(2)}) collective-permute-start(bf16[288,256]{1,0:T(8,128)(2,1)S(1)} %slice_bitcast_fusion.6), channel_id=1, source_target_pairs={{0,2},{1,3},{2,0},{3,1},{4,6},{5,7},{6,4},{7,5},{8,10},{9,11},{10,... | collective-permute-start | bytes 442376 | tf_op jit(solution)/shard_map/ppermute | solution.py:23
  45.9 9.3 %collective-permute-start.19 = (bf16[288,256]{1,0:T(8,128)(2,1)S(1)}, bf16[288,256]{1,0:T(8,128)(2,1)S(1)}, u32[]{:S(2)}, u32[]{:S(2)}) collective-permute-start(bf16[288,256]{1,0:T(8,128)(2,1)S(1)} %slice_bitcast_fusion.4), channel_id=1, source_target_pairs={{0,2},{1,3},{2,0},{3,1},{4,6},{5,7},{6,4},{7,5},{8,10},{9,11},{10,... | collective-permute-start | bytes 442376 | tf_op jit(solution)/shard_map/ppermute | solution.py:23
  47.5 11.9 %collective-permute-start.22 = (bf16[288,256]{1,0:T(8,128)(2,1)S(1)}, bf16[288,256]{1,0:T(8,128)(2,1)S(1)}, u32[]{:S(2)}, u32[]{:S(2)}) collective-permute-start(bf16[288,256]{1,0:T(8,128)(2,1)S(1)} %slice_bitcast_fusion.2), channel_id=1, source_target_pairs={{0,2},{1,3},{2,0},{3,1},{4,6},{5,7},{6,4},{7,5},{8,10},{9,11},{10,... | collective-permute-start | bytes 442376 | tf_op jit(solution)/shard_map/ppermute | solution.py:23
  48.2 13.1 %collective-permute-start.25 = (bf16[288,256]{1,0:T(8,128)(2,1)S(1)}, bf16[288,256]{1,0:T(8,128)(2,1)S(1)}, u32[]{:S(2)}, u32[]{:S(2)}) collective-permute-start(bf16[288,256]{1,0:T(8,128)(2,1)S(1)} %slice_bitcast_fusion), channel_id=1, source_target_pairs={{0,2},{1,3},{2,0},{3,1},{4,6},{5,7},{6,4},{7,5},{8,10},{9,11},{10,... | collective-permute-start | bytes 442376 | tf_op jit(solution)/shard_map/ppermute | solution.py:23
  52.0 61.5 %slice-start = ((s8[6291456]{0:T(1024)(128)(4,1)}), s8[4194304]{0:T(1024)(128)(4,1)S(1)}, s32[]{:S(2)}) async-start(s8[6291456]{0:T(1024)(128)(4,1)} %bitcast.82), calls=%async_computation | async-start | bytes 8388608
  52.0 9.3 %collective-permute-start.17 = (bf16[288,256]{1,0:T(8,128)(2,1)S(1)}, bf16[288,256]{1,0:T(8,128)(2,1)S(1)}, u32[]{:S(2)}, u32[]{:S(2)}) collective-permute-start(bf16[288,256]{1,0:T(8,128)(2,1)S(1)} %fusion.7), channel_id=1, source_target_pairs={{0,12},{1,13},{2,14},{3,15},{4,8},{5,9},{6,10},{7,11},{8,4},{9,5},... | collective-permute-start | bytes 442376 | tf_op jit(solution)/shard_map/ppermute | solution.py:23
  55.2 12.5 %collective-permute-start.20 = (bf16[288,256]{1,0:T(8,128)(2,1)S(1)}, bf16[288,256]{1,0:T(8,128)(2,1)S(1)}, u32[]{:S(2)}, u32[]{:S(2)}) collective-permute-start(bf16[288,256]{1,0:T(8,128)(2,1)S(1)} %fusion.6), channel_id=1, source_target_pairs={{0,8},{1,9},{2,10},{3,11},{4,12},{5,13},{6,14},{7,15},{8,0},{9,1},... | collective-permute-start | bytes 442376 | tf_op jit(solution)/shard_map/ppermute | solution.py:23
  59.4 8.2 %collective-permute-start.23 = (bf16[288,256]{1,0:T(8,128)(2,1)S(1)}, bf16[288,256]{1,0:T(8,128)(2,1)S(1)}, u32[]{:S(2)}, u32[]{:S(2)}) collective-permute-start(bf16[288,256]{1,0:T(8,128)(2,1)S(1)} %fusion.5), channel_id=1, source_target_pairs={{0,4},{1,5},{2,6},{3,7},{4,0},{5,1},{6,2},{7,3},{8,12},{9,13},{10,... | collective-permute-start | bytes 442376 | tf_op jit(solution)/shard_map/ppermute | solution.py:23
  69.4 1.6 %collective-permute-start.26 = (bf16[2,16,4096]{2,1,0:T(8,128)(2,1)S(1)}, bf16[2,16,4096]{2,1,0:T(8,128)(2,1)S(1)}, u32[]{:S(2)}, u32[]{:S(2)}) collective-permute-start(bf16[2,16,4096]{2,1,0:T(8,128)(2,1)S(1)} %get-tuple-element.38), channel_id=1, source_target_pairs={{0,1},{1,0},{2,3},{3,2},{4,5},{5,4},{6,7},{7,6},{8,9},{9,8},{10,11... | collective-permute-start | bytes 786440 | tf_op jit(solution)/shard_map/ppermute | solution.py:23
  69.5 2.2 %collective-permute-start.29 = (bf16[2,16,4096]{2,1,0:T(8,128)(2,1)S(1)}, bf16[2,16,4096]{2,1,0:T(8,128)(2,1)S(1)}, u32[]{:S(2)}, u32[]{:S(2)}) collective-permute-start(bf16[2,16,4096]{2,1,0:T(8,128)(2,1)S(1)} %get-tuple-element.40), channel_id=1, source_target_pairs={{0,1},{1,0},{2,3},{3,2},{4,5},{5,4},{6,7},{7,6},{8,9},{9,8},{10,11... | collective-permute-start | bytes 786440 | tf_op jit(solution)/shard_map/ppermute | solution.py:23
  70.0 3.4 %collective-permute-start.32 = (bf16[2,16,4096]{2,1,0:T(8,128)(2,1)S(1)}, bf16[2,16,4096]{2,1,0:T(8,128)(2,1)S(1)}, u32[]{:S(2)}, u32[]{:S(2)}) collective-permute-start(bf16[2,16,4096]{2,1,0:T(8,128)(2,1)S(1)} %get-tuple-element.42), channel_id=1, source_target_pairs={{0,1},{1,0},{2,3},{3,2},{4,5},{5,4},{6,7},{7,6},{8,9},{9,8},{10,11... | collective-permute-start | bytes 786440 | tf_op jit(solution)/shard_map/ppermute | solution.py:23
  70.1 4.0 %collective-permute-start.35 = (bf16[2,16,4096]{2,1,0:T(8,128)(2,1)S(1)}, bf16[2,16,4096]{2,1,0:T(8,128)(2,1)S(1)}, u32[]{:S(2)}, u32[]{:S(2)}) collective-permute-start(bf16[2,16,4096]{2,1,0:T(8,128)(2,1)S(1)} %get-tuple-element.44), channel_id=1, source_target_pairs={{0,1},{1,0},{2,3},{3,2},{4,5},{5,4},{6,7},{7,6},{8,9},{9,8},{10,11... | collective-permute-start | bytes 786440 | tf_op jit(solution)/shard_map/ppermute | solution.py:23
  71.1 6.4 %collective-permute-start.27 = (bf16[16,4096]{1,0:T(8,128)(2,1)S(1)}, bf16[16,4096]{1,0:T(8,128)(2,1)S(1)}, u32[]{:S(2)}, u32[]{:S(2)}) collective-permute-start(bf16[16,4096]{1,0:T(8,128)(2,1)S(1)} %slice_bitcast_fusion.22), channel_id=1, source_target_pairs={{0,2},{1,3},{2,0},{3,1},{4,6},{5,7},{6,4},{7,5},{8,10},{9,11},{10,... | collective-permute-start | bytes 393224 | tf_op jit(solution)/shard_map/ppermute | solution.py:23
  71.8 8.5 %collective-permute-start.30 = (bf16[16,4096]{1,0:T(8,128)(2,1)S(1)}, bf16[16,4096]{1,0:T(8,128)(2,1)S(1)}, u32[]{:S(2)}, u32[]{:S(2)}) collective-permute-start(bf16[16,4096]{1,0:T(8,128)(2,1)S(1)} %slice_bitcast_fusion.20), channel_id=1, source_target_pairs={{0,2},{1,3},{2,0},{3,1},{4,6},{5,7},{6,4},{7,5},{8,10},{9,11},{10,... | collective-permute-start | bytes 393224 | tf_op jit(solution)/shard_map/ppermute | solution.py:23
  73.4 9.7 %collective-permute-start.33 = (bf16[16,4096]{1,0:T(8,128)(2,1)S(1)}, bf16[16,4096]{1,0:T(8,128)(2,1)S(1)}, u32[]{:S(2)}, u32[]{:S(2)}) collective-permute-start(bf16[16,4096]{1,0:T(8,128)(2,1)S(1)} %slice_bitcast_fusion.18), channel_id=1, source_target_pairs={{0,2},{1,3},{2,0},{3,1},{4,6},{5,7},{6,4},{7,5},{8,10},{9,11},{10,... | collective-permute-start | bytes 393224 | tf_op jit(solution)/shard_map/ppermute | solution.py:23
  74.1 11.0 %collective-permute-start.36 = (bf16[16,4096]{1,0:T(8,128)(2,1)S(1)}, bf16[16,4096]{1,0:T(8,128)(2,1)S(1)}, u32[]{:S(2)}, u32[]{:S(2)}) collective-permute-start(bf16[16,4096]{1,0:T(8,128)(2,1)S(1)} %slice_bitcast_fusion.16), channel_id=1, source_target_pairs={{0,2},{1,3},{2,0},{3,1},{4,6},{5,7},{6,4},{7,5},{8,10},{9,11},{10,... | collective-permute-start | bytes 393224 | tf_op jit(solution)/shard_map/ppermute | solution.py:23
  77.5 7.6 %collective-permute-start.28 = (bf16[16,4096]{1,0:T(8,128)(2,1)S(1)}, bf16[16,4096]{1,0:T(8,128)(2,1)S(1)}, u32[]{:S(2)}, u32[]{:S(2)}) collective-permute-start(bf16[16,4096]{1,0:T(8,128)(2,1)S(1)} %fusion.15), channel_id=1, source_target_pairs={{0,12},{1,13},{2,14},{3,15},{4,8},{5,9},{6,10},{7,11},{8,4},{9,5},... | collective-permute-start | bytes 393224 | tf_op jit(solution)/shard_map/ppermute | solution.py:23
  80.3 9.5 %collective-permute-start.31 = (bf16[16,4096]{1,0:T(8,128)(2,1)S(1)}, bf16[16,4096]{1,0:T(8,128)(2,1)S(1)}, u32[]{:S(2)}, u32[]{:S(2)}) collective-permute-start(bf16[16,4096]{1,0:T(8,128)(2,1)S(1)} %fusion.14), channel_id=1, source_target_pairs={{0,8},{1,9},{2,10},{3,11},{4,12},{5,13},{6,14},{7,15},{8,0},{9,1},... | collective-permute-start | bytes 393224 | tf_op jit(solution)/shard_map/ppermute | solution.py:23
  83.2 7.3 %collective-permute-start.34 = (bf16[16,4096]{1,0:T(8,128)(2,1)S(1)}, bf16[16,4096]{1,0:T(8,128)(2,1)S(1)}, u32[]{:S(2)}, u32[]{:S(2)}) collective-permute-start(bf16[16,4096]{1,0:T(8,128)(2,1)S(1)} %fusion.13), channel_id=1, source_target_pairs={{0,4},{1,5},{2,6},{3,7},{4,0},{5,1},{6,2},{7,3},{8,12},{9,13},{10,... | collective-permute-start | bytes 393224 | tf_op jit(solution)/shard_map/ppermute | solution.py:23
  90.9 5.0 %collective-permute-start.40 = (bf16[16,4096]{1,0:T(8,128)(2,1)S(1)}, bf16[16,4096]{1,0:T(8,128)(2,1)S(1)}, u32[]{:S(2)}, u32[]{:S(2)}) collective-permute-start(bf16[16,4096]{1,0:T(8,128)(2,1)S(1)} %fusion.2.rest_0_), channel_id=1, source_target_pairs={{0,2},{1,3},{2,0},{3,1},{4,6},{5,7},{6,4},{7,5},{8,10},{9,11},{10,... | collective-permute-start | bytes 393224 | tf_op jit(solution)/shard_map/ppermute | solution.py:23
  91.4 8.3 %collective-permute-start.39 = (bf16[16,4096]{1,0:T(8,128)(2,1)S(1)}, bf16[16,4096]{1,0:T(8,128)(2,1)S(1)}, u32[]{:S(2)}, u32[]{:S(2)}) collective-permute-start(bf16[16,4096]{1,0:T(8,128)(2,1)S(1)} %fusion.2.rest_0_), channel_id=1, source_target_pairs={{0,12},{1,13},{2,14},{3,15},{4,8},{5,9},{6,10},{7,11},{8,4},{9,5},... | collective-permute-start | bytes 393224 | tf_op jit(solution)/shard_map/ppermute | solution.py:23
  93.4 6.3 %collective-permute-start.44 = (bf16[16,4096]{1,0:T(8,128)(2,1)S(1)}, bf16[16,4096]{1,0:T(8,128)(2,1)S(1)}, u32[]{:S(2)}, u32[]{:S(2)}) collective-permute-start(bf16[16,4096]{1,0:T(8,128)(2,1)S(1)} %fusion.2.rest_0_), channel_id=1, source_target_pairs={{0,1},{1,0},{2,3},{3,2},{4,5},{5,4},{6,7},{7,6},{8,9},{9,8},{10,11... | collective-permute-start | bytes 393224 | tf_op jit(solution)/shard_map/ppermute | solution.py:23
  93.4 10.4 %collective-permute-start.38 = (bf16[16,4096]{1,0:T(8,128)(2,1)S(1)}, bf16[16,4096]{1,0:T(8,128)(2,1)S(1)}, u32[]{:S(2)}, u32[]{:S(2)}) collective-permute-start(bf16[16,4096]{1,0:T(8,128)(2,1)S(1)} %fusion.2.rest_0_), channel_id=1, source_target_pairs={{0,8},{1,9},{2,10},{3,11},{4,12},{5,13},{6,14},{7,15},{8,0},{9,1},... | collective-permute-start | bytes 393224 | tf_op jit(solution)/shard_map/ppermute | solution.py:23
  93.4 11.9 %collective-permute-start.37 = (bf16[16,4096]{1,0:T(8,128)(2,1)S(1)}, bf16[16,4096]{1,0:T(8,128)(2,1)S(1)}, u32[]{:S(2)}, u32[]{:S(2)}) collective-permute-start(bf16[16,4096]{1,0:T(8,128)(2,1)S(1)} %fusion.2.rest_0_), channel_id=1, source_target_pairs={{0,4},{1,5},{2,6},{3,7},{4,0},{5,1},{6,2},{7,3},{8,12},{9,13},{10,... | collective-permute-start | bytes 393224 | tf_op jit(solution)/shard_map/ppermute | solution.py:23
  95.9 10.0 %collective-permute-start.48 = (bf16[16,4096]{1,0:T(8,128)(2,1)S(1)}, bf16[16,4096]{1,0:T(8,128)(2,1)S(1)}, u32[]{:S(2)}, u32[]{:S(2)}) collective-permute-start(bf16[16,4096]{1,0:T(8,128)(2,1)S(1)} %collective-permute-done.40.rest_4_), channel_id=1, source_target_pairs={{0,1},{1,0},{2,3},{3,2},{4,5},{5,4},{6,7},{7,6},{8,9},{9,8},{10,11... | collective-permute-start | bytes 393224 | tf_op jit(solution)/shard_map/ppermute | solution.py:23
  99.7 6.2 %collective-permute-start.47 = (bf16[16,4096]{1,0:T(8,128)(2,1)S(1)}, bf16[16,4096]{1,0:T(8,128)(2,1)S(1)}, u32[]{:S(2)}, u32[]{:S(2)}) collective-permute-start(bf16[16,4096]{1,0:T(8,128)(2,1)S(1)} %collective-permute-done.39.rest_3_), channel_id=1, source_target_pairs={{0,1},{1,0},{2,3},{3,2},{4,5},{5,4},{6,7},{7,6},{8,9},{9,8},{10,11... | collective-permute-start | bytes 393224 | tf_op jit(solution)/shard_map/ppermute | solution.py:23
  99.7 6.7 %collective-permute-start.43 = (bf16[16,4096]{1,0:T(8,128)(2,1)S(1)}, bf16[16,4096]{1,0:T(8,128)(2,1)S(1)}, u32[]{:S(2)}, u32[]{:S(2)}) collective-permute-start(bf16[16,4096]{1,0:T(8,128)(2,1)S(1)} %collective-permute-done.39.rest_3_), channel_id=1, source_target_pairs={{0,2},{1,3},{2,0},{3,1},{4,6},{5,7},{6,4},{7,5},{8,10},{9,11},{10,... | collective-permute-start | bytes 393224 | tf_op jit(solution)/shard_map/ppermute | solution.py:23
  103.8 6.4 %collective-permute-start.42 = (bf16[16,4096]{1,0:T(8,128)(2,1)S(1)}, bf16[16,4096]{1,0:T(8,128)(2,1)S(1)}, u32[]{:S(2)}, u32[]{:S(2)}) collective-permute-start(bf16[16,4096]{1,0:T(8,128)(2,1)S(1)} %collective-permute-done.38.rest_2_), channel_id=1, source_target_pairs={{0,2},{1,3},{2,0},{3,1},{4,6},{5,7},{6,4},{7,5},{8,10},{9,11},{10,... | collective-permute-start | bytes 393224 | tf_op jit(solution)/shard_map/ppermute | solution.py:23
  105.4 6.7 %collective-permute-start.41 = (bf16[16,4096]{1,0:T(8,128)(2,1)S(1)}, bf16[16,4096]{1,0:T(8,128)(2,1)S(1)}, u32[]{:S(2)}, u32[]{:S(2)}) collective-permute-start(bf16[16,4096]{1,0:T(8,128)(2,1)S(1)} %collective-permute-done.37.rest_1_), channel_id=1, source_target_pairs={{0,2},{1,3},{2,0},{3,1},{4,6},{5,7},{6,4},{7,5},{8,10},{9,11},{10,... | collective-permute-start | bytes 393224 | tf_op jit(solution)/shard_map/ppermute | solution.py:23
  105.9 6.2 %collective-permute-start.46 = (bf16[16,4096]{1,0:T(8,128)(2,1)S(1)}, bf16[16,4096]{1,0:T(8,128)(2,1)S(1)}, u32[]{:S(2)}, u32[]{:S(2)}) collective-permute-start(bf16[16,4096]{1,0:T(8,128)(2,1)S(1)} %collective-permute-done.38.rest_2_), channel_id=1, source_target_pairs={{0,1},{1,0},{2,3},{3,2},{4,5},{5,4},{6,7},{7,6},{8,9},{9,8},{10,11... | collective-permute-start | bytes 393224 | tf_op jit(solution)/shard_map/ppermute | solution.py:23
  105.9 6.2 %collective-permute-start.45 = (bf16[16,4096]{1,0:T(8,128)(2,1)S(1)}, bf16[16,4096]{1,0:T(8,128)(2,1)S(1)}, u32[]{:S(2)}, u32[]{:S(2)}) collective-permute-start(bf16[16,4096]{1,0:T(8,128)(2,1)S(1)} %collective-permute-done.37.rest_1_), channel_id=1, source_target_pairs={{0,1},{1,0},{2,3},{3,2},{4,5},{5,4},{6,7},{7,6},{8,9},{9,8},{10,11... | collective-permute-start | bytes 393224 | tf_op jit(solution)/shard_map/ppermute | solution.py:23
  106.4 5.7 %collective-permute-start.51 = (bf16[16,4096]{1,0:T(8,128)(2,1)S(1)}, bf16[16,4096]{1,0:T(8,128)(2,1)S(1)}, u32[]{:S(2)}, u32[]{:S(2)}) collective-permute-start(bf16[16,4096]{1,0:T(8,128)(2,1)S(1)} %collective-permute-done.43.rest_7_), channel_id=1, source_target_pairs={{0,1},{1,0},{2,3},{3,2},{4,5},{5,4},{6,7},{7,6},{8,9},{9,8},{10,11... | collective-permute-start | bytes 393224 | tf_op jit(solution)/shard_map/ppermute | solution.py:23
  110.2 1.9 %collective-permute-start.50 = (bf16[16,4096]{1,0:T(8,128)(2,1)S(1)}, bf16[16,4096]{1,0:T(8,128)(2,1)S(1)}, u32[]{:S(2)}, u32[]{:S(2)}) collective-permute-start(bf16[16,4096]{1,0:T(8,128)(2,1)S(1)} %collective-permute-done.42.rest_6_), channel_id=1, source_target_pairs={{0,1},{1,0},{2,3},{3,2},{4,5},{5,4},{6,7},{7,6},{8,9},{9,8},{10,11... | collective-permute-start | bytes 393224 | tf_op jit(solution)/shard_map/ppermute | solution.py:23
  112.1 1.3 collective-permute-start.49
  121.4 1.6 %collective-permute-start.52 = (bf16[2,16,4096]{2,1,0:T(8,128)(2,1)S(1)}, bf16[2,16,4096]{2,1,0:T(8,128)(2,1)S(1)}, u32[]{:S(2)}, u32[]{:S(2)}) collective-permute-start(bf16[2,16,4096]{2,1,0:T(8,128)(2,1)S(1)} %get-tuple-element.46), channel_id=1, source_target_pairs={{0,1},{1,0},{2,3},{3,2},{4,5},{5,4},{6,7},{7,6},{8,9},{9,8},{10,11... | collective-permute-start | bytes 786440 | tf_op jit(solution)/shard_map/ppermute | solution.py:23
  121.6 3.1 %collective-permute-start.55 = (bf16[2,16,4096]{2,1,0:T(8,128)(2,1)S(1)}, bf16[2,16,4096]{2,1,0:T(8,128)(2,1)S(1)}, u32[]{:S(2)}, u32[]{:S(2)}) collective-permute-start(bf16[2,16,4096]{2,1,0:T(8,128)(2,1)S(1)} %get-tuple-element.48), channel_id=1, source_target_pairs={{0,1},{1,0},{2,3},{3,2},{4,5},{5,4},{6,7},{7,6},{8,9},{9,8},{10,11... | collective-permute-start | bytes 786440 | tf_op jit(solution)/shard_map/ppermute | solution.py:23
  121.9 3.4 %collective-permute-start.58 = (bf16[2,16,4096]{2,1,0:T(8,128)(2,1)S(1)}, bf16[2,16,4096]{2,1,0:T(8,128)(2,1)S(1)}, u32[]{:S(2)}, u32[]{:S(2)}) collective-permute-start(bf16[2,16,4096]{2,1,0:T(8,128)(2,1)S(1)} %get-tuple-element.50), channel_id=1, source_target_pairs={{0,1},{1,0},{2,3},{3,2},{4,5},{5,4},{6,7},{7,6},{8,9},{9,8},{10,11... | collective-permute-start | bytes 786440 | tf_op jit(solution)/shard_map/ppermute | solution.py:23
  122.1 4.9 %collective-permute-start.61 = (bf16[2,16,4096]{2,1,0:T(8,128)(2,1)S(1)}, bf16[2,16,4096]{2,1,0:T(8,128)(2,1)S(1)}, u32[]{:S(2)}, u32[]{:S(2)}) collective-permute-start(bf16[2,16,4096]{2,1,0:T(8,128)(2,1)S(1)} %get-tuple-element.52), channel_id=1, source_target_pairs={{0,1},{1,0},{2,3},{3,2},{4,5},{5,4},{6,7},{7,6},{8,9},{9,8},{10,11... | collective-permute-start | bytes 786440 | tf_op jit(solution)/shard_map/ppermute | solution.py:23
  123.1 6.4 %collective-permute-start.53 = (bf16[16,4096]{1,0:T(8,128)(2,1)S(1)}, bf16[16,4096]{1,0:T(8,128)(2,1)S(1)}, u32[]{:S(2)}, u32[]{:S(2)}) collective-permute-start(bf16[16,4096]{1,0:T(8,128)(2,1)S(1)} %slice_bitcast_fusion.14), channel_id=1, source_target_pairs={{0,2},{1,3},{2,0},{3,1},{4,6},{5,7},{6,4},{7,5},{8,10},{9,11},{10,... | collective-permute-start | bytes 393224 | tf_op jit(solution)/shard_map/ppermute | solution.py:23
  124.7 7.6 %collective-permute-start.56 = (bf16[16,4096]{1,0:T(8,128)(2,1)S(1)}, bf16[16,4096]{1,0:T(8,128)(2,1)S(1)}, u32[]{:S(2)}, u32[]{:S(2)}) collective-permute-start(bf16[16,4096]{1,0:T(8,128)(2,1)S(1)} %slice_bitcast_fusion.12), channel_id=1, source_target_pairs={{0,2},{1,3},{2,0},{3,1},{4,6},{5,7},{6,4},{7,5},{8,10},{9,11},{10,... | collective-permute-start | bytes 393224 | tf_op jit(solution)/shard_map/ppermute | solution.py:23
  125.4 9.7 %collective-permute-start.59 = (bf16[16,4096]{1,0:T(8,128)(2,1)S(1)}, bf16[16,4096]{1,0:T(8,128)(2,1)S(1)}, u32[]{:S(2)}, u32[]{:S(2)}) collective-permute-start(bf16[16,4096]{1,0:T(8,128)(2,1)S(1)} %slice_bitcast_fusion.10), channel_id=1, source_target_pairs={{0,2},{1,3},{2,0},{3,1},{4,6},{5,7},{6,4},{7,5},{8,10},{9,11},{10,... | collective-permute-start | bytes 393224 | tf_op jit(solution)/shard_map/ppermute | solution.py:23
  127.0 10.0 %collective-permute-start.62 = (bf16[16,4096]{1,0:T(8,128)(2,1)S(1)}, bf16[16,4096]{1,0:T(8,128)(2,1)S(1)}, u32[]{:S(2)}, u32[]{:S(2)}) collective-permute-start(bf16[16,4096]{1,0:T(8,128)(2,1)S(1)} %slice_bitcast_fusion.8), channel_id=1, source_target_pairs={{0,2},{1,3},{2,0},{3,1},{4,6},{5,7},{6,4},{7,5},{8,10},{9,11},{10,... | collective-permute-start | bytes 393224 | tf_op jit(solution)/shard_map/ppermute | solution.py:23
  129.5 7.6 %collective-permute-start.54 = (bf16[16,4096]{1,0:T(8,128)(2,1)S(1)}, bf16[16,4096]{1,0:T(8,128)(2,1)S(1)}, u32[]{:S(2)}, u32[]{:S(2)}) collective-permute-start(bf16[16,4096]{1,0:T(8,128)(2,1)S(1)} %fusion.11), channel_id=1, source_target_pairs={{0,12},{1,13},{2,14},{3,15},{4,8},{5,9},{6,10},{7,11},{8,4},{9,5},... | collective-permute-start | bytes 393224 | tf_op jit(solution)/shard_map/ppermute | solution.py:23
  132.3 9.9 %collective-permute-start.57 = (bf16[16,4096]{1,0:T(8,128)(2,1)S(1)}, bf16[16,4096]{1,0:T(8,128)(2,1)S(1)}, u32[]{:S(2)}, u32[]{:S(2)}) collective-permute-start(bf16[16,4096]{1,0:T(8,128)(2,1)S(1)} %fusion.10), channel_id=1, source_target_pairs={{0,8},{1,9},{2,10},{3,11},{4,12},{5,13},{6,14},{7,15},{8,0},{9,1},... | collective-permute-start | bytes 393224 | tf_op jit(solution)/shard_map/ppermute | solution.py:23
  135.1 7.3 %collective-permute-start.60 = (bf16[16,4096]{1,0:T(8,128)(2,1)S(1)}, bf16[16,4096]{1,0:T(8,128)(2,1)S(1)}, u32[]{:S(2)}, u32[]{:S(2)}) collective-permute-start(bf16[16,4096]{1,0:T(8,128)(2,1)S(1)} %fusion.9), channel_id=1, source_target_pairs={{0,4},{1,5},{2,6},{3,7},{4,0},{5,1},{6,2},{7,3},{8,12},{9,13},{10,... | collective-permute-start | bytes 393224 | tf_op jit(solution)/shard_map/ppermute | solution.py:23
  (11 other events, 251.6 us)

commit v3 on v2

--- a/solution.py
+++ b/solution.py
@@ -7,6 +7,7 @@
 from jax.experimental.pallas import tpu as pltpu
 from jax.sharding import PartitionSpec as P
 
+
 HEAD_SIZE = 128
 LANES = 128
 NEG = -1e30
@@ -23,20 +24,30 @@
     return lax.ppermute(x, "dev", [(i, i ^ mask) for i in range(devices)])
 
 
-def gather_blocks(x, devices):
+def far_order(devices):
     far = devices // 4
-    z_order = sorted(range(1, far), reverse=True)
-    z_parts = {0: x}
-    for i in z_order:
-        z_parts[i] = swap(x, 4 * i, devices)
-    near = [z_parts[i] for i in range(far)]
-    near = near + [swap(b, 2, devices) for b in near]
-    return near + [swap(b, 1, devices) for b in near]
+    order = [i for i in range(2, far)]
+    return order[:1] + [1] + order[1:] if order else [i for i in range(1, far)]
+
+
+def gather_blocks(x, devices, mine=None, visit=None):
+    far = devices // 4
+    near = [x] + [None] * (far - 1)
+    for i in far_order(devices):
+        near[i] = swap(x, 4 * i, devices)
+    if visit is not None:
+        near[1] = visit(near[1])
+    side = [swap(b, 2, devices) for b in near]
+    near_c = [swap(b, 1, devices) for b in near]
+    side_c = [swap(b, 1, devices) for b in side]
+    if mine is not None:
+        near[0] = mine
+    return near + side + near_c + side_c
 
 
 def scatter_blocks(keep, send, devices):
     pieces = []
-    for i in range(devices // 4 - 1, -1, -1):
+    for i in reversed(range(devices // 4)):
         pair = keep[i] + swap(send[i], 1, devices)
         mine = pair[0] + swap(pair[1], 2, devices)
         pieces.append(swap(mine, 4 * i, devices) if i else mine)
@@ -44,7 +55,7 @@
 
 
 def split_shapes(devices, tail):
-    return [jax.ShapeDtypeStruct((2,) + tail, BF)] * (devices // 2)
+    return [pltpu.VMEM((2,) + tail, BF)] * (devices // 2)
 
 
 def split_refs(refs, devices):
@@ -52,46 +63,89 @@
     return [(refs[c * far + z], y) for c in range(2) for y in range(2) for z in range(far)]
 
 
+def in_hbm(x):
+    return pltpu.with_memory_space_constraint(x, pltpu.HBM)
+
+
+def in_vmem(x):
+    return pltpu.with_memory_space_constraint(x, pltpu.VMEM)
+
+
 def lane_pick(vec, lane_iota, index):
     return jnp.sum(jnp.where(lane_iota == index, vec, 0.0), axis=1, keepdims=True)
 
 
-def payload_kernel(q_ref, fresh_ref, ids_ref, score_ref, owner_ref, out_ref, *, top):
+def payload_kernel(
+    me_ref, q_ref, fresh_ref, ids_ref, score_ref, owner_ref, length_ref,
+    out_ref, mine_ref, meta_ref, turn_scr,
+):
     row_dev, qk = q_ref.shape
     kv = fresh_ref.shape[2]
-    out_ref[:, :qk] = q_ref[...]
-    out_ref[:, qk : qk + kv] = fresh_ref[:, 0, :]
-    out_ref[:, qk + kv : qk + 2 * kv] = fresh_ref[:, 1, :]
+    top = ids_ref.shape[0]
+    turn_scr[...] = jnp.zeros(turn_scr.shape, F32)
+    turn_scr[0:top, 0:row_dev] = ids_ref[...].astype(F32)
+    turn_scr[top : 2 * top, 0:row_dev] = score_ref[...].astype(F32)
     segs = owner_ref.shape[1]
     owner = owner_ref[...]
     first = jnp.broadcast_to(owner[:, 0:1], (row_dev, LANES))
     last = jnp.broadcast_to(owner[:, segs - 1 : segs], (row_dev, LANES))
     lane = lax.broadcasted_iota(jnp.int32, (row_dev, LANES), 1)
-    extra = jnp.zeros((row_dev, LANES), jnp.int32)
-    for k in range(top):
-        extra = jnp.where(lane == k, ids_ref[:, k : k + 1], extra)
-        extra = jnp.where(lane == top + k, score_ref[:, k : k + 1], extra)
+    extra = turn_scr[...].T[0:row_dev, :]
     for k, v in enumerate((first // 16, first % 16, last // 16, last % 16)):
-        extra = jnp.where(lane == 2 * top + k, v, extra)
-    out_ref[:, qk + 2 * kv :] = extra.astype(F32).astype(BF)
+        extra = jnp.where(lane == 2 * top + k, v.astype(F32), extra)
+    extra = extra.astype(BF)
+    for ref in (out_ref, mine_ref):
+        ref[:, :qk] = q_ref[...]
+        ref[:, qk : qk + kv] = fresh_ref[:, 0, :]
+        ref[:, qk + kv : qk + 2 * kv] = fresh_ref[:, 1, :]
+        ref[:, qk + 2 * kv :] = extra
+    meta_ref[0:1, :] = owner
+    meta_ref[1:2, :] = length_ref[...]
+
+
+def stage_kernel(x_ref, *refs):
+    count = (len(refs) - 2) // 2
+    ins, out_ref, outs, sems = refs[:count], refs[count], refs[count + 1 : -1], refs[-1]
+    copies = [
+        pltpu.make_async_copy(a, b, sems.at[i]) for i, (a, b) in enumerate(zip(ins, outs))
+    ]
+    for c in copies:
+        c.start()
+    out_ref[...] = x_ref[...]
+    for c in copies:
+        c.wait()
 
 
 def attend_kernel(
-    me_ref, owner_row_ref, length_ref, k_ref, v_ref, *rest,
+    me_ref, meta_ref, k_ref, v_ref, *rest,
     devices, row_dev, width, q_heads, kv_heads, slots, seg_width,
 ):
     pieces = rest[:devices]
     outs = split_refs(rest[devices : devices + devices // 2], devices)
-    q_scr, o_scr, m_scr, t_scr, l_scr = rest[devices + devices // 2 :]
+    own_ref, q_scr, o_scr, m_scr, t_scr, l_scr = rest[devices + devices // 2 :]
+    kv_mine = (me_ref[0] * (q_heads // devices)) // (q_heads // kv_heads)
+    lo = 0
+    for start, size in (
+        (me_ref[0] * width, width),
+        ((q_heads + kv_mine) * HEAD_SIZE, HEAD_SIZE),
+        ((q_heads + kv_heads + kv_mine) * HEAD_SIZE, HEAD_SIZE),
+        ((q_heads + 2 * kv_heads) * HEAD_SIZE, LANES),
+    ):
+        for p, piece in enumerate(pieces):
+            cut = piece[:, pl.ds(pl.multiple_of(start, LANES), size)]
+            own_ref[p * row_dev : (p + 1) * row_dev, lo : lo + size] = cut
+        lo += size
+    owner_row = meta_ref[0:1, :]
+    length_row = meta_ref[1:2, :]
     me = me_ref[0]
     masks = xor_masks(devices)
     rows = devices * row_dev
-    segs = owner_row_ref.shape[1]
+    segs = meta_ref.shape[1]
     hp = q_heads // devices
     per_kv = q_heads // kv_heads
     qk = q_heads * HEAD_SIZE
     ext = qk + 2 * kv_heads * HEAD_SIZE
-    owner_col = jnp.broadcast_to(owner_row_ref[...].astype(F32), (LANES, segs)).T.astype(jnp.int32)
+    owner_col = jnp.broadcast_to(owner_row.astype(F32), (LANES, segs)).T.astype(jnp.int32)
     hots = []
     per_lane = LANES // row_dev
     lane = lax.broadcasted_iota(jnp.int32, (1, LANES), 1)
@@ -116,7 +170,7 @@
     ones = jnp.ones((wide, HEAD_SIZE), BF)
     of_group = lax.broadcasted_iota(jnp.int32, (segs // group, segs), 1) // group
     g_i = lax.broadcasted_iota(jnp.int32, (segs // group, segs), 0)
-    lens = jnp.where(of_group == g_i, length_ref[...], 0).astype(F32).astype(BF)
+    lens = jnp.where(of_group == g_i, length_row, 0).astype(F32).astype(BF)
     e_i = lax.broadcasted_iota(jnp.int32, (segs, wide), 0) % group
     e_j = lax.broadcasted_iota(jnp.int32, (segs, wide), 1) // seg_width
     spread = jnp.where(e_i == e_j, 1.0, 0.0).astype(BF)
@@ -158,7 +212,7 @@
         vec = pieces[p][0:1, ext : ext + LANES].astype(F32)
         ext_sum = ext_sum + jnp.where((me ^ masks[p]) == me - 1, vec, 0.0)
     prev_last = 16.0 * lane_pick(ext_sum, lane, 18) + lane_pick(ext_sum, lane, 19)
-    owner = owner_row_ref[...]
+    owner = owner_row
     first = jnp.min(owner.astype(F32), axis=1, keepdims=True)
     repeated = jnp.logical_and(first == prev_last, me > 0)
     slot = jnp.where(
@@ -218,19 +272,17 @@
 
 
 def combine_kernel(
-    me_ref, w_ref, *rest, devices, row_dev, width, q_heads, kv_heads, slots,
+    me_ref, w_ref, own_ref, *rest, devices, row_dev, width, q_heads, slots,
 ):
-    pieces = rest[:devices]
     far = devices // 4
-    shares = rest[devices : devices + far]
-    outs = split_refs(rest[devices + far : devices + far + devices // 2], devices)
-    x_scr, l_scr = rest[devices + far + devices // 2 :]
+    shares = rest[:far]
+    outs = split_refs(rest[far : far + devices // 2], devices)
+    x_scr, l_scr = rest[far + devices // 2 :]
     me = me_ref[0]
     masks = xor_masks(devices)
     rows = devices * row_dev
     hp = q_heads // devices
-    qk = q_heads * HEAD_SIZE
-    ext = qk + 2 * kv_heads * HEAD_SIZE
+    ext = width + 2 * HEAD_SIZE
     total = shares[0][...].astype(F32)
     for s in shares[1:]:
         total = total + s[...].astype(F32)
@@ -252,7 +304,7 @@
     first = jnp.full((1, LANES), -1.0, F32)
     before = jnp.full((1, LANES), -2.0, F32)
     for p in range(devices):
-        vec = pieces[p][0:1, ext : ext + LANES].astype(F32)
+        vec = own_ref[p * row_dev : p * row_dev + 1, ext : ext + LANES].astype(F32)
         dev = me ^ masks[p]
         first = jnp.where(
             lane == dev, 16.0 * lane_pick(vec, lane, 16) + lane_pick(vec, lane, 17), first
@@ -274,13 +326,9 @@
     lse_col = jnp.concatenate(
         [l_scr[pl.ds((me ^ masks[p]) * row_dev, row_dev), :] for p in range(devices)], axis=0
     )
-    kv = (me * hp) // (q_heads // kv_heads)
-    q_at = pl.multiple_of(me * width, LANES)
-    k_at = pl.multiple_of(qk + kv * HEAD_SIZE, LANES)
-    v_at = pl.multiple_of(qk + (kv_heads + kv) * HEAD_SIZE, LANES)
-    q = jnp.concatenate([p[:, pl.ds(q_at, width)] for p in pieces], axis=0).astype(F32)
-    key = jnp.concatenate([p[:, pl.ds(k_at, HEAD_SIZE)] for p in pieces], axis=0).astype(F32)
-    val = jnp.concatenate([p[:, pl.ds(v_at, HEAD_SIZE)] for p in pieces], axis=0).astype(F32)
+    q = own_ref[:, :width].astype(F32)
+    key = own_ref[:, width : width + HEAD_SIZE].astype(F32)
+    val = own_ref[:, width + HEAD_SIZE : ext].astype(F32)
     chosen = row_id == again
     heads = []
     for hh in range(hp):
@@ -310,11 +358,14 @@
             out_ref[y, :, cut] = r[p * row_dev : (p + 1) * row_dev]
 
 
-def expert_kernel(me_ref, gate_ref, up_ref, down_ref, *rest, devices, row_dev, top, ext_at):
+def expert_kernel(
+    me_ref, gate_ref, up_ref, down_ref, own_ref, *rest, devices, row_dev, top, ext_at
+):
     pieces = rest[:devices]
-    ext = rest[devices : 2 * devices]
-    outs = split_refs(rest[2 * devices : 2 * devices + devices // 2], devices)
-    x_scr, h_scr = rest[2 * devices + devices // 2 :]
+    outs = split_refs(rest[devices : devices + devices // 2], devices)
+    x_scr, h_scr = rest[devices + devices // 2 :]
+    rows = devices * row_dev
+    me = me_ref[0].astype(F32)
     for p in range(devices):
         x_scr[p * row_dev : (p + 1) * row_dev, :] = pieces[p][...]
     ff = gate_ref.shape[2]
@@ -325,18 +376,14 @@
         a = jnp.dot(x_scr[...], gate_ref[0, :, cut], preferred_element_type=F32)
         b = jnp.dot(x_scr[...], up_ref[0, :, cut], preferred_element_type=F32)
         h_scr[:, cut] = (a / (1.0 + jnp.exp(-a)) * b).astype(BF)
-    me = me_ref[0].astype(F32)
-    lane = lax.broadcasted_iota(jnp.int32, (row_dev, LANES), 1)
-    weights = []
-    for p in range(devices):
-        e = ext[p][:, ext_at : ext_at + LANES].astype(F32)
-        score = jnp.where(jnp.logical_and(lane >= top, lane < 2 * top), jnp.exp(e * 0.25), 0.0)
-        total = jnp.sum(score, axis=1, keepdims=True)
-        weight = jnp.zeros((row_dev, 1), F32)
-        for k in range(top):
-            weight = weight + jnp.where(e[:, k : k + 1] == me, score[:, top + k : top + k + 1], 0.0)
-        weights.append(weight / total)
-    weight = jnp.concatenate(weights, axis=0)
+    e = own_ref[:, ext_at : ext_at + LANES].astype(F32)
+    lane = lax.broadcasted_iota(jnp.int32, (rows, LANES), 1)
+    score = jnp.where(jnp.logical_and(lane >= top, lane < 2 * top), jnp.exp(e * 0.25), 0.0)
+    total = jnp.sum(score, axis=1, keepdims=True)
+    weight = jnp.zeros((rows, 1), F32)
+    for k in range(top):
+        weight = weight + jnp.where(e[:, k : k + 1] == me, score[:, top + k : top + k + 1], 0.0)
+    weight = weight / total
     step = 512
     for c in range(d_model // step):
         cut = slice(c * step, (c + 1) * step)
@@ -366,28 +413,64 @@
     tall = slots + -(-strips // 2) * 16
     smem = pl.BlockSpec(memory_space=pltpu.SMEM)
     vmem = pl.BlockSpec(memory_space=pltpu.VMEM)
+    hbm = pl.BlockSpec(memory_space=pltpu.HBM)
+
+    def budget(mib):
+        return pltpu.CompilerParams(vmem_limit_bytes=mib * 2**20 * max(1, devices // 16))
+
     half = devices // 2
     far = devices // 4
-    owner_row = segment_owner_row.reshape(1, segs)
     ext_at = (q_heads + 2 * kv_heads) * HEAD_SIZE
-    payload = pl.pallas_call(
-        functools.partial(payload_kernel, top=top),
-        out_shape=jax.ShapeDtypeStruct((row_dev, ext_at + LANES), BF),
-        in_specs=[vmem] * 5,
-        out_specs=vmem,
+    load = jax.ShapeDtypeStruct((row_dev, ext_at + LANES), BF)
+    payload, mine, meta = pl.pallas_call(
+        payload_kernel,
+        out_shape=[load, pltpu.VMEM(load.shape, BF), pltpu.VMEM((8, segs), jnp.int32)],
+        in_specs=[smem] + [vmem] * 6,
+        out_specs=[vmem] * 3,
+        scratch_shapes=[pltpu.VMEM((LANES, LANES), F32)],
+        compiler_params=budget(2),
         name="payload",
-    )(queries, fresh_key_value, expert_ids, gate_score, owner_row)
-    pieces = gather_blocks(payload, devices)
-    params = pltpu.CompilerParams(vmem_limit_bytes=24 * 1024 * 1024)
+    )(
+        me,
+        *map(
+            in_hbm,
+            (
+                queries, fresh_key_value, expert_ids.T, gate_score.T,
+                segment_owner_row.reshape(1, segs), segment_length.reshape(1, segs),
+            ),
+        )
+    )
+    staged = []
+
+    def stage(x):
+        arrays = [
+            segment_key_cache.reshape(segs * seg_width, -1),
+            segment_value_cache.reshape(segs * seg_width, -1),
+            out_proj,
+        ]
+        x, *copied = pl.pallas_call(
+            stage_kernel,
+            out_shape=[pltpu.VMEM(a.shape, a.dtype) for a in [x] + arrays],
+            in_specs=[vmem] + [hbm] * len(arrays),
+            out_specs=[vmem] * (1 + len(arrays)),
+            scratch_shapes=[pltpu.SemaphoreType.DMA((len(arrays),))],
+            compiler_params=budget(8),
+            name="stage",
+        )(x, *map(in_hbm, arrays))
+        staged.extend(copied)
+        return x
+
+    pieces = gather_blocks(payload, devices, mine, stage)
     stats = devices * 8
-    table = pl.pallas_call(
+    own_at = width + 2 * HEAD_SIZE
+    *table, own = pl.pallas_call(
         functools.partial(
             attend_kernel, devices=devices, row_dev=row_dev, width=width, q_heads=q_heads,
             kv_heads=kv_heads, slots=slots, seg_width=seg_width,
         ),
-        out_shape=split_shapes(devices, (tall, width)),
-        in_specs=[smem] + [vmem] * (4 + devices),
-        out_specs=[vmem] * half,
+        out_shape=split_shapes(devices, (tall, width)) + [pltpu.VMEM((rows, own_at + LANES), BF)],
+        in_specs=[smem] + [vmem] * (3 + devices),
+        out_specs=[vmem] * (half + 1),
         scratch_shapes=[
             pltpu.VMEM((segs, q_heads * HEAD_SIZE), BF),
             pltpu.VMEM((q_heads, segs, 2 * HEAD_SIZE), BF),
@@ -395,27 +478,26 @@
             pltpu.VMEM((LANES, segs), F32),
             pltpu.VMEM((stats, max(strips * width, -(-slots // LANES) * LANES)), F32),
         ],
-        compiler_params=params,
+        compiler_params=budget(14),
         name="attend",
     )(
-        me, owner_row, segment_length.reshape(1, segs),
-        segment_key_cache.reshape(segs * seg_width, -1),
-        segment_value_cache.reshape(segs * seg_width, -1),
-        *pieces,
+        me, meta,
+        in_vmem(staged[0]), in_vmem(staged[1]),
+        *map(in_vmem, pieces),
     )
     shares = scatter_blocks(table[:far], table[far:], devices)
     part = pl.pallas_call(
         functools.partial(
             combine_kernel, devices=devices, row_dev=row_dev, width=width, q_heads=q_heads,
-            kv_heads=kv_heads, slots=slots,
+            slots=slots,
         ),
         out_shape=split_shapes(devices, (row_dev, d_model)),
-        in_specs=[smem] + [vmem] * (1 + devices + far),
+        in_specs=[smem] + [vmem] * (2 + far),
         out_specs=[vmem] * half,
         scratch_shapes=[pltpu.VMEM((tall, width), F32), pltpu.VMEM((rows, LANES), F32)],
-        compiler_params=params,
+        compiler_params=budget(8),
         name="combine",
-    )(me, out_proj, *pieces, *shares)
+    )(me, in_vmem(staged[2]), own, *map(in_vmem, shares))
     projected = sum(p.astype(F32) for p in scatter_blocks(part[:far], part[far:], devices))
     mixed = (hidden_in.astype(F32) + projected).astype(BF).astype(F32)
     normed = (
@@ -427,15 +509,18 @@
     ff = w_gate.shape[2]
     moe = pl.pallas_call(
         functools.partial(
-            expert_kernel, devices=devices, row_dev=row_dev, top=top, ext_at=ext_at
+            expert_kernel, devices=devices, row_dev=row_dev, top=top, ext_at=own_at
         ),
         out_shape=split_shapes(devices, (row_dev, d_model)),
-        in_specs=[smem] + [vmem] * (3 + 2 * devices),
+        in_specs=[smem] + [vmem] * (4 + devices),
         out_specs=[vmem] * half,
-        scratch_shapes=[pltpu.VMEM((rows, d_model), BF), pltpu.VMEM((rows, ff), BF)],
-        compiler_params=pltpu.CompilerParams(vmem_limit_bytes=34 * 1024 * 1024),
+        scratch_shapes=[
+            pltpu.VMEM((rows, d_model), BF),
+            pltpu.VMEM((rows, ff), BF),
+        ],
+        compiler_params=budget(14),
         name="experts",
-    )(me, w_gate, w_up, w_down, *tokens, *pieces)
+    )(me, w_gate, w_up, w_down, own, *map(in_vmem, tokens))
     summed = sum(p.astype(F32) for p in scatter_blocks(moe[:far], moe[far:], devices))
     return (mixed + summed).astype(BF)
 
@@ -447,6 +532,5 @@
         P(both, None, None), P(both), P(both), P(both, None), P(both, None),
         P("dev", None), P(), P("dev", None, None), P("dev", None, None), P("dev", None, None),
     )
-    return jax.shard_map(
-        on_device, mesh=mesh, in_specs=placed, out_specs=P(both, None), check_vma=False
-    )
+
+    return jax.shard_map(on_device, mesh=mesh, in_specs=placed, out_specs=P(both, None), check_vma=False)

time: 144 us -> 134 us (0.931)
  local copies, waits for them, and re-layouts: 7.54 us -> 0.16 us
  waiting for transfers between devices: 67 us -> 62.9 us
  starting transfers between devices: 49.3 us -> 52.9 us
    unnamed x26 -> x12, local copies, waits for them, and re-layouts: 7.41 us -> 0.03 us
    ppermute x63, waiting for transfers between devices: 67 us -> 62.9 us  [swap(): return lax.ppermute(x, 'dev', [(i, i ^ mask) for i in range(devices)])]
    ppermute x63, starting transfers between devices: 49.3 us -> 52.9 us  [swap(): return lax.ppermute(x, 'dev', [(i, i ^ mask) for i in range(devices)])]
    pallas_call x1, Pallas kernels: 7.92 us -> 5.17 us  [on_device(): pl.pallas_call(functools.partial(expert_kernel, devices=devices, row_dev=...]
    pallas_call x1 -> x2, Pallas kernels: 1.71 us -> 3.3 us  [the longest x1 2.26 us: stage(): pl.pallas_call(stage_kernel, out_shape=[pltpu.VMEM(a.shape, a.dtype) for...]
  transfers between devices with their start and end apart: 63 -> 63, of which waited for: 29 -> 31; matrix products, arithmetic and copies ran while one was open for 1% -> 1% of each run, Pallas kernels for 0% -> 2%
where the time goes in v3:
time: 134 us
  waiting for transfers between devices  62.9 us (47%)
  starting transfers between devices  52.9 us (39%)
  Pallas kernels  15.6 us (12%)
  other arithmetic  2.08 us (2%)
    ppermute x63, waiting for transfers between devices, swap(): return lax.ppermute(x, 'dev', [(i, i ^ mask) for i in range(devices)])  62.9 us
    ppermute x63, starting transfers between devices, swap(): return lax.ppermute(x, 'dev', [(i, i ^ mask) for i in range(devices)])  52.9 us
    pallas_call x1, Pallas kernels, on_device(): pl.pallas_call(functools.partial(attend_kernel, devices=devices, row_dev=...  5.36 us
    pallas_call x1, Pallas kernels, on_device(): pl.pallas_call(functools.partial(expert_kernel, devices=devices, row_dev=...  5.17 us
  transfers between devices with their start and end apart: 63, of which 31 were waited for; matrix products, arithmetic and copies ran while one was open for 1% of the time, Pallas kernels for 2%

profile of v3, /device:TPU:0, one launch (start us, length us, event | category | flops | bytes accessed | tf_op | source)
XLA Modules:
  0.0 134.0 jit_solution(10253039170115332703)
XLA Ops:
  0.0 1.0 payload.1
  1.0 3.1 %collective-permute-start = (bf16[16,4736]{1,0:T(8,128)(2,1)S(1)}, bf16[16,4736]{1,0:T(8,128)(2,1)S(1)}, u32[]{:S(2)}, u32[]{:S(2)}) collective-permute-start(bf16[16,4736]{1,0:T(8,128)(2,1)S(1)} %get-tuple-element.37), channel_id=1, source_target_pairs={{0,4},{1,5},{2,6},{3,7},{4,0},{5,1},{6,2},{7,3},{8,12},{9,13},{10,... | collective-permute-start | bytes 454664 | tf_op jit(solution)/shard_map/ppermute | solution.py:24
  4.2 2.6 %collective-permute-start.1 = (bf16[16,4736]{1,0:T(8,128)(2,1)S(1)}, bf16[16,4736]{1,0:T(8,128)(2,1)S(1)}, u32[]{:S(2)}, u32[]{:S(2)}) collective-permute-start(bf16[16,4736]{1,0:T(8,128)(2,1)S(1)} %get-tuple-element.37), channel_id=1, source_target_pairs={{0,8},{1,9},{2,10},{3,11},{4,12},{5,13},{6,14},{7,15},{8,0},{9,1},... | collective-permute-start | bytes 454664 | tf_op jit(solution)/shard_map/ppermute | solution.py:24
  6.8 1.7 %collective-permute-start.3 = (bf16[16,4736]{1,0:T(8,128)(2,1)S(1)}, bf16[16,4736]{1,0:T(8,128)(2,1)S(1)}, u32[]{:S(2)}, u32[]{:S(2)}) collective-permute-start(bf16[16,4736]{1,0:T(8,128)(2,1)S(1)} %get-tuple-element.37), channel_id=1, source_target_pairs={{0,2},{1,3},{2,0},{3,1},{4,6},{5,7},{6,4},{7,5},{8,10},{9,11},{10,... | collective-permute-start | bytes 454664 | tf_op jit(solution)/shard_map/ppermute | solution.py:24
  8.5 1.8 %collective-permute-done.x_ref = bf16[16,4736]{1,0:T(8,128)(2,1)S(1)} collective-permute-done((bf16[16,4736]{1,0:T(8,128)(2,1)S(1)}, bf16[16,4736]{1,0:T(8,128)(2,1)S(1)}, u32[]{:S(2)}, u32[]{:S(2)}) %collective-permute-start) | collective-permute-done | bytes 151584 | tf_op jit(solution)/shard_map/ppermute | solution.py:24
  10.3 2.3 %stage.1 = (bf16[16,4736]{1,0:T(8,128)(2,1)S(1)}, bf16[2048,256]{1,0:T(8,128)(2,1)S(1)}, bf16[2048,256]{1,0:T(8,128)(2,1)S(1)}, bf16[256,4096]{1,0:T(8,128)(2,1)S(1)}) custom-call(bf16[16,4736]{1,0:T(8,128)(2,1)S(1)} %collective-permute-done.x_ref, bf16[2048,256]{1,0:T(8,128)(2,1)} %bitcast.86, bf16[2048,256]{1,0:T(8,128)(2,1)} %bitcast.87, ...), custom_call_target="tpu_custom_call" | custom-call | tf_op jit(solution)/shard_map/stage/pallas_call | solution.py:451
  12.5 1.8 %collective-permute-start.4 = (bf16[16,4736]{1,0:T(8,128)(2,1)S(1)}, bf16[16,4736]{1,0:T(8,128)(2,1)S(1)}, u32[]{:S(2)}, u32[]{:S(2)}) collective-permute-start(bf16[16,4736]{1,0:T(8,128)(2,1)S(1)} %get-tuple-element.43.rest_1_), channel_id=1, source_target_pairs={{0,2},{1,3},{2,0},{3,1},{4,6},{5,7},{6,4},{7,5},{8,10},{9,11},{10,... | collective-permute-start | bytes 454664 | tf_op jit(solution)/shard_map/ppermute | solution.py:24
  14.3 4.0 %collective-permute-done.1.rest_2_ = bf16[16,4736]{1,0:T(8,128)(2,1)S(1)} collective-permute-done((bf16[16,4736]{1,0:T(8,128)(2,1)S(1)}, bf16[16,4736]{1,0:T(8,128)(2,1)S(1)}, u32[]{:S(2)}, u32[]{:S(2)}) %collective-permute-start.1) | collective-permute-done | bytes 151584 | tf_op jit(solution)/shard_map/ppermute | solution.py:24
  18.4 1.5 %collective-permute-start.5 = (bf16[16,4736]{1,0:T(8,128)(2,1)S(1)}, bf16[16,4736]{1,0:T(8,128)(2,1)S(1)}, u32[]{:S(2)}, u32[]{:S(2)}) collective-permute-start(bf16[16,4736]{1,0:T(8,128)(2,1)S(1)} %collective-permute-done.1.rest_2_), channel_id=1, source_target_pairs={{0,2},{1,3},{2,0},{3,1},{4,6},{5,7},{6,4},{7,5},{8,10},{9,11},{10,... | collective-permute-start | bytes 454664 | tf_op jit(solution)/shard_map/ppermute | solution.py:24
  19.9 0.5 collective-permute-start.6
  21.0 2.6 %collective-permute-done.5.rest_6_ = bf16[16,4736]{1,0:T(8,128)(2,1)S(1)} collective-permute-done((bf16[16,4736]{1,0:T(8,128)(2,1)S(1)}, bf16[16,4736]{1,0:T(8,128)(2,1)S(1)}, u32[]{:S(2)}, u32[]{:S(2)}) %collective-permute-start.5) | collective-permute-done | bytes 151584 | tf_op jit(solution)/shard_map/ppermute | solution.py:24
  23.6 1.6 %collective-permute-done.6.rest_7_ = bf16[16,4736]{1,0:T(8,128)(2,1)S(1)} collective-permute-done((bf16[16,4736]{1,0:T(8,128)(2,1)S(1)}, bf16[16,4736]{1,0:T(8,128)(2,1)S(1)}, u32[]{:S(2)}, u32[]{:S(2)}) %collective-permute-start.6) | collective-permute-done | bytes 151584 | tf_op jit(solution)/shard_map/ppermute | solution.py:24
  25.2 0.5 collective-permute-start.13
  25.8 0.8 collective-permute-done.12.rest_13_
  27.1 5.4 %attend.1 = (bf16[2,288,256]{2,1,0:T(8,128)(2,1)S(1)}, bf16[2,288,256]{2,1,0:T(8,128)(2,1)S(1)}, bf16[2,288,256]{2,1,0:T(8,128)(2,1)S(1)}, bf16[2,288,256]{2,1,0...) custom-call(s32[1]{0:T(128)} %bitcast.me_ref, ...), custom_call_target="tpu_custom_call" | custom-call | tf_op jit(solution)/shard_map/attend/pallas_call | solution.py:466
  33.5 0.6 collective-permute-done.15
  34.2 1.6 %collective-permute-start.16 = (bf16[288,256]{1,0:T(8,128)(2,1)S(1)}, bf16[288,256]{1,0:T(8,128)(2,1)S(1)}, u32[]{:S(2)}, u32[]{:S(2)}) collective-permute-start(bf16[288,256]{1,0:T(8,128)(2,1)S(1)} %slice_bitcast_fusion.6), channel_id=1, source_target_pairs={{0,2},{1,3},{2,0},{3,1},{4,6},{5,7},{6,4},{7,5},{8,10},{9,11},{10,... | collective-permute-start | bytes 442376 | tf_op jit(solution)/shard_map/ppermute | solution.py:24
  35.9 0.6 collective-permute-start.19
  36.6 1.6 %collective-permute-start.22 = (bf16[288,256]{1,0:T(8,128)(2,1)S(1)}, bf16[288,256]{1,0:T(8,128)(2,1)S(1)}, u32[]{:S(2)}, u32[]{:S(2)}) collective-permute-start(bf16[288,256]{1,0:T(8,128)(2,1)S(1)} %slice_bitcast_fusion.2), channel_id=1, source_target_pairs={{0,2},{1,3},{2,0},{3,1},{4,6},{5,7},{6,4},{7,5},{8,10},{9,11},{10,... | collective-permute-start | bytes 442376 | tf_op jit(solution)/shard_map/ppermute | solution.py:24
  38.3 0.6 collective-permute-start.25
  38.8 2.1 %collective-permute-done.16 = bf16[288,256]{1,0:T(8,128)(2,1)S(1)} collective-permute-done((bf16[288,256]{1,0:T(8,128)(2,1)S(1)}, bf16[288,256]{1,0:T(8,128)(2,1)S(1)}, u32[]{:S(2)}, u32[]{:S(2)}) %collective-permute-start.16) | collective-permute-done | bytes 147488 | tf_op jit(solution)/shard_map/ppermute | solution.py:24
  41.0 2.8 %collective-permute-start.17 = (bf16[288,256]{1,0:T(8,128)(2,1)S(1)}, bf16[288,256]{1,0:T(8,128)(2,1)S(1)}, u32[]{:S(2)}, u32[]{:S(2)}) collective-permute-start(bf16[288,256]{1,0:T(8,128)(2,1)S(1)} %fusion.7), channel_id=1, source_target_pairs={{0,12},{1,13},{2,14},{3,15},{4,8},{5,9},{6,10},{7,11},{8,4},{9,5},... | collective-permute-start | bytes 442376 | tf_op jit(solution)/shard_map/ppermute | solution.py:24
  44.2 1.9 %collective-permute-start.20 = (bf16[288,256]{1,0:T(8,128)(2,1)S(1)}, bf16[288,256]{1,0:T(8,128)(2,1)S(1)}, u32[]{:S(2)}, u32[]{:S(2)}) collective-permute-start(bf16[288,256]{1,0:T(8,128)(2,1)S(1)} %fusion.6), channel_id=1, source_target_pairs={{0,8},{1,9},{2,10},{3,11},{4,12},{5,13},{6,14},{7,15},{8,0},{9,1},... | collective-permute-start | bytes 442376 | tf_op jit(solution)/shard_map/ppermute | solution.py:24
  46.0 1.2 collective-permute-done.22
  47.3 1.1 collective-permute-start.23
  48.5 1.2 collective-permute-done.25
  49.7 5.7 %collective-permute-done.20.rest_1_ = bf16[288,256]{1,0:T(8,128)(2,1)S(1)} collective-permute-done((bf16[288,256]{1,0:T(8,128)(2,1)S(1)}, bf16[288,256]{1,0:T(8,128)(2,1)S(1)}, u32[]{:S(2)}, u32[]{:S(2)}) %collective-permute-start.20) | collective-permute-done | bytes 147488 | tf_op jit(solution)/shard_map/ppermute | solution.py:24
  55.4 1.8 %combine.1 = (bf16[2,16,4096]{2,1,0:T(8,128)(2,1)S(1)}, bf16[2,16,4096]{2,1,0:T(8,128)(2,1)S(1)}, bf16[2,16,4096]{2,1,0:T(8,128)(2,1)S(1)}, bf16[2,16,4096]{2,1,...) custom-call(s32[1]{0:T(128)} %bitcast.me_ref, ...), custom_call_target="tpu_custom_call" | custom-call | tf_op jit(solution)/shard_map/combine/pallas_call | solution.py:489
  58.3 0.5 collective-permute-done.35
  58.9 1.6 %collective-permute-start.36 = (bf16[16,4096]{1,0:T(8,128)(2,1)S(1)}, bf16[16,4096]{1,0:T(8,128)(2,1)S(1)}, u32[]{:S(2)}, u32[]{:S(2)}) collective-permute-start(bf16[16,4096]{1,0:T(8,128)(2,1)S(1)} %slice_bitcast_fusion.16), channel_id=1, source_target_pairs={{0,2},{1,3},{2,0},{3,1},{4,6},{5,7},{6,4},{7,5},{8,10},{9,11},{10,... | collective-permute-start | bytes 393224 | tf_op jit(solution)/shard_map/ppermute | solution.py:24
  60.5 0.6 collective-permute-start.33
  61.2 1.6 %collective-permute-start.30 = (bf16[16,4096]{1,0:T(8,128)(2,1)S(1)}, bf16[16,4096]{1,0:T(8,128)(2,1)S(1)}, u32[]{:S(2)}, u32[]{:S(2)}) collective-permute-start(bf16[16,4096]{1,0:T(8,128)(2,1)S(1)} %slice_bitcast_fusion.20), channel_id=1, source_target_pairs={{0,2},{1,3},{2,0},{3,1},{4,6},{5,7},{6,4},{7,5},{8,10},{9,11},{10,... | collective-permute-start | bytes 393224 | tf_op jit(solution)/shard_map/ppermute | solution.py:24
  62.9 0.6 collective-permute-start.27
  63.4 4.7 %collective-permute-done.33 = bf16[16,4096]{1,0:T(8,128)(2,1)S(1)} collective-permute-done((bf16[16,4096]{1,0:T(8,128)(2,1)S(1)}, bf16[16,4096]{1,0:T(8,128)(2,1)S(1)}, u32[]{:S(2)}, u32[]{:S(2)}) %collective-permute-start.33) | collective-permute-done | bytes 131104 | tf_op jit(solution)/shard_map/ppermute | solution.py:24
  68.2 2.7 %collective-permute-done.30 = bf16[16,4096]{1,0:T(8,128)(2,1)S(1)} collective-permute-done((bf16[16,4096]{1,0:T(8,128)(2,1)S(1)}, bf16[16,4096]{1,0:T(8,128)(2,1)S(1)}, u32[]{:S(2)}, u32[]{:S(2)}) %collective-permute-start.30) | collective-permute-done | bytes 131104 | tf_op jit(solution)/shard_map/ppermute | solution.py:24
  70.9 0.9 collective-permute-start.31
  71.8 1.1 collective-permute-done.27
  72.9 2.8 %collective-permute-start.28 = (bf16[16,4096]{1,0:T(8,128)(2,1)S(1)}, bf16[16,4096]{1,0:T(8,128)(2,1)S(1)}, u32[]{:S(2)}, u32[]{:S(2)}) collective-permute-start(bf16[16,4096]{1,0:T(8,128)(2,1)S(1)} %fusion.15), channel_id=1, source_target_pairs={{0,12},{1,13},{2,14},{3,15},{4,8},{5,9},{6,10},{7,11},{8,4},{9,5},... | collective-permute-start | bytes 393224 | tf_op jit(solution)/shard_map/ppermute | solution.py:24
  75.7 6.7 %collective-permute-done.31 = bf16[16,4096]{1,0:T(8,128)(2,1)S(1)} collective-permute-done((bf16[16,4096]{1,0:T(8,128)(2,1)S(1)}, bf16[16,4096]{1,0:T(8,128)(2,1)S(1)}, u32[]{:S(2)}, u32[]{:S(2)}) %collective-permute-start.31) | collective-permute-done | bytes 131104 | tf_op jit(solution)/shard_map/ppermute | solution.py:24
  82.7 2.5 %collective-permute-start.37 = (bf16[16,4096]{1,0:T(8,128)(2,1)S(1)}, bf16[16,4096]{1,0:T(8,128)(2,1)S(1)}, u32[]{:S(2)}, u32[]{:S(2)}) collective-permute-start(bf16[16,4096]{1,0:T(8,128)(2,1)S(1)} %fusion.2.rest_0_), channel_id=1, source_target_pairs={{0,4},{1,5},{2,6},{3,7},{4,0},{5,1},{6,2},{7,3},{8,12},{9,13},{10,... | collective-permute-start | bytes 393224 | tf_op jit(solution)/shard_map/ppermute | solution.py:24
  85.2 0.6 collective-permute-start.38
  85.8 1.8 %collective-permute-start.39 = (bf16[16,4096]{1,0:T(8,128)(2,1)S(1)}, bf16[16,4096]{1,0:T(8,128)(2,1)S(1)}, u32[]{:S(2)}, u32[]{:S(2)}) collective-permute-start(bf16[16,4096]{1,0:T(8,128)(2,1)S(1)} %fusion.2.rest_0_), channel_id=1, source_target_pairs={{0,12},{1,13},{2,14},{3,15},{4,8},{5,9},{6,10},{7,11},{8,4},{9,5},... | collective-permute-start | bytes 393224 | tf_op jit(solution)/shard_map/ppermute | solution.py:24
  87.6 1.5 %collective-permute-start.40 = (bf16[16,4096]{1,0:T(8,128)(2,1)S(1)}, bf16[16,4096]{1,0:T(8,128)(2,1)S(1)}, u32[]{:S(2)}, u32[]{:S(2)}) collective-permute-start(bf16[16,4096]{1,0:T(8,128)(2,1)S(1)} %fusion.2.rest_0_), channel_id=1, source_target_pairs={{0,2},{1,3},{2,0},{3,1},{4,6},{5,7},{6,4},{7,5},{8,10},{9,11},{10,... | collective-permute-start | bytes 393224 | tf_op jit(solution)/shard_map/ppermute | solution.py:24
  89.2 1.5 %collective-permute-start.41 = (bf16[16,4096]{1,0:T(8,128)(2,1)S(1)}, bf16[16,4096]{1,0:T(8,128)(2,1)S(1)}, u32[]{:S(2)}, u32[]{:S(2)}) collective-permute-start(bf16[16,4096]{1,0:T(8,128)(2,1)S(1)} %collective-permute-done.37.rest_1_), channel_id=1, source_target_pairs={{0,2},{1,3},{2,0},{3,1},{4,6},{5,7},{6,4},{7,5},{8,10},{9,11},{10,... | collective-permute-start | bytes 393224 | tf_op jit(solution)/shard_map/ppermute | solution.py:24
  90.7 6.5 %collective-permute-done.38.rest_2_ = bf16[16,4096]{1,0:T(8,128)(2,1)S(1)} collective-permute-done((bf16[16,4096]{1,0:T(8,128)(2,1)S(1)}, bf16[16,4096]{1,0:T(8,128)(2,1)S(1)}, u32[]{:S(2)}, u32[]{:S(2)}) %collective-permute-start.38) | collective-permute-done | bytes 131104 | tf_op jit(solution)/shard_map/ppermute | solution.py:24
  97.2 1.6 %collective-permute-start.42 = (bf16[16,4096]{1,0:T(8,128)(2,1)S(1)}, bf16[16,4096]{1,0:T(8,128)(2,1)S(1)}, u32[]{:S(2)}, u32[]{:S(2)}) collective-permute-start(bf16[16,4096]{1,0:T(8,128)(2,1)S(1)} %collective-permute-done.38.rest_2_), channel_id=1, source_target_pairs={{0,2},{1,3},{2,0},{3,1},{4,6},{5,7},{6,4},{7,5},{8,10},{9,11},{10,... | collective-permute-start | bytes 393224 | tf_op jit(solution)/shard_map/ppermute | solution.py:24
  99.9 2.3 %collective-permute-done.42.rest_6_ = bf16[16,4096]{1,0:T(8,128)(2,1)S(1)} collective-permute-done((bf16[16,4096]{1,0:T(8,128)(2,1)S(1)}, bf16[16,4096]{1,0:T(8,128)(2,1)S(1)}, u32[]{:S(2)}, u32[]{:S(2)}) %collective-permute-start.42) | collective-permute-done | bytes 131104 | tf_op jit(solution)/shard_map/ppermute | solution.py:24
  102.2 1.6 %collective-permute-done.43.rest_7_ = bf16[16,4096]{1,0:T(8,128)(2,1)S(1)} collective-permute-done((bf16[16,4096]{1,0:T(8,128)(2,1)S(1)}, bf16[16,4096]{1,0:T(8,128)(2,1)S(1)}, u32[]{:S(2)}, u32[]{:S(2)}) %collective-permute-start.43) | collective-permute-done | bytes 131104 | tf_op jit(solution)/shard_map/ppermute | solution.py:24
  103.8 0.5 collective-permute-start.50
  104.4 0.8 collective-permute-done.49.rest_13_
  105.7 5.2 %experts.1 = (bf16[2,16,4096]{2,1,0:T(8,128)(2,1)S(1)}, bf16[2,16,4096]{2,1,0:T(8,128)(2,1)S(1)}, bf16[2,16,4096]{2,1,0:T(8,128)(2,1)S(1)}, bf16[2,16,4096]{2,1,...) custom-call(s32[1]{0:T(128)} %bitcast.me_ref, ...), custom_call_target="tpu_custom_call" | custom-call | tf_op jit(solution)/shard_map/experts/pallas_call | solution.py:510
  111.9 0.5 collective-permute-done.58
  112.5 1.5 %collective-permute-start.59 = (bf16[16,4096]{1,0:T(8,128)(2,1)S(1)}, bf16[16,4096]{1,0:T(8,128)(2,1)S(1)}, u32[]{:S(2)}, u32[]{:S(2)}) collective-permute-start(bf16[16,4096]{1,0:T(8,128)(2,1)S(1)} %slice_bitcast_fusion.10), channel_id=1, source_target_pairs={{0,2},{1,3},{2,0},{3,1},{4,6},{5,7},{6,4},{7,5},{8,10},{9,11},{10,... | collective-permute-start | bytes 393224 | tf_op jit(solution)/shard_map/ppermute | solution.py:24
  114.1 0.7 collective-permute-start.56
  114.9 1.5 %collective-permute-start.53 = (bf16[16,4096]{1,0:T(8,128)(2,1)S(1)}, bf16[16,4096]{1,0:T(8,128)(2,1)S(1)}, u32[]{:S(2)}, u32[]{:S(2)}) collective-permute-start(bf16[16,4096]{1,0:T(8,128)(2,1)S(1)} %slice_bitcast_fusion.14), channel_id=1, source_target_pairs={{0,2},{1,3},{2,0},{3,1},{4,6},{5,7},{6,4},{7,5},{8,10},{9,11},{10,... | collective-permute-start | bytes 393224 | tf_op jit(solution)/shard_map/ppermute | solution.py:24
  116.4 0.7 collective-permute-start.62
  117.1 1.9 %collective-permute-done.59 = bf16[16,4096]{1,0:T(8,128)(2,1)S(1)} collective-permute-done((bf16[16,4096]{1,0:T(8,128)(2,1)S(1)}, bf16[16,4096]{1,0:T(8,128)(2,1)S(1)}, u32[]{:S(2)}, u32[]{:S(2)}) %collective-permute-start.59) | collective-permute-done | bytes 131104 | tf_op jit(solution)/shard_map/ppermute | solution.py:24
  119.0 0.6 collective-permute-start.60
  119.5 2.2 %collective-permute-done.56 = bf16[16,4096]{1,0:T(8,128)(2,1)S(1)} collective-permute-done((bf16[16,4096]{1,0:T(8,128)(2,1)S(1)}, bf16[16,4096]{1,0:T(8,128)(2,1)S(1)}, u32[]{:S(2)}, u32[]{:S(2)}) %collective-permute-start.56) | collective-permute-done | bytes 131104 | tf_op jit(solution)/shard_map/ppermute | solution.py:24
  121.8 1.2 collective-permute-start.57
  123.0 1.6 %collective-permute-done.53 = bf16[16,4096]{1,0:T(8,128)(2,1)S(1)} collective-permute-done((bf16[16,4096]{1,0:T(8,128)(2,1)S(1)}, bf16[16,4096]{1,0:T(8,128)(2,1)S(1)}, u32[]{:S(2)}, u32[]{:S(2)}) %collective-permute-start.53) | collective-permute-done | bytes 131104 | tf_op jit(solution)/shard_map/ppermute | solution.py:24
  124.6 1.9 %collective-permute-start.54 = (bf16[16,4096]{1,0:T(8,128)(2,1)S(1)}, bf16[16,4096]{1,0:T(8,128)(2,1)S(1)}, u32[]{:S(2)}, u32[]{:S(2)}) collective-permute-start(bf16[16,4096]{1,0:T(8,128)(2,1)S(1)} %fusion.11), channel_id=1, source_target_pairs={{0,12},{1,13},{2,14},{3,15},{4,8},{5,9},{6,10},{7,11},{8,4},{9,5},... | collective-permute-start | bytes 393224 | tf_op jit(solution)/shard_map/ppermute | solution.py:24
  126.6 6.7 %collective-permute-done.57 = bf16[16,4096]{1,0:T(8,128)(2,1)S(1)} collective-permute-done((bf16[16,4096]{1,0:T(8,128)(2,1)S(1)}, bf16[16,4096]{1,0:T(8,128)(2,1)S(1)}, u32[]{:S(2)}, u32[]{:S(2)}) %collective-permute-start.57) | collective-permute-done | bytes 131104 | tf_op jit(solution)/shard_map/ppermute | solution.py:24
  133.3 0.8 fusion.3
  (119 shorter events, 8.3 us)
Async XLA Ops:
  1.0 9.2 %collective-permute-start = (bf16[16,4736]{1,0:T(8,128)(2,1)S(1)}, bf16[16,4736]{1,0:T(8,128)(2,1)S(1)}, u32[]{:S(2)}, u32[]{:S(2)}) collective-permute-start(bf16[16,4736]{1,0:T(8,128)(2,1)S(1)} %get-tuple-element.37), channel_id=1, source_target_pairs={{0,4},{1,5},{2,6},{3,7},{4,0},{5,1},{6,2},{7,3},{8,12},{9,13},{10,... | collective-permute-start | bytes 454664 | tf_op jit(solution)/shard_map/ppermute | solution.py:24
  4.2 14.2 %collective-permute-start.1 = (bf16[16,4736]{1,0:T(8,128)(2,1)S(1)}, bf16[16,4736]{1,0:T(8,128)(2,1)S(1)}, u32[]{:S(2)}, u32[]{:S(2)}) collective-permute-start(bf16[16,4736]{1,0:T(8,128)(2,1)S(1)} %get-tuple-element.37), channel_id=1, source_target_pairs={{0,8},{1,9},{2,10},{3,11},{4,12},{5,13},{6,14},{7,15},{8,0},{9,1},... | collective-permute-start | bytes 454664 | tf_op jit(solution)/shard_map/ppermute | solution.py:24
  6.7 13.1 %collective-permute-start.2 = (bf16[16,4736]{1,0:T(8,128)(2,1)S(1)}, bf16[16,4736]{1,0:T(8,128)(2,1)S(1)}, u32[]{:S(2)}, u32[]{:S(2)}) collective-permute-start(bf16[16,4736]{1,0:T(8,128)(2,1)S(1)} %get-tuple-element.37), channel_id=1, source_target_pairs={{0,12},{1,13},{2,14},{3,15},{4,8},{5,9},{6,10},{7,11},{8,4},{9,5},... | collective-permute-start | bytes 454664 | tf_op jit(solution)/shard_map/ppermute | solution.py:24
  6.8 13.6 %collective-permute-start.3 = (bf16[16,4736]{1,0:T(8,128)(2,1)S(1)}, bf16[16,4736]{1,0:T(8,128)(2,1)S(1)}, u32[]{:S(2)}, u32[]{:S(2)}) collective-permute-start(bf16[16,4736]{1,0:T(8,128)(2,1)S(1)} %get-tuple-element.37), channel_id=1, source_target_pairs={{0,2},{1,3},{2,0},{3,1},{4,6},{5,7},{6,4},{7,5},{8,10},{9,11},{10,... | collective-permute-start | bytes 454664 | tf_op jit(solution)/shard_map/ppermute | solution.py:24
  8.5 11.9 %collective-permute-start.7 = (bf16[16,4736]{1,0:T(8,128)(2,1)S(1)}, bf16[16,4736]{1,0:T(8,128)(2,1)S(1)}, u32[]{:S(2)}, u32[]{:S(2)}) collective-permute-start(bf16[16,4736]{1,0:T(8,128)(2,1)S(1)} %get-tuple-element.37), channel_id=1, source_target_pairs={{0,1},{1,0},{2,3},{3,2},{4,5},{5,4},{6,7},{7,6},{8,9},{9,8},{10,11... | collective-permute-start | bytes 454664 | tf_op jit(solution)/shard_map/ppermute | solution.py:24
  12.5 8.4 %collective-permute-start.4 = (bf16[16,4736]{1,0:T(8,128)(2,1)S(1)}, bf16[16,4736]{1,0:T(8,128)(2,1)S(1)}, u32[]{:S(2)}, u32[]{:S(2)}) collective-permute-start(bf16[16,4736]{1,0:T(8,128)(2,1)S(1)} %get-tuple-element.43.rest_1_), channel_id=1, source_target_pairs={{0,2},{1,3},{2,0},{3,1},{4,6},{5,7},{6,4},{7,5},{8,10},{9,11},{10,... | collective-permute-start | bytes 454664 | tf_op jit(solution)/shard_map/ppermute | solution.py:24
  18.4 5.2 %collective-permute-start.5 = (bf16[16,4736]{1,0:T(8,128)(2,1)S(1)}, bf16[16,4736]{1,0:T(8,128)(2,1)S(1)}, u32[]{:S(2)}, u32[]{:S(2)}) collective-permute-start(bf16[16,4736]{1,0:T(8,128)(2,1)S(1)} %collective-permute-done.1.rest_2_), channel_id=1, source_target_pairs={{0,2},{1,3},{2,0},{3,1},{4,6},{5,7},{6,4},{7,5},{8,10},{9,11},{10,... | collective-permute-start | bytes 454664 | tf_op jit(solution)/shard_map/ppermute | solution.py:24
  19.9 5.3 %collective-permute-start.6 = (bf16[16,4736]{1,0:T(8,128)(2,1)S(1)}, bf16[16,4736]{1,0:T(8,128)(2,1)S(1)}, u32[]{:S(2)}, u32[]{:S(2)}) collective-permute-start(bf16[16,4736]{1,0:T(8,128)(2,1)S(1)} %collective-permute-done.2.rest_3_), channel_id=1, source_target_pairs={{0,2},{1,3},{2,0},{3,1},{4,6},{5,7},{6,4},{7,5},{8,10},{9,11},{10,... | collective-permute-start | bytes 454664 | tf_op jit(solution)/shard_map/ppermute | solution.py:24
  20.4 4.8 %collective-permute-start.8 = (bf16[16,4736]{1,0:T(8,128)(2,1)S(1)}, bf16[16,4736]{1,0:T(8,128)(2,1)S(1)}, u32[]{:S(2)}, u32[]{:S(2)}) collective-permute-start(bf16[16,4736]{1,0:T(8,128)(2,1)S(1)} %get-tuple-element.43.rest_1_), channel_id=1, source_target_pairs={{0,1},{1,0},{2,3},{3,2},{4,5},{5,4},{6,7},{7,6},{8,9},{9,8},{10,11... | collective-permute-start | bytes 454664 | tf_op jit(solution)/shard_map/ppermute | solution.py:24
  20.4 5.3 %collective-permute-start.9 = (bf16[16,4736]{1,0:T(8,128)(2,1)S(1)}, bf16[16,4736]{1,0:T(8,128)(2,1)S(1)}, u32[]{:S(2)}, u32[]{:S(2)}) collective-permute-start(bf16[16,4736]{1,0:T(8,128)(2,1)S(1)} %collective-permute-done.1.rest_2_), channel_id=1, source_target_pairs={{0,1},{1,0},{2,3},{3,2},{4,5},{5,4},{6,7},{7,6},{8,9},{9,8},{10,11... | collective-permute-start | bytes 454664 | tf_op jit(solution)/shard_map/ppermute | solution.py:24
  20.9 4.9 %collective-permute-start.10 = (bf16[16,4736]{1,0:T(8,128)(2,1)S(1)}, bf16[16,4736]{1,0:T(8,128)(2,1)S(1)}, u32[]{:S(2)}, u32[]{:S(2)}) collective-permute-start(bf16[16,4736]{1,0:T(8,128)(2,1)S(1)} %collective-permute-done.2.rest_3_), channel_id=1, source_target_pairs={{0,1},{1,0},{2,3},{3,2},{4,5},{5,4},{6,7},{7,6},{8,9},{9,8},{10,11... | collective-permute-start | bytes 454664 | tf_op jit(solution)/shard_map/ppermute | solution.py:24
  23.6 2.2 %collective-permute-start.11 = (bf16[16,4736]{1,0:T(8,128)(2,1)S(1)}, bf16[16,4736]{1,0:T(8,128)(2,1)S(1)}, u32[]{:S(2)}, u32[]{:S(2)}) collective-permute-start(bf16[16,4736]{1,0:T(8,128)(2,1)S(1)} %collective-permute-done.3.rest_4_), channel_id=1, source_target_pairs={{0,1},{1,0},{2,3},{3,2},{4,5},{5,4},{6,7},{7,6},{8,9},{9,8},{10,11... | collective-permute-start | bytes 454664 | tf_op jit(solution)/shard_map/ppermute | solution.py:24
  25.2 1.4 %collective-permute-start.12 = (bf16[16,4736]{1,0:T(8,128)(2,1)S(1)}, bf16[16,4736]{1,0:T(8,128)(2,1)S(1)}, u32[]{:S(2)}, u32[]{:S(2)}) collective-permute-start(bf16[16,4736]{1,0:T(8,128)(2,1)S(1)} %collective-permute-done.4.rest_5_), channel_id=1, source_target_pairs={{0,1},{1,0},{2,3},{3,2},{4,5},{5,4},{6,7},{7,6},{8,9},{9,8},{10,11... | collective-permute-start | bytes 454664 | tf_op jit(solution)/shard_map/ppermute | solution.py:24
  25.2 1.6 %collective-permute-start.13 = (bf16[16,4736]{1,0:T(8,128)(2,1)S(1)}, bf16[16,4736]{1,0:T(8,128)(2,1)S(1)}, u32[]{:S(2)}, u32[]{:S(2)}) collective-permute-start(bf16[16,4736]{1,0:T(8,128)(2,1)S(1)} %collective-permute-done.5.rest_6_), channel_id=1, source_target_pairs={{0,1},{1,0},{2,3},{3,2},{4,5},{5,4},{6,7},{7,6},{8,9},{9,8},{10,11... | collective-permute-start | bytes 454664 | tf_op jit(solution)/shard_map/ppermute | solution.py:24
  25.7 1.4 %collective-permute-start.14 = (bf16[16,4736]{1,0:T(8,128)(2,1)S(1)}, bf16[16,4736]{1,0:T(8,128)(2,1)S(1)}, u32[]{:S(2)}, u32[]{:S(2)}) collective-permute-start(bf16[16,4736]{1,0:T(8,128)(2,1)S(1)} %collective-permute-done.6.rest_7_), channel_id=1, source_target_pairs={{0,1},{1,0},{2,3},{3,2},{4,5},{5,4},{6,7},{7,6},{8,9},{9,8},{10,11... | collective-permute-start | bytes 454664 | tf_op jit(solution)/shard_map/ppermute | solution.py:24
  27.1 78.6 %copy-start.1 = (bf16[1,768,4096]{2,1,0:T(8,128)(2,1)S(1)}, bf16[1,768,4096]{2,1,0:T(8,128)(2,1)}, u32[]{:S(2)}) copy-start(bf16[1,768,4096]{2,1,0:T(8,128)(2,1)} %down_ref.1) | copy-start | bytes 18874372
  32.4 1.6 %collective-permute-start.15 = (bf16[2,288,256]{2,1,0:T(8,128)(2,1)S(1)}, bf16[2,288,256]{2,1,0:T(8,128)(2,1)S(1)}, u32[]{:S(2)}, u32[]{:S(2)}) collective-permute-start(bf16[2,288,256]{2,1,0:T(8,128)(2,1)S(1)} %get-tuple-element.46), channel_id=1, source_target_pairs={{0,1},{1,0},{2,3},{3,2},{4,5},{5,4},{6,7},{7,6},{8,9},{9,8},{10,11... | collective-permute-start | bytes 884744 | tf_op jit(solution)/shard_map/ppermute | solution.py:24
  32.7 3.1 %collective-permute-start.18 = (bf16[2,288,256]{2,1,0:T(8,128)(2,1)S(1)}, bf16[2,288,256]{2,1,0:T(8,128)(2,1)S(1)}, u32[]{:S(2)}, u32[]{:S(2)}) collective-permute-start(bf16[2,288,256]{2,1,0:T(8,128)(2,1)S(1)} %get-tuple-element.48), channel_id=1, source_target_pairs={{0,1},{1,0},{2,3},{3,2},{4,5},{5,4},{6,7},{7,6},{8,9},{9,8},{10,11... | collective-permute-start | bytes 884744 | tf_op jit(solution)/shard_map/ppermute | solution.py:24
  33.0 3.5 %collective-permute-start.21 = (bf16[2,288,256]{2,1,0:T(8,128)(2,1)S(1)}, bf16[2,288,256]{2,1,0:T(8,128)(2,1)S(1)}, u32[]{:S(2)}, u32[]{:S(2)}) collective-permute-start(bf16[2,288,256]{2,1,0:T(8,128)(2,1)S(1)} %get-tuple-element.50), channel_id=1, source_target_pairs={{0,1},{1,0},{2,3},{3,2},{4,5},{5,4},{6,7},{7,6},{8,9},{9,8},{10,11... | collective-permute-start | bytes 884744 | tf_op jit(solution)/shard_map/ppermute | solution.py:24
  33.2 4.9 %collective-permute-start.24 = (bf16[2,288,256]{2,1,0:T(8,128)(2,1)S(1)}, bf16[2,288,256]{2,1,0:T(8,128)(2,1)S(1)}, u32[]{:S(2)}, u32[]{:S(2)}) collective-permute-start(bf16[2,288,256]{2,1,0:T(8,128)(2,1)S(1)} %get-tuple-element.52), channel_id=1, source_target_pairs={{0,1},{1,0},{2,3},{3,2},{4,5},{5,4},{6,7},{7,6},{8,9},{9,8},{10,11... | collective-permute-start | bytes 884744 | tf_op jit(solution)/shard_map/ppermute | solution.py:24
  34.2 6.8 %collective-permute-start.16 = (bf16[288,256]{1,0:T(8,128)(2,1)S(1)}, bf16[288,256]{1,0:T(8,128)(2,1)S(1)}, u32[]{:S(2)}, u32[]{:S(2)}) collective-permute-start(bf16[288,256]{1,0:T(8,128)(2,1)S(1)} %slice_bitcast_fusion.6), channel_id=1, source_target_pairs={{0,2},{1,3},{2,0},{3,1},{4,6},{5,7},{6,4},{7,5},{8,10},{9,11},{10,... | collective-permute-start | bytes 442376 | tf_op jit(solution)/shard_map/ppermute | solution.py:24
  35.9 8.2 %collective-permute-start.19 = (bf16[288,256]{1,0:T(8,128)(2,1)S(1)}, bf16[288,256]{1,0:T(8,128)(2,1)S(1)}, u32[]{:S(2)}, u32[]{:S(2)}) collective-permute-start(bf16[288,256]{1,0:T(8,128)(2,1)S(1)} %slice_bitcast_fusion.4), channel_id=1, source_target_pairs={{0,2},{1,3},{2,0},{3,1},{4,6},{5,7},{6,4},{7,5},{8,10},{9,11},{10,... | collective-permute-start | bytes 442376 | tf_op jit(solution)/shard_map/ppermute | solution.py:24
  36.6 10.7 %collective-permute-start.22 = (bf16[288,256]{1,0:T(8,128)(2,1)S(1)}, bf16[288,256]{1,0:T(8,128)(2,1)S(1)}, u32[]{:S(2)}, u32[]{:S(2)}) collective-permute-start(bf16[288,256]{1,0:T(8,128)(2,1)S(1)} %slice_bitcast_fusion.2), channel_id=1, source_target_pairs={{0,2},{1,3},{2,0},{3,1},{4,6},{5,7},{6,4},{7,5},{8,10},{9,11},{10,... | collective-permute-start | bytes 442376 | tf_op jit(solution)/shard_map/ppermute | solution.py:24
  38.3 11.4 %collective-permute-start.25 = (bf16[288,256]{1,0:T(8,128)(2,1)S(1)}, bf16[288,256]{1,0:T(8,128)(2,1)S(1)}, u32[]{:S(2)}, u32[]{:S(2)}) collective-permute-start(bf16[288,256]{1,0:T(8,128)(2,1)S(1)} %slice_bitcast_fusion), channel_id=1, source_target_pairs={{0,2},{1,3},{2,0},{3,1},{4,6},{5,7},{6,4},{7,5},{8,10},{9,11},{10,... | collective-permute-start | bytes 442376 | tf_op jit(solution)/shard_map/ppermute | solution.py:24
  41.0 8.7 %collective-permute-start.17 = (bf16[288,256]{1,0:T(8,128)(2,1)S(1)}, bf16[288,256]{1,0:T(8,128)(2,1)S(1)}, u32[]{:S(2)}, u32[]{:S(2)}) collective-permute-start(bf16[288,256]{1,0:T(8,128)(2,1)S(1)} %fusion.7), channel_id=1, source_target_pairs={{0,12},{1,13},{2,14},{3,15},{4,8},{5,9},{6,10},{7,11},{8,4},{9,5},... | collective-permute-start | bytes 442376 | tf_op jit(solution)/shard_map/ppermute | solution.py:24
  44.2 11.3 %collective-permute-start.20 = (bf16[288,256]{1,0:T(8,128)(2,1)S(1)}, bf16[288,256]{1,0:T(8,128)(2,1)S(1)}, u32[]{:S(2)}, u32[]{:S(2)}) collective-permute-start(bf16[288,256]{1,0:T(8,128)(2,1)S(1)} %fusion.6), channel_id=1, source_target_pairs={{0,8},{1,9},{2,10},{3,11},{4,12},{5,13},{6,14},{7,15},{8,0},{9,1},... | collective-permute-start | bytes 442376 | tf_op jit(solution)/shard_map/ppermute | solution.py:24
  47.3 8.1 %collective-permute-start.23 = (bf16[288,256]{1,0:T(8,128)(2,1)S(1)}, bf16[288,256]{1,0:T(8,128)(2,1)S(1)}, u32[]{:S(2)}, u32[]{:S(2)}) collective-permute-start(bf16[288,256]{1,0:T(8,128)(2,1)S(1)} %fusion.5), channel_id=1, source_target_pairs={{0,4},{1,5},{2,6},{3,7},{4,0},{5,1},{6,2},{7,3},{8,12},{9,13},{10,... | collective-permute-start | bytes 442376 | tf_op jit(solution)/shard_map/ppermute | solution.py:24
  57.2 1.6 %collective-permute-start.35 = (bf16[2,16,4096]{2,1,0:T(8,128)(2,1)S(1)}, bf16[2,16,4096]{2,1,0:T(8,128)(2,1)S(1)}, u32[]{:S(2)}, u32[]{:S(2)}) collective-permute-start(bf16[2,16,4096]{2,1,0:T(8,128)(2,1)S(1)} %get-tuple-element.60), channel_id=1, source_target_pairs={{0,1},{1,0},{2,3},{3,2},{4,5},{5,4},{6,7},{7,6},{8,9},{9,8},{10,11... | collective-permute-start | bytes 786440 | tf_op jit(solution)/shard_map/ppermute | solution.py:24
  57.2 3.2 %collective-permute-start.32 = (bf16[2,16,4096]{2,1,0:T(8,128)(2,1)S(1)}, bf16[2,16,4096]{2,1,0:T(8,128)(2,1)S(1)}, u32[]{:S(2)}, u32[]{:S(2)}) collective-permute-start(bf16[2,16,4096]{2,1,0:T(8,128)(2,1)S(1)} %get-tuple-element.58), channel_id=1, source_target_pairs={{0,1},{1,0},{2,3},{3,2},{4,5},{5,4},{6,7},{7,6},{8,9},{9,8},{10,11... | collective-permute-start | bytes 786440 | tf_op jit(solution)/shard_map/ppermute | solution.py:24
  57.7 3.4 %collective-permute-start.29 = (bf16[2,16,4096]{2,1,0:T(8,128)(2,1)S(1)}, bf16[2,16,4096]{2,1,0:T(8,128)(2,1)S(1)}, u32[]{:S(2)}, u32[]{:S(2)}) collective-permute-start(bf16[2,16,4096]{2,1,0:T(8,128)(2,1)S(1)} %get-tuple-element.56), channel_id=1, source_target_pairs={{0,1},{1,0},{2,3},{3,2},{4,5},{5,4},{6,7},{7,6},{8,9},{9,8},{10,11... | collective-permute-start | bytes 786440 | tf_op jit(solution)/shard_map/ppermute | solution.py:24
  57.8 5.0 %collective-permute-start.26 = (bf16[2,16,4096]{2,1,0:T(8,128)(2,1)S(1)}, bf16[2,16,4096]{2,1,0:T(8,128)(2,1)S(1)}, u32[]{:S(2)}, u32[]{:S(2)}) collective-permute-start(bf16[2,16,4096]{2,1,0:T(8,128)(2,1)S(1)} %get-tuple-element.54), channel_id=1, source_target_pairs={{0,1},{1,0},{2,3},{3,2},{4,5},{5,4},{6,7},{7,6},{8,9},{9,8},{10,11... | collective-permute-start | bytes 786440 | tf_op jit(solution)/shard_map/ppermute | solution.py:24
  58.9 16.8 %collective-permute-start.36 = (bf16[16,4096]{1,0:T(8,128)(2,1)S(1)}, bf16[16,4096]{1,0:T(8,128)(2,1)S(1)}, u32[]{:S(2)}, u32[]{:S(2)}) collective-permute-start(bf16[16,4096]{1,0:T(8,128)(2,1)S(1)} %slice_bitcast_fusion.16), channel_id=1, source_target_pairs={{0,2},{1,3},{2,0},{3,1},{4,6},{5,7},{6,4},{7,5},{8,10},{9,11},{10,... | collective-permute-start | bytes 393224 | tf_op jit(solution)/shard_map/ppermute | solution.py:24
  60.5 7.6 %collective-permute-start.33 = (bf16[16,4096]{1,0:T(8,128)(2,1)S(1)}, bf16[16,4096]{1,0:T(8,128)(2,1)S(1)}, u32[]{:S(2)}, u32[]{:S(2)}) collective-permute-start(bf16[16,4096]{1,0:T(8,128)(2,1)S(1)} %slice_bitcast_fusion.18), channel_id=1, source_target_pairs={{0,2},{1,3},{2,0},{3,1},{4,6},{5,7},{6,4},{7,5},{8,10},{9,11},{10,... | collective-permute-start | bytes 393224 | tf_op jit(solution)/shard_map/ppermute | solution.py:24
  61.2 9.7 %collective-permute-start.30 = (bf16[16,4096]{1,0:T(8,128)(2,1)S(1)}, bf16[16,4096]{1,0:T(8,128)(2,1)S(1)}, u32[]{:S(2)}, u32[]{:S(2)}) collective-permute-start(bf16[16,4096]{1,0:T(8,128)(2,1)S(1)} %slice_bitcast_fusion.20), channel_id=1, source_target_pairs={{0,2},{1,3},{2,0},{3,1},{4,6},{5,7},{6,4},{7,5},{8,10},{9,11},{10,... | collective-permute-start | bytes 393224 | tf_op jit(solution)/shard_map/ppermute | solution.py:24
  62.9 10.0 %collective-permute-start.27 = (bf16[16,4096]{1,0:T(8,128)(2,1)S(1)}, bf16[16,4096]{1,0:T(8,128)(2,1)S(1)}, u32[]{:S(2)}, u32[]{:S(2)}) collective-permute-start(bf16[16,4096]{1,0:T(8,128)(2,1)S(1)} %slice_bitcast_fusion.22), channel_id=1, source_target_pairs={{0,2},{1,3},{2,0},{3,1},{4,6},{5,7},{6,4},{7,5},{8,10},{9,11},{10,... | collective-permute-start | bytes 393224 | tf_op jit(solution)/shard_map/ppermute | solution.py:24
  68.1 7.6 %collective-permute-start.34 = (bf16[16,4096]{1,0:T(8,128)(2,1)S(1)}, bf16[16,4096]{1,0:T(8,128)(2,1)S(1)}, u32[]{:S(2)}, u32[]{:S(2)}) collective-permute-start(bf16[16,4096]{1,0:T(8,128)(2,1)S(1)} %fusion.13), channel_id=1, source_target_pairs={{0,4},{1,5},{2,6},{3,7},{4,0},{5,1},{6,2},{7,3},{8,12},{9,13},{10,... | collective-permute-start | bytes 393224 | tf_op jit(solution)/shard_map/ppermute | solution.py:24
  70.9 11.4 %collective-permute-start.31 = (bf16[16,4096]{1,0:T(8,128)(2,1)S(1)}, bf16[16,4096]{1,0:T(8,128)(2,1)S(1)}, u32[]{:S(2)}, u32[]{:S(2)}) collective-permute-start(bf16[16,4096]{1,0:T(8,128)(2,1)S(1)} %fusion.14), channel_id=1, source_target_pairs={{0,8},{1,9},{2,10},{3,11},{4,12},{5,13},{6,14},{7,15},{8,0},{9,1},... | collective-permute-start | bytes 393224 | tf_op jit(solution)/shard_map/ppermute | solution.py:24
  72.9 9.4 %collective-permute-start.28 = (bf16[16,4096]{1,0:T(8,128)(2,1)S(1)}, bf16[16,4096]{1,0:T(8,128)(2,1)S(1)}, u32[]{:S(2)}, u32[]{:S(2)}) collective-permute-start(bf16[16,4096]{1,0:T(8,128)(2,1)S(1)} %fusion.15), channel_id=1, source_target_pairs={{0,12},{1,13},{2,14},{3,15},{4,8},{5,9},{6,10},{7,11},{8,4},{9,5},... | collective-permute-start | bytes 393224 | tf_op jit(solution)/shard_map/ppermute | solution.py:24
  82.7 6.5 %collective-permute-start.37 = (bf16[16,4096]{1,0:T(8,128)(2,1)S(1)}, bf16[16,4096]{1,0:T(8,128)(2,1)S(1)}, u32[]{:S(2)}, u32[]{:S(2)}) collective-permute-start(bf16[16,4096]{1,0:T(8,128)(2,1)S(1)} %fusion.2.rest_0_), channel_id=1, source_target_pairs={{0,4},{1,5},{2,6},{3,7},{4,0},{5,1},{6,2},{7,3},{8,12},{9,13},{10,... | collective-permute-start | bytes 393224 | tf_op jit(solution)/shard_map/ppermute | solution.py:24
  85.2 12.1 %collective-permute-start.38 = (bf16[16,4096]{1,0:T(8,128)(2,1)S(1)}, bf16[16,4096]{1,0:T(8,128)(2,1)S(1)}, u32[]{:S(2)}, u32[]{:S(2)}) collective-permute-start(bf16[16,4096]{1,0:T(8,128)(2,1)S(1)} %fusion.2.rest_0_), channel_id=1, source_target_pairs={{0,8},{1,9},{2,10},{3,11},{4,12},{5,13},{6,14},{7,15},{8,0},{9,1},... | collective-permute-start | bytes 393224 | tf_op jit(solution)/shard_map/ppermute | solution.py:24
  85.8 13.0 %collective-permute-start.39 = (bf16[16,4096]{1,0:T(8,128)(2,1)S(1)}, bf16[16,4096]{1,0:T(8,128)(2,1)S(1)}, u32[]{:S(2)}, u32[]{:S(2)}) collective-permute-start(bf16[16,4096]{1,0:T(8,128)(2,1)S(1)} %fusion.2.rest_0_), channel_id=1, source_target_pairs={{0,12},{1,13},{2,14},{3,15},{4,8},{5,9},{6,10},{7,11},{8,4},{9,5},... | collective-permute-start | bytes 393224 | tf_op jit(solution)/shard_map/ppermute | solution.py:24
  87.6 11.7 %collective-permute-start.40 = (bf16[16,4096]{1,0:T(8,128)(2,1)S(1)}, bf16[16,4096]{1,0:T(8,128)(2,1)S(1)}, u32[]{:S(2)}, u32[]{:S(2)}) collective-permute-start(bf16[16,4096]{1,0:T(8,128)(2,1)S(1)} %fusion.2.rest_0_), channel_id=1, source_target_pairs={{0,2},{1,3},{2,0},{3,1},{4,6},{5,7},{6,4},{7,5},{8,10},{9,11},{10,... | collective-permute-start | bytes 393224 | tf_op jit(solution)/shard_map/ppermute | solution.py:24
  89.1 10.1 %collective-permute-start.44 = (bf16[16,4096]{1,0:T(8,128)(2,1)S(1)}, bf16[16,4096]{1,0:T(8,128)(2,1)S(1)}, u32[]{:S(2)}, u32[]{:S(2)}) collective-permute-start(bf16[16,4096]{1,0:T(8,128)(2,1)S(1)} %fusion.2.rest_0_), channel_id=1, source_target_pairs={{0,1},{1,0},{2,3},{3,2},{4,5},{5,4},{6,7},{7,6},{8,9},{9,8},{10,11... | collective-permute-start | bytes 393224 | tf_op jit(solution)/shard_map/ppermute | solution.py:24
  89.2 10.6 %collective-permute-start.41 = (bf16[16,4096]{1,0:T(8,128)(2,1)S(1)}, bf16[16,4096]{1,0:T(8,128)(2,1)S(1)}, u32[]{:S(2)}, u32[]{:S(2)}) collective-permute-start(bf16[16,4096]{1,0:T(8,128)(2,1)S(1)} %collective-permute-done.37.rest_1_), channel_id=1, source_target_pairs={{0,2},{1,3},{2,0},{3,1},{4,6},{5,7},{6,4},{7,5},{8,10},{9,11},{10,... | collective-permute-start | bytes 393224 | tf_op jit(solution)/shard_map/ppermute | solution.py:24
  97.2 5.0 %collective-permute-start.42 = (bf16[16,4096]{1,0:T(8,128)(2,1)S(1)}, bf16[16,4096]{1,0:T(8,128)(2,1)S(1)}, u32[]{:S(2)}, u32[]{:S(2)}) collective-permute-start(bf16[16,4096]{1,0:T(8,128)(2,1)S(1)} %collective-permute-done.38.rest_2_), channel_id=1, source_target_pairs={{0,2},{1,3},{2,0},{3,1},{4,6},{5,7},{6,4},{7,5},{8,10},{9,11},{10,... | collective-permute-start | bytes 393224 | tf_op jit(solution)/shard_map/ppermute | solution.py:24
  98.8 5.0 %collective-permute-start.43 = (bf16[16,4096]{1,0:T(8,128)(2,1)S(1)}, bf16[16,4096]{1,0:T(8,128)(2,1)S(1)}, u32[]{:S(2)}, u32[]{:S(2)}) collective-permute-start(bf16[16,4096]{1,0:T(8,128)(2,1)S(1)} %collective-permute-done.39.rest_3_), channel_id=1, source_target_pairs={{0,2},{1,3},{2,0},{3,1},{4,6},{5,7},{6,4},{7,5},{8,10},{9,11},{10,... | collective-permute-start | bytes 393224 | tf_op jit(solution)/shard_map/ppermute | solution.py:24
  99.3 4.5 %collective-permute-start.45 = (bf16[16,4096]{1,0:T(8,128)(2,1)S(1)}, bf16[16,4096]{1,0:T(8,128)(2,1)S(1)}, u32[]{:S(2)}, u32[]{:S(2)}) collective-permute-start(bf16[16,4096]{1,0:T(8,128)(2,1)S(1)} %collective-permute-done.37.rest_1_), channel_id=1, source_target_pairs={{0,1},{1,0},{2,3},{3,2},{4,5},{5,4},{6,7},{7,6},{8,9},{9,8},{10,11... | collective-permute-start | bytes 393224 | tf_op jit(solution)/shard_map/ppermute | solution.py:24
  99.3 5.0 %collective-permute-start.46 = (bf16[16,4096]{1,0:T(8,128)(2,1)S(1)}, bf16[16,4096]{1,0:T(8,128)(2,1)S(1)}, u32[]{:S(2)}, u32[]{:S(2)}) collective-permute-start(bf16[16,4096]{1,0:T(8,128)(2,1)S(1)} %collective-permute-done.38.rest_2_), channel_id=1, source_target_pairs={{0,1},{1,0},{2,3},{3,2},{4,5},{5,4},{6,7},{7,6},{8,9},{9,8},{10,11... | collective-permute-start | bytes 393224 | tf_op jit(solution)/shard_map/ppermute | solution.py:24
  99.8 4.6 %collective-permute-start.47 = (bf16[16,4096]{1,0:T(8,128)(2,1)S(1)}, bf16[16,4096]{1,0:T(8,128)(2,1)S(1)}, u32[]{:S(2)}, u32[]{:S(2)}) collective-permute-start(bf16[16,4096]{1,0:T(8,128)(2,1)S(1)} %collective-permute-done.39.rest_3_), channel_id=1, source_target_pairs={{0,1},{1,0},{2,3},{3,2},{4,5},{5,4},{6,7},{7,6},{8,9},{9,8},{10,11... | collective-permute-start | bytes 393224 | tf_op jit(solution)/shard_map/ppermute | solution.py:24
  102.2 2.2 %collective-permute-start.48 = (bf16[16,4096]{1,0:T(8,128)(2,1)S(1)}, bf16[16,4096]{1,0:T(8,128)(2,1)S(1)}, u32[]{:S(2)}, u32[]{:S(2)}) collective-permute-start(bf16[16,4096]{1,0:T(8,128)(2,1)S(1)} %collective-permute-done.40.rest_4_), channel_id=1, source_target_pairs={{0,1},{1,0},{2,3},{3,2},{4,5},{5,4},{6,7},{7,6},{8,9},{9,8},{10,11... | collective-permute-start | bytes 393224 | tf_op jit(solution)/shard_map/ppermute | solution.py:24
  103.8 1.3 %collective-permute-start.49 = (bf16[16,4096]{1,0:T(8,128)(2,1)S(1)}, bf16[16,4096]{1,0:T(8,128)(2,1)S(1)}, u32[]{:S(2)}, u32[]{:S(2)}) collective-permute-start(bf16[16,4096]{1,0:T(8,128)(2,1)S(1)} %collective-permute-done.41.rest_5_), channel_id=1, source_target_pairs={{0,1},{1,0},{2,3},{3,2},{4,5},{5,4},{6,7},{7,6},{8,9},{9,8},{10,11... | collective-permute-start | bytes 393224 | tf_op jit(solution)/shard_map/ppermute | solution.py:24
  103.8 1.5 %collective-permute-start.50 = (bf16[16,4096]{1,0:T(8,128)(2,1)S(1)}, bf16[16,4096]{1,0:T(8,128)(2,1)S(1)}, u32[]{:S(2)}, u32[]{:S(2)}) collective-permute-start(bf16[16,4096]{1,0:T(8,128)(2,1)S(1)} %collective-permute-done.42.rest_6_), channel_id=1, source_target_pairs={{0,1},{1,0},{2,3},{3,2},{4,5},{5,4},{6,7},{7,6},{8,9},{9,8},{10,11... | collective-permute-start | bytes 393224 | tf_op jit(solution)/shard_map/ppermute | solution.py:24
  104.3 1.3 %collective-permute-start.51 = (bf16[16,4096]{1,0:T(8,128)(2,1)S(1)}, bf16[16,4096]{1,0:T(8,128)(2,1)S(1)}, u32[]{:S(2)}, u32[]{:S(2)}) collective-permute-start(bf16[16,4096]{1,0:T(8,128)(2,1)S(1)} %collective-permute-done.43.rest_7_), channel_id=1, source_target_pairs={{0,1},{1,0},{2,3},{3,2},{4,5},{5,4},{6,7},{7,6},{8,9},{9,8},{10,11... | collective-permute-start | bytes 393224 | tf_op jit(solution)/shard_map/ppermute | solution.py:24
  110.8 1.6 %collective-permute-start.58 = (bf16[2,16,4096]{2,1,0:T(8,128)(2,1)S(1)}, bf16[2,16,4096]{2,1,0:T(8,128)(2,1)S(1)}, u32[]{:S(2)}, u32[]{:S(2)}) collective-permute-start(bf16[2,16,4096]{2,1,0:T(8,128)(2,1)S(1)} %get-tuple-element.66), channel_id=1, source_target_pairs={{0,1},{1,0},{2,3},{3,2},{4,5},{5,4},{6,7},{7,6},{8,9},{9,8},{10,11... | collective-permute-start | bytes 786440 | tf_op jit(solution)/shard_map/ppermute | solution.py:24
  111.1 2.9 %collective-permute-start.55 = (bf16[2,16,4096]{2,1,0:T(8,128)(2,1)S(1)}, bf16[2,16,4096]{2,1,0:T(8,128)(2,1)S(1)}, u32[]{:S(2)}, u32[]{:S(2)}) collective-permute-start(bf16[2,16,4096]{2,1,0:T(8,128)(2,1)S(1)} %get-tuple-element.64), channel_id=1, source_target_pairs={{0,1},{1,0},{2,3},{3,2},{4,5},{5,4},{6,7},{7,6},{8,9},{9,8},{10,11... | collective-permute-start | bytes 786440 | tf_op jit(solution)/shard_map/ppermute | solution.py:24
  111.4 3.4 %collective-permute-start.52 = (bf16[2,16,4096]{2,1,0:T(8,128)(2,1)S(1)}, bf16[2,16,4096]{2,1,0:T(8,128)(2,1)S(1)}, u32[]{:S(2)}, u32[]{:S(2)}) collective-permute-start(bf16[2,16,4096]{2,1,0:T(8,128)(2,1)S(1)} %get-tuple-element.62), channel_id=1, source_target_pairs={{0,1},{1,0},{2,3},{3,2},{4,5},{5,4},{6,7},{7,6},{8,9},{9,8},{10,11... | collective-permute-start | bytes 786440 | tf_op jit(solution)/shard_map/ppermute | solution.py:24
  111.6 4.7 %collective-permute-start.61 = (bf16[2,16,4096]{2,1,0:T(8,128)(2,1)S(1)}, bf16[2,16,4096]{2,1,0:T(8,128)(2,1)S(1)}, u32[]{:S(2)}, u32[]{:S(2)}) collective-permute-start(bf16[2,16,4096]{2,1,0:T(8,128)(2,1)S(1)} %get-tuple-element.68), channel_id=1, source_target_pairs={{0,1},{1,0},{2,3},{3,2},{4,5},{5,4},{6,7},{7,6},{8,9},{9,8},{10,11... | collective-permute-start | bytes 786440 | tf_op jit(solution)/shard_map/ppermute | solution.py:24
  112.5 6.4 %collective-permute-start.59 = (bf16[16,4096]{1,0:T(8,128)(2,1)S(1)}, bf16[16,4096]{1,0:T(8,128)(2,1)S(1)}, u32[]{:S(2)}, u32[]{:S(2)}) collective-permute-start(bf16[16,4096]{1,0:T(8,128)(2,1)S(1)} %slice_bitcast_fusion.10), channel_id=1, source_target_pairs={{0,2},{1,3},{2,0},{3,1},{4,6},{5,7},{6,4},{7,5},{8,10},{9,11},{10,... | collective-permute-start | bytes 393224 | tf_op jit(solution)/shard_map/ppermute | solution.py:24
  114.1 7.7 %collective-permute-start.56 = (bf16[16,4096]{1,0:T(8,128)(2,1)S(1)}, bf16[16,4096]{1,0:T(8,128)(2,1)S(1)}, u32[]{:S(2)}, u32[]{:S(2)}) collective-permute-start(bf16[16,4096]{1,0:T(8,128)(2,1)S(1)} %slice_bitcast_fusion.12), channel_id=1, source_target_pairs={{0,2},{1,3},{2,0},{3,1},{4,6},{5,7},{6,4},{7,5},{8,10},{9,11},{10,... | collective-permute-start | bytes 393224 | tf_op jit(solution)/shard_map/ppermute | solution.py:24
  114.9 9.7 %collective-permute-start.53 = (bf16[16,4096]{1,0:T(8,128)(2,1)S(1)}, bf16[16,4096]{1,0:T(8,128)(2,1)S(1)}, u32[]{:S(2)}, u32[]{:S(2)}) collective-permute-start(bf16[16,4096]{1,0:T(8,128)(2,1)S(1)} %slice_bitcast_fusion.14), channel_id=1, source_target_pairs={{0,2},{1,3},{2,0},{3,1},{4,6},{5,7},{6,4},{7,5},{8,10},{9,11},{10,... | collective-permute-start | bytes 393224 | tf_op jit(solution)/shard_map/ppermute | solution.py:24
  116.4 10.2 %collective-permute-start.62 = (bf16[16,4096]{1,0:T(8,128)(2,1)S(1)}, bf16[16,4096]{1,0:T(8,128)(2,1)S(1)}, u32[]{:S(2)}, u32[]{:S(2)}) collective-permute-start(bf16[16,4096]{1,0:T(8,128)(2,1)S(1)} %slice_bitcast_fusion.8), channel_id=1, source_target_pairs={{0,2},{1,3},{2,0},{3,1},{4,6},{5,7},{6,4},{7,5},{8,10},{9,11},{10,... | collective-permute-start | bytes 393224 | tf_op jit(solution)/shard_map/ppermute | solution.py:24
  119.0 7.6 %collective-permute-start.60 = (bf16[16,4096]{1,0:T(8,128)(2,1)S(1)}, bf16[16,4096]{1,0:T(8,128)(2,1)S(1)}, u32[]{:S(2)}, u32[]{:S(2)}) collective-permute-start(bf16[16,4096]{1,0:T(8,128)(2,1)S(1)} %fusion.9), channel_id=1, source_target_pairs={{0,4},{1,5},{2,6},{3,7},{4,0},{5,1},{6,2},{7,3},{8,12},{9,13},{10,... | collective-permute-start | bytes 393224 | tf_op jit(solution)/shard_map/ppermute | solution.py:24
  121.8 11.5 %collective-permute-start.57 = (bf16[16,4096]{1,0:T(8,128)(2,1)S(1)}, bf16[16,4096]{1,0:T(8,128)(2,1)S(1)}, u32[]{:S(2)}, u32[]{:S(2)}) collective-permute-start(bf16[16,4096]{1,0:T(8,128)(2,1)S(1)} %fusion.10), channel_id=1, source_target_pairs={{0,8},{1,9},{2,10},{3,11},{4,12},{5,13},{6,14},{7,15},{8,0},{9,1},... | collective-permute-start | bytes 393224 | tf_op jit(solution)/shard_map/ppermute | solution.py:24
  124.6 8.7 %collective-permute-start.54 = (bf16[16,4096]{1,0:T(8,128)(2,1)S(1)}, bf16[16,4096]{1,0:T(8,128)(2,1)S(1)}, u32[]{:S(2)}, u32[]{:S(2)}) collective-permute-start(bf16[16,4096]{1,0:T(8,128)(2,1)S(1)} %fusion.11), channel_id=1, source_target_pairs={{0,12},{1,13},{2,14},{3,15},{4,8},{5,9},{6,10},{7,11},{8,4},{9,5},... | collective-permute-start | bytes 393224 | tf_op jit(solution)/shard_map/ppermute | solution.py:24
  (5 other events, 273.2 us)

commit v4 on v3

--- a/solution.py
+++ b/solution.py
@@ -50,6 +50,17 @@
     for i in reversed(range(devices // 4)):
         pair = keep[i] + swap(send[i], 1, devices)
         mine = pair[0] + swap(pair[1], 2, devices)
+        pieces.append(swap(mine, 4 * i, devices) if i else mine)
+    return pieces
+
+
+def scatter_sides(blocks, devices):
+    far = devices // 4
+    pieces = []
+    for i in reversed(range(far)):
+        away = blocks[far + i] + swap(blocks[3 * far + i], 1, devices)
+        home = blocks[i] + swap(blocks[2 * far + i], 1, devices)
+        mine = home + swap(away, 2, devices)
         pieces.append(swap(mine, 4 * i, devices) if i else mine)
     return pieces
 
@@ -359,14 +370,14 @@
 
 
 def expert_kernel(
-    me_ref, gate_ref, up_ref, down_ref, own_ref, *rest, devices, row_dev, top, ext_at
+    me_ref, gate_ref, up_ref, down_ref, own_ref, *rest, spots, row_dev, top, ext_at
 ):
-    pieces = rest[:devices]
-    outs = split_refs(rest[devices : devices + devices // 2], devices)
-    x_scr, h_scr = rest[devices + devices // 2 :]
-    rows = devices * row_dev
+    count = len(spots)
+    pieces, outs = rest[:count], rest[count : 2 * count]
+    x_scr, h_scr = rest[2 * count :]
+    rows = count * row_dev
     me = me_ref[0].astype(F32)
-    for p in range(devices):
+    for p in range(count):
         x_scr[p * row_dev : (p + 1) * row_dev, :] = pieces[p][...]
     ff = gate_ref.shape[2]
     d_model = gate_ref.shape[1]
@@ -376,7 +387,9 @@
         a = jnp.dot(x_scr[...], gate_ref[0, :, cut], preferred_element_type=F32)
         b = jnp.dot(x_scr[...], up_ref[0, :, cut], preferred_element_type=F32)
         h_scr[:, cut] = (a / (1.0 + jnp.exp(-a)) * b).astype(BF)
-    e = own_ref[:, ext_at : ext_at + LANES].astype(F32)
+    e = jnp.concatenate(
+        [own_ref[p * row_dev : (p + 1) * row_dev, ext_at : ext_at + LANES] for p in spots], axis=0
+    ).astype(F32)
     lane = lax.broadcasted_iota(jnp.int32, (rows, LANES), 1)
     score = jnp.where(jnp.logical_and(lane >= top, lane < 2 * top), jnp.exp(e * 0.25), 0.0)
     total = jnp.sum(score, axis=1, keepdims=True)
@@ -389,9 +402,8 @@
         cut = slice(c * step, (c + 1) * step)
         y = jnp.dot(h_scr[...], down_ref[0, :, cut], preferred_element_type=F32)
         y = (y.astype(BF).astype(F32) * weight).astype(BF)
-        for p in range(devices):
-            out_ref, side = outs[p]
-            out_ref[side, :, cut] = y[p * row_dev : (p + 1) * row_dev]
+        for p in range(count):
+            outs[p][:, cut] = y[p * row_dev : (p + 1) * row_dev]
 
 
 def on_device(
@@ -507,21 +519,26 @@
     ).astype(BF)
     tokens = gather_blocks(normed, devices)
     ff = w_gate.shape[2]
-    moe = pl.pallas_call(
-        functools.partial(
-            expert_kernel, devices=devices, row_dev=row_dev, top=top, ext_at=own_at
-        ),
-        out_shape=split_shapes(devices, (row_dev, d_model)),
-        in_specs=[smem] + [vmem] * (4 + devices),
-        out_specs=[vmem] * half,
-        scratch_shapes=[
-            pltpu.VMEM((rows, d_model), BF),
-            pltpu.VMEM((rows, ff), BF),
-        ],
-        compiler_params=budget(14),
-        name="experts",
-    )(me, w_gate, w_up, w_down, own, *map(in_vmem, tokens))
-    summed = sum(p.astype(F32) for p in scatter_blocks(moe[:far], moe[far:], devices))
+    moe = [None] * devices
+    for side in range(2):
+        spots = [p for p in range(devices) if p // far % 2 == side]
+        call = pl.pallas_call(
+            functools.partial(
+                expert_kernel, spots=spots, row_dev=row_dev, top=top, ext_at=own_at
+            ),
+            out_shape=[pltpu.VMEM((row_dev, d_model), BF)] * half,
+            in_specs=[smem] + [vmem] * (4 + half),
+            out_specs=[vmem] * half,
+            scratch_shapes=[
+                pltpu.VMEM((half * row_dev, d_model), BF),
+                pltpu.VMEM((half * row_dev, ff), BF),
+            ],
+            compiler_params=budget(14),
+        )
+        done = call(me, w_gate, w_up, w_down, own, *(in_vmem(tokens[p]) for p in spots))
+        for p, y in zip(spots, done):
+            moe[p] = y
+    summed = sum(p.astype(F32) for p in scatter_sides(moe, devices))
     return (mixed + summed).astype(BF)
 
 

time: 134 us -> 135 us (level)
  starting transfers between devices: 52.9 us -> 54.9 us
  waiting for transfers between devices: 62.9 us -> 61.4 us
    ppermute x63 -> x67, starting transfers between devices: 52.9 us -> 54.9 us  [swap(): return lax.ppermute(x, 'dev', [(i, i ^ mask) for i in range(devices)])]
    ppermute x63 -> x67, waiting for transfers between devices: 62.9 us -> 61.4 us  [swap(): return lax.ppermute(x, 'dev', [(i, i ^ mask) for i in range(devices)])]
    pallas_call x1 -> x2, Pallas kernels: 5.17 us -> 5.59 us  [on_device(): call(me, w_gate, w_up, w_down, own, *(in_vmem(tokens[p]) for p in spots))]
  transfers between devices with their start and end apart: 63 -> 67, of which waited for: 31 -> 28; matrix products, arithmetic and copies ran while one was open for 1% -> 1% of each run, Pallas kernels for 2% -> 6%
where the time goes in v4:
time: 135 us
  waiting for transfers between devices  61.4 us (45%)
  starting transfers between devices  54.9 us (41%)
  Pallas kernels  16 us (12%)
  other arithmetic  2 us (1%)
    ppermute x67, waiting for transfers between devices, swap(): return lax.ppermute(x, 'dev', [(i, i ^ mask) for i in range(devices)])  61.4 us
    ppermute x67, starting transfers between devices, swap(): return lax.ppermute(x, 'dev', [(i, i ^ mask) for i in range(devices)])  54.9 us
    pallas_call x2, Pallas kernels, on_device(): call(me, w_gate, w_up, w_down, own, *(in_vmem(tokens[p]) for p in spots))  5.59 us
    pallas_call x1, Pallas kernels, on_device(): pl.pallas_call(functools.partial(attend_kernel, devices=devices, row_dev=...  5.35 us
  transfers between devices with their start and end apart: 67, of which 28 were waited for; matrix products, arithmetic and copies ran while one was open for 1% of the time, Pallas kernels for 6%

profile of v4, /device:TPU:0, one launch (start us, length us, event | category | flops | bytes accessed | tf_op | source)
XLA Modules:
  0.0 134.9 jit_solution(435488321133365612)
XLA Ops:
  0.0 1.0 payload.1
  1.0 3.1 %collective-permute-start = (bf16[16,4736]{1,0:T(8,128)(2,1)S(1)}, bf16[16,4736]{1,0:T(8,128)(2,1)S(1)}, u32[]{:S(2)}, u32[]{:S(2)}) collective-permute-start(bf16[16,4736]{1,0:T(8,128)(2,1)S(1)} %get-tuple-element.45), channel_id=1, source_target_pairs={{0,4},{1,5},{2,6},{3,7},{4,0},{5,1},{6,2},{7,3},{8,12},{9,13},{10,... | collective-permute-start | bytes 454664 | tf_op jit(solution)/shard_map/ppermute | solution.py:24
  4.2 2.6 %collective-permute-start.1 = (bf16[16,4736]{1,0:T(8,128)(2,1)S(1)}, bf16[16,4736]{1,0:T(8,128)(2,1)S(1)}, u32[]{:S(2)}, u32[]{:S(2)}) collective-permute-start(bf16[16,4736]{1,0:T(8,128)(2,1)S(1)} %get-tuple-element.45), channel_id=1, source_target_pairs={{0,8},{1,9},{2,10},{3,11},{4,12},{5,13},{6,14},{7,15},{8,0},{9,1},... | collective-permute-start | bytes 454664 | tf_op jit(solution)/shard_map/ppermute | solution.py:24
  6.8 1.7 %collective-permute-start.3 = (bf16[16,4736]{1,0:T(8,128)(2,1)S(1)}, bf16[16,4736]{1,0:T(8,128)(2,1)S(1)}, u32[]{:S(2)}, u32[]{:S(2)}) collective-permute-start(bf16[16,4736]{1,0:T(8,128)(2,1)S(1)} %get-tuple-element.45), channel_id=1, source_target_pairs={{0,2},{1,3},{2,0},{3,1},{4,6},{5,7},{6,4},{7,5},{8,10},{9,11},{10,... | collective-permute-start | bytes 454664 | tf_op jit(solution)/shard_map/ppermute | solution.py:24
  8.5 1.8 %collective-permute-done.x_ref = bf16[16,4736]{1,0:T(8,128)(2,1)S(1)} collective-permute-done((bf16[16,4736]{1,0:T(8,128)(2,1)S(1)}, bf16[16,4736]{1,0:T(8,128)(2,1)S(1)}, u32[]{:S(2)}, u32[]{:S(2)}) %collective-permute-start) | collective-permute-done | bytes 151584 | tf_op jit(solution)/shard_map/ppermute | solution.py:24
  10.3 2.3 %stage.1 = (bf16[16,4736]{1,0:T(8,128)(2,1)S(1)}, bf16[2048,256]{1,0:T(8,128)(2,1)S(1)}, bf16[2048,256]{1,0:T(8,128)(2,1)S(1)}, bf16[256,4096]{1,0:T(8,128)(2,1)S(1)}) custom-call(bf16[16,4736]{1,0:T(8,128)(2,1)S(1)} %collective-permute-done.x_ref, bf16[2048,256]{1,0:T(8,128)(2,1)} %bitcast.60, bf16[2048,256]{1,0:T(8,128)(2,1)} %bitcast.61, ...), custom_call_target="tpu_custom_call" | custom-call | tf_op jit(solution)/shard_map/stage/pallas_call | solution.py:463
  12.5 1.8 %collective-permute-start.4 = (bf16[16,4736]{1,0:T(8,128)(2,1)S(1)}, bf16[16,4736]{1,0:T(8,128)(2,1)S(1)}, u32[]{:S(2)}, u32[]{:S(2)}) collective-permute-start(bf16[16,4736]{1,0:T(8,128)(2,1)S(1)} %get-tuple-element.51.rest_1_), channel_id=1, source_target_pairs={{0,2},{1,3},{2,0},{3,1},{4,6},{5,7},{6,4},{7,5},{8,10},{9,11},{10,... | collective-permute-start | bytes 454664 | tf_op jit(solution)/shard_map/ppermute | solution.py:24
  14.3 4.0 %collective-permute-done.1.rest_2_ = bf16[16,4736]{1,0:T(8,128)(2,1)S(1)} collective-permute-done((bf16[16,4736]{1,0:T(8,128)(2,1)S(1)}, bf16[16,4736]{1,0:T(8,128)(2,1)S(1)}, u32[]{:S(2)}, u32[]{:S(2)}) %collective-permute-start.1) | collective-permute-done | bytes 151584 | tf_op jit(solution)/shard_map/ppermute | solution.py:24
  18.4 1.5 %collective-permute-start.5 = (bf16[16,4736]{1,0:T(8,128)(2,1)S(1)}, bf16[16,4736]{1,0:T(8,128)(2,1)S(1)}, u32[]{:S(2)}, u32[]{:S(2)}) collective-permute-start(bf16[16,4736]{1,0:T(8,128)(2,1)S(1)} %collective-permute-done.1.rest_2_), channel_id=1, source_target_pairs={{0,2},{1,3},{2,0},{3,1},{4,6},{5,7},{6,4},{7,5},{8,10},{9,11},{10,... | collective-permute-start | bytes 454664 | tf_op jit(solution)/shard_map/ppermute | solution.py:24
  19.9 0.5 collective-permute-start.6
  21.0 2.6 %collective-permute-done.5.rest_6_ = bf16[16,4736]{1,0:T(8,128)(2,1)S(1)} collective-permute-done((bf16[16,4736]{1,0:T(8,128)(2,1)S(1)}, bf16[16,4736]{1,0:T(8,128)(2,1)S(1)}, u32[]{:S(2)}, u32[]{:S(2)}) %collective-permute-start.5) | collective-permute-done | bytes 151584 | tf_op jit(solution)/shard_map/ppermute | solution.py:24
  23.6 1.6 %collective-permute-done.6.rest_7_ = bf16[16,4736]{1,0:T(8,128)(2,1)S(1)} collective-permute-done((bf16[16,4736]{1,0:T(8,128)(2,1)S(1)}, bf16[16,4736]{1,0:T(8,128)(2,1)S(1)}, u32[]{:S(2)}, u32[]{:S(2)}) %collective-permute-start.6) | collective-permute-done | bytes 151584 | tf_op jit(solution)/shard_map/ppermute | solution.py:24
  25.2 0.5 collective-permute-start.13
  25.8 0.8 collective-permute-done.12.rest_13_
  27.1 5.4 %attend.1 = (bf16[2,288,256]{2,1,0:T(8,128)(2,1)S(1)}, bf16[2,288,256]{2,1,0:T(8,128)(2,1)S(1)}, bf16[2,288,256]{2,1,0:T(8,128)(2,1)S(1)}, bf16[2,288,256]{2,1,0...) custom-call(s32[1]{0:T(128)} %bitcast.me_ref, ...), custom_call_target="tpu_custom_call" | custom-call | tf_op jit(solution)/shard_map/attend/pallas_call | solution.py:478
  33.5 0.6 collective-permute-done.15
  34.2 1.6 %collective-permute-start.16 = (bf16[288,256]{1,0:T(8,128)(2,1)S(1)}, bf16[288,256]{1,0:T(8,128)(2,1)S(1)}, u32[]{:S(2)}, u32[]{:S(2)}) collective-permute-start(bf16[288,256]{1,0:T(8,128)(2,1)S(1)} %slice_bitcast_fusion.6), channel_id=1, source_target_pairs={{0,2},{1,3},{2,0},{3,1},{4,6},{5,7},{6,4},{7,5},{8,10},{9,11},{10,... | collective-permute-start | bytes 442376 | tf_op jit(solution)/shard_map/ppermute | solution.py:24
  35.9 0.6 collective-permute-start.19
  36.6 1.6 %collective-permute-start.22 = (bf16[288,256]{1,0:T(8,128)(2,1)S(1)}, bf16[288,256]{1,0:T(8,128)(2,1)S(1)}, u32[]{:S(2)}, u32[]{:S(2)}) collective-permute-start(bf16[288,256]{1,0:T(8,128)(2,1)S(1)} %slice_bitcast_fusion.2), channel_id=1, source_target_pairs={{0,2},{1,3},{2,0},{3,1},{4,6},{5,7},{6,4},{7,5},{8,10},{9,11},{10,... | collective-permute-start | bytes 442376 | tf_op jit(solution)/shard_map/ppermute | solution.py:24
  38.3 0.6 collective-permute-start.25
  38.8 2.1 %collective-permute-done.16 = bf16[288,256]{1,0:T(8,128)(2,1)S(1)} collective-permute-done((bf16[288,256]{1,0:T(8,128)(2,1)S(1)}, bf16[288,256]{1,0:T(8,128)(2,1)S(1)}, u32[]{:S(2)}, u32[]{:S(2)}) %collective-permute-start.16) | collective-permute-done | bytes 147488 | tf_op jit(solution)/shard_map/ppermute | solution.py:24
  41.0 2.8 %collective-permute-start.17 = (bf16[288,256]{1,0:T(8,128)(2,1)S(1)}, bf16[288,256]{1,0:T(8,128)(2,1)S(1)}, u32[]{:S(2)}, u32[]{:S(2)}) collective-permute-start(bf16[288,256]{1,0:T(8,128)(2,1)S(1)} %fusion.7), channel_id=1, source_target_pairs={{0,12},{1,13},{2,14},{3,15},{4,8},{5,9},{6,10},{7,11},{8,4},{9,5},... | collective-permute-start | bytes 442376 | tf_op jit(solution)/shard_map/ppermute | solution.py:24
  44.2 1.9 %collective-permute-start.20 = (bf16[288,256]{1,0:T(8,128)(2,1)S(1)}, bf16[288,256]{1,0:T(8,128)(2,1)S(1)}, u32[]{:S(2)}, u32[]{:S(2)}) collective-permute-start(bf16[288,256]{1,0:T(8,128)(2,1)S(1)} %fusion.6), channel_id=1, source_target_pairs={{0,8},{1,9},{2,10},{3,11},{4,12},{5,13},{6,14},{7,15},{8,0},{9,1},... | collective-permute-start | bytes 442376 | tf_op jit(solution)/shard_map/ppermute | solution.py:24
  46.1 1.2 collective-permute-done.22
  47.3 1.2 collective-permute-start.23
  48.5 1.2 collective-permute-done.25
  49.7 5.7 %collective-permute-done.20.rest_1_ = bf16[288,256]{1,0:T(8,128)(2,1)S(1)} collective-permute-done((bf16[288,256]{1,0:T(8,128)(2,1)S(1)}, bf16[288,256]{1,0:T(8,128)(2,1)S(1)}, u32[]{:S(2)}, u32[]{:S(2)}) %collective-permute-start.20) | collective-permute-done | bytes 147488 | tf_op jit(solution)/shard_map/ppermute | solution.py:24
  55.4 1.7 %combine.1 = (bf16[2,16,4096]{2,1,0:T(8,128)(2,1)S(1)}, bf16[2,16,4096]{2,1,0:T(8,128)(2,1)S(1)}, bf16[2,16,4096]{2,1,0:T(8,128)(2,1)S(1)}, bf16[2,16,4096]{2,1,...) custom-call(s32[1]{0:T(128)} %bitcast.me_ref, ...), custom_call_target="tpu_custom_call" | custom-call | tf_op jit(solution)/shard_map/combine/pallas_call | solution.py:501
  58.3 0.5 collective-permute-done.35
  58.9 1.6 %collective-permute-start.36 = (bf16[16,4096]{1,0:T(8,128)(2,1)S(1)}, bf16[16,4096]{1,0:T(8,128)(2,1)S(1)}, u32[]{:S(2)}, u32[]{:S(2)}) collective-permute-start(bf16[16,4096]{1,0:T(8,128)(2,1)S(1)} %slice_bitcast_fusion.8), channel_id=1, source_target_pairs={{0,2},{1,3},{2,0},{3,1},{4,6},{5,7},{6,4},{7,5},{8,10},{9,11},{10,... | collective-permute-start | bytes 393224 | tf_op jit(solution)/shard_map/ppermute | solution.py:24
  60.5 0.6 collective-permute-start.33
  61.2 1.6 %collective-permute-start.30 = (bf16[16,4096]{1,0:T(8,128)(2,1)S(1)}, bf16[16,4096]{1,0:T(8,128)(2,1)S(1)}, u32[]{:S(2)}, u32[]{:S(2)}) collective-permute-start(bf16[16,4096]{1,0:T(8,128)(2,1)S(1)} %slice_bitcast_fusion.12), channel_id=1, source_target_pairs={{0,2},{1,3},{2,0},{3,1},{4,6},{5,7},{6,4},{7,5},{8,10},{9,11},{10,... | collective-permute-start | bytes 393224 | tf_op jit(solution)/shard_map/ppermute | solution.py:24
  62.9 0.6 collective-permute-start.27
  63.4 4.7 %collective-permute-done.33 = bf16[16,4096]{1,0:T(8,128)(2,1)S(1)} collective-permute-done((bf16[16,4096]{1,0:T(8,128)(2,1)S(1)}, bf16[16,4096]{1,0:T(8,128)(2,1)S(1)}, u32[]{:S(2)}, u32[]{:S(2)}) %collective-permute-start.33) | collective-permute-done | bytes 131104 | tf_op jit(solution)/shard_map/ppermute | solution.py:24
  68.2 2.7 %collective-permute-done.30 = bf16[16,4096]{1,0:T(8,128)(2,1)S(1)} collective-permute-done((bf16[16,4096]{1,0:T(8,128)(2,1)S(1)}, bf16[16,4096]{1,0:T(8,128)(2,1)S(1)}, u32[]{:S(2)}, u32[]{:S(2)}) %collective-permute-start.30) | collective-permute-done | bytes 131104 | tf_op jit(solution)/shard_map/ppermute | solution.py:24
  70.9 0.9 collective-permute-start.31
  71.8 1.1 collective-permute-done.27
  72.9 2.7 %collective-permute-start.28 = (bf16[16,4096]{1,0:T(8,128)(2,1)S(1)}, bf16[16,4096]{1,0:T(8,128)(2,1)S(1)}, u32[]{:S(2)}, u32[]{:S(2)}) collective-permute-start(bf16[16,4096]{1,0:T(8,128)(2,1)S(1)} %fusion.11), channel_id=1, source_target_pairs={{0,12},{1,13},{2,14},{3,15},{4,8},{5,9},{6,10},{7,11},{8,4},{9,5},... | collective-permute-start | bytes 393224 | tf_op jit(solution)/shard_map/ppermute | solution.py:24
  75.7 6.7 %collective-permute-done.31 = bf16[16,4096]{1,0:T(8,128)(2,1)S(1)} collective-permute-done((bf16[16,4096]{1,0:T(8,128)(2,1)S(1)}, bf16[16,4096]{1,0:T(8,128)(2,1)S(1)}, u32[]{:S(2)}, u32[]{:S(2)}) %collective-permute-start.31) | collective-permute-done | bytes 131104 | tf_op jit(solution)/shard_map/ppermute | solution.py:24
  82.7 2.5 %collective-permute-start.37 = (bf16[16,4096]{1,0:T(8,128)(2,1)S(1)}, bf16[16,4096]{1,0:T(8,128)(2,1)S(1)}, u32[]{:S(2)}, u32[]{:S(2)}) collective-permute-start(bf16[16,4096]{1,0:T(8,128)(2,1)S(1)} %fusion.2.rest_0_), channel_id=1, source_target_pairs={{0,4},{1,5},{2,6},{3,7},{4,0},{5,1},{6,2},{7,3},{8,12},{9,13},{10,... | collective-permute-start | bytes 393224 | tf_op jit(solution)/shard_map/ppermute | solution.py:24
  85.2 0.6 collective-permute-start.38
  85.8 1.8 %collective-permute-start.39 = (bf16[16,4096]{1,0:T(8,128)(2,1)S(1)}, bf16[16,4096]{1,0:T(8,128)(2,1)S(1)}, u32[]{:S(2)}, u32[]{:S(2)}) collective-permute-start(bf16[16,4096]{1,0:T(8,128)(2,1)S(1)} %fusion.2.rest_0_), channel_id=1, source_target_pairs={{0,12},{1,13},{2,14},{3,15},{4,8},{5,9},{6,10},{7,11},{8,4},{9,5},... | collective-permute-start | bytes 393224 | tf_op jit(solution)/shard_map/ppermute | solution.py:24
  87.6 1.5 %collective-permute-start.45 = (bf16[16,4096]{1,0:T(8,128)(2,1)S(1)}, bf16[16,4096]{1,0:T(8,128)(2,1)S(1)}, u32[]{:S(2)}, u32[]{:S(2)}) collective-permute-start(bf16[16,4096]{1,0:T(8,128)(2,1)S(1)} %fusion.2.rest_0_), channel_id=1, source_target_pairs={{0,2},{1,3},{2,0},{3,1},{4,6},{5,7},{6,4},{7,5},{8,10},{9,11},{10,... | collective-permute-start | bytes 393224 | tf_op jit(solution)/shard_map/ppermute | solution.py:24
  89.2 1.5 %collective-permute-start.46 = (bf16[16,4096]{1,0:T(8,128)(2,1)S(1)}, bf16[16,4096]{1,0:T(8,128)(2,1)S(1)}, u32[]{:S(2)}, u32[]{:S(2)}) collective-permute-start(bf16[16,4096]{1,0:T(8,128)(2,1)S(1)} %collective-permute-done.37.rest_1_), channel_id=1, source_target_pairs={{0,2},{1,3},{2,0},{3,1},{4,6},{5,7},{6,4},{7,5},{8,10},{9,11},{10,... | collective-permute-start | bytes 393224 | tf_op jit(solution)/shard_map/ppermute | solution.py:24
  90.7 6.5 %collective-permute-done.38.rest_2_ = bf16[16,4096]{1,0:T(8,128)(2,1)S(1)} collective-permute-done((bf16[16,4096]{1,0:T(8,128)(2,1)S(1)}, bf16[16,4096]{1,0:T(8,128)(2,1)S(1)}, u32[]{:S(2)}, u32[]{:S(2)}) %collective-permute-start.38) | collective-permute-done | bytes 131104 | tf_op jit(solution)/shard_map/ppermute | solution.py:24
  97.3 1.5 %collective-permute-start.47 = (bf16[16,4096]{1,0:T(8,128)(2,1)S(1)}, bf16[16,4096]{1,0:T(8,128)(2,1)S(1)}, u32[]{:S(2)}, u32[]{:S(2)}) collective-permute-start(bf16[16,4096]{1,0:T(8,128)(2,1)S(1)} %collective-permute-done.38.rest_2_), channel_id=1, source_target_pairs={{0,2},{1,3},{2,0},{3,1},{4,6},{5,7},{6,4},{7,5},{8,10},{9,11},{10,... | collective-permute-start | bytes 393224 | tf_op jit(solution)/shard_map/ppermute | solution.py:24
  98.8 0.5 collective-permute-start.48
  99.8 2.4 %collective-permute-done.47.rest_2_ = bf16[16,4096]{1,0:T(8,128)(2,1)S(1)} collective-permute-done((bf16[16,4096]{1,0:T(8,128)(2,1)S(1)}, bf16[16,4096]{1,0:T(8,128)(2,1)S(1)}, u32[]{:S(2)}, u32[]{:S(2)}) %collective-permute-start.47) | collective-permute-done | bytes 131104 | tf_op jit(solution)/shard_map/ppermute | solution.py:24
  102.2 1.5 %collective-permute-done.48.rest_3_ = bf16[16,4096]{1,0:T(8,128)(2,1)S(1)} collective-permute-done((bf16[16,4096]{1,0:T(8,128)(2,1)S(1)}, bf16[16,4096]{1,0:T(8,128)(2,1)S(1)}, u32[]{:S(2)}, u32[]{:S(2)}) %collective-permute-start.48) | collective-permute-done | bytes 131104 | tf_op jit(solution)/shard_map/ppermute | solution.py:24
  103.7 0.5 collective-permute-start.40
  105.1 2.8 %shard_map.137 = (bf16[16,4096]{1,0:T(8,128)(2,1)S(1)}, bf16[16,4096]{1,0:T(8,128)(2,1)S(1)}, bf16[16,4096]{1,0:T(8,128)(2,1)S(1)}, bf16[16,4096]{1,0:T(8,128)(2...) custom-call(s32[1]{0:T(128)} %bitcast.me_ref, ...), custom_call_target="tpu_custom_call" | custom-call | tf_op jit(solution)/shard_map/pallas_call | solution.py:538
  109.0 2.8 %shard_map.136 = (bf16[16,4096]{1,0:T(8,128)(2,1)S(1)}, bf16[16,4096]{1,0:T(8,128)(2,1)S(1)}, bf16[16,4096]{1,0:T(8,128)(2,1)S(1)}, bf16[16,4096]{1,0:T(8,128)(2...) custom-call(s32[1]{0:T(128)} %bitcast.me_ref, ...), custom_call_target="tpu_custom_call" | custom-call | tf_op jit(solution)/shard_map/pallas_call | solution.py:538
  112.1 1.5 %collective-permute-start.62 = (bf16[16,4096]{1,0:T(8,128)(2,1)S(1)}, bf16[16,4096]{1,0:T(8,128)(2,1)S(1)}, u32[]{:S(2)}, u32[]{:S(2)}) collective-permute-start(bf16[16,4096]{1,0:T(8,128)(2,1)S(1)} %add.145), channel_id=1, source_target_pairs={{0,2},{1,3},{2,0},{3,1},{4,6},{5,7},{6,4},{7,5},{8,10},{9,11},{10,... | collective-permute-start | bytes 393224 | tf_op jit(solution)/shard_map/ppermute | solution.py:24
  113.7 0.6 collective-permute-start.44
  114.4 0.7 collective-permute-start.58
  115.1 3.1 %collective-permute-done.62 = bf16[16,4096]{1,0:T(8,128)(2,1)S(1)} collective-permute-done((bf16[16,4096]{1,0:T(8,128)(2,1)S(1)}, bf16[16,4096]{1,0:T(8,128)(2,1)S(1)}, u32[]{:S(2)}, u32[]{:S(2)}) %collective-permute-start.62) | collective-permute-done | bytes 131104 | tf_op jit(solution)/shard_map/ppermute | solution.py:24
  118.2 1.7 %collective-permute-start.54 = (bf16[16,4096]{1,0:T(8,128)(2,1)S(1)}, bf16[16,4096]{1,0:T(8,128)(2,1)S(1)}, u32[]{:S(2)}, u32[]{:S(2)}) collective-permute-start(bf16[16,4096]{1,0:T(8,128)(2,1)S(1)} %add.138), channel_id=1, source_target_pairs={{0,2},{1,3},{2,0},{3,1},{4,6},{5,7},{6,4},{7,5},{8,10},{9,11},{10,... | collective-permute-start | bytes 393224 | tf_op jit(solution)/shard_map/ppermute | solution.py:24
  120.4 0.7 collective-permute-done.58
  121.5 2.0 %collective-permute-start.59 = (bf16[16,4096]{1,0:T(8,128)(2,1)S(1)}, bf16[16,4096]{1,0:T(8,128)(2,1)S(1)}, u32[]{:S(2)}, u32[]{:S(2)}) collective-permute-start(bf16[16,4096]{1,0:T(8,128)(2,1)S(1)} %add_add_fusion.1), channel_id=1, source_target_pairs={{0,8},{1,9},{2,10},{3,11},{4,12},{5,13},{6,14},{7,15},{8,0},{9,1},... | collective-permute-start | bytes 393224 | tf_op jit(solution)/shard_map/ppermute | solution.py:24
  123.6 1.1 collective-permute-done.54
  124.6 1.9 %collective-permute-start.55 = (bf16[16,4096]{1,0:T(8,128)(2,1)S(1)}, bf16[16,4096]{1,0:T(8,128)(2,1)S(1)}, u32[]{:S(2)}, u32[]{:S(2)}) collective-permute-start(bf16[16,4096]{1,0:T(8,128)(2,1)S(1)} %add_add_fusion.2), channel_id=1, source_target_pairs={{0,12},{1,13},{2,14},{3,15},{4,8},{5,9},{6,10},{7,11},{8,4},{9,5},... | collective-permute-start | bytes 393224 | tf_op jit(solution)/shard_map/ppermute | solution.py:24
  126.6 1.1 collective-permute-done.63
  127.7 6.4 %collective-permute-done.59 = bf16[16,4096]{1,0:T(8,128)(2,1)S(1)} collective-permute-done((bf16[16,4096]{1,0:T(8,128)(2,1)S(1)}, bf16[16,4096]{1,0:T(8,128)(2,1)S(1)}, u32[]{:S(2)}, u32[]{:S(2)}) %collective-permute-start.59) | collective-permute-done | bytes 131104 | tf_op jit(solution)/shard_map/ppermute | solution.py:24
  134.1 0.8 fusion.3
  (124 shorter events, 9.0 us)
Async XLA Ops:
  1.0 9.2 %collective-permute-start = (bf16[16,4736]{1,0:T(8,128)(2,1)S(1)}, bf16[16,4736]{1,0:T(8,128)(2,1)S(1)}, u32[]{:S(2)}, u32[]{:S(2)}) collective-permute-start(bf16[16,4736]{1,0:T(8,128)(2,1)S(1)} %get-tuple-element.45), channel_id=1, source_target_pairs={{0,4},{1,5},{2,6},{3,7},{4,0},{5,1},{6,2},{7,3},{8,12},{9,13},{10,... | collective-permute-start | bytes 454664 | tf_op jit(solution)/shard_map/ppermute | solution.py:24
  4.2 14.2 %collective-permute-start.1 = (bf16[16,4736]{1,0:T(8,128)(2,1)S(1)}, bf16[16,4736]{1,0:T(8,128)(2,1)S(1)}, u32[]{:S(2)}, u32[]{:S(2)}) collective-permute-start(bf16[16,4736]{1,0:T(8,128)(2,1)S(1)} %get-tuple-element.45), channel_id=1, source_target_pairs={{0,8},{1,9},{2,10},{3,11},{4,12},{5,13},{6,14},{7,15},{8,0},{9,1},... | collective-permute-start | bytes 454664 | tf_op jit(solution)/shard_map/ppermute | solution.py:24
  6.7 13.1 %collective-permute-start.2 = (bf16[16,4736]{1,0:T(8,128)(2,1)S(1)}, bf16[16,4736]{1,0:T(8,128)(2,1)S(1)}, u32[]{:S(2)}, u32[]{:S(2)}) collective-permute-start(bf16[16,4736]{1,0:T(8,128)(2,1)S(1)} %get-tuple-element.45), channel_id=1, source_target_pairs={{0,12},{1,13},{2,14},{3,15},{4,8},{5,9},{6,10},{7,11},{8,4},{9,5},... | collective-permute-start | bytes 454664 | tf_op jit(solution)/shard_map/ppermute | solution.py:24
  6.8 13.6 %collective-permute-start.3 = (bf16[16,4736]{1,0:T(8,128)(2,1)S(1)}, bf16[16,4736]{1,0:T(8,128)(2,1)S(1)}, u32[]{:S(2)}, u32[]{:S(2)}) collective-permute-start(bf16[16,4736]{1,0:T(8,128)(2,1)S(1)} %get-tuple-element.45), channel_id=1, source_target_pairs={{0,2},{1,3},{2,0},{3,1},{4,6},{5,7},{6,4},{7,5},{8,10},{9,11},{10,... | collective-permute-start | bytes 454664 | tf_op jit(solution)/shard_map/ppermute | solution.py:24
  8.5 11.9 %collective-permute-start.7 = (bf16[16,4736]{1,0:T(8,128)(2,1)S(1)}, bf16[16,4736]{1,0:T(8,128)(2,1)S(1)}, u32[]{:S(2)}, u32[]{:S(2)}) collective-permute-start(bf16[16,4736]{1,0:T(8,128)(2,1)S(1)} %get-tuple-element.45), channel_id=1, source_target_pairs={{0,1},{1,0},{2,3},{3,2},{4,5},{5,4},{6,7},{7,6},{8,9},{9,8},{10,11... | collective-permute-start | bytes 454664 | tf_op jit(solution)/shard_map/ppermute | solution.py:24
  12.5 8.4 %collective-permute-start.4 = (bf16[16,4736]{1,0:T(8,128)(2,1)S(1)}, bf16[16,4736]{1,0:T(8,128)(2,1)S(1)}, u32[]{:S(2)}, u32[]{:S(2)}) collective-permute-start(bf16[16,4736]{1,0:T(8,128)(2,1)S(1)} %get-tuple-element.51.rest_1_), channel_id=1, source_target_pairs={{0,2},{1,3},{2,0},{3,1},{4,6},{5,7},{6,4},{7,5},{8,10},{9,11},{10,... | collective-permute-start | bytes 454664 | tf_op jit(solution)/shard_map/ppermute | solution.py:24
  18.4 5.2 %collective-permute-start.5 = (bf16[16,4736]{1,0:T(8,128)(2,1)S(1)}, bf16[16,4736]{1,0:T(8,128)(2,1)S(1)}, u32[]{:S(2)}, u32[]{:S(2)}) collective-permute-start(bf16[16,4736]{1,0:T(8,128)(2,1)S(1)} %collective-permute-done.1.rest_2_), channel_id=1, source_target_pairs={{0,2},{1,3},{2,0},{3,1},{4,6},{5,7},{6,4},{7,5},{8,10},{9,11},{10,... | collective-permute-start | bytes 454664 | tf_op jit(solution)/shard_map/ppermute | solution.py:24
  19.9 5.3 %collective-permute-start.6 = (bf16[16,4736]{1,0:T(8,128)(2,1)S(1)}, bf16[16,4736]{1,0:T(8,128)(2,1)S(1)}, u32[]{:S(2)}, u32[]{:S(2)}) collective-permute-start(bf16[16,4736]{1,0:T(8,128)(2,1)S(1)} %collective-permute-done.2.rest_3_), channel_id=1, source_target_pairs={{0,2},{1,3},{2,0},{3,1},{4,6},{5,7},{6,4},{7,5},{8,10},{9,11},{10,... | collective-permute-start | bytes 454664 | tf_op jit(solution)/shard_map/ppermute | solution.py:24
  20.4 4.8 %collective-permute-start.8 = (bf16[16,4736]{1,0:T(8,128)(2,1)S(1)}, bf16[16,4736]{1,0:T(8,128)(2,1)S(1)}, u32[]{:S(2)}, u32[]{:S(2)}) collective-permute-start(bf16[16,4736]{1,0:T(8,128)(2,1)S(1)} %get-tuple-element.51.rest_1_), channel_id=1, source_target_pairs={{0,1},{1,0},{2,3},{3,2},{4,5},{5,4},{6,7},{7,6},{8,9},{9,8},{10,11... | collective-permute-start | bytes 454664 | tf_op jit(solution)/shard_map/ppermute | solution.py:24
  20.4 5.3 %collective-permute-start.9 = (bf16[16,4736]{1,0:T(8,128)(2,1)S(1)}, bf16[16,4736]{1,0:T(8,128)(2,1)S(1)}, u32[]{:S(2)}, u32[]{:S(2)}) collective-permute-start(bf16[16,4736]{1,0:T(8,128)(2,1)S(1)} %collective-permute-done.1.rest_2_), channel_id=1, source_target_pairs={{0,1},{1,0},{2,3},{3,2},{4,5},{5,4},{6,7},{7,6},{8,9},{9,8},{10,11... | collective-permute-start | bytes 454664 | tf_op jit(solution)/shard_map/ppermute | solution.py:24
  20.9 4.9 %collective-permute-start.10 = (bf16[16,4736]{1,0:T(8,128)(2,1)S(1)}, bf16[16,4736]{1,0:T(8,128)(2,1)S(1)}, u32[]{:S(2)}, u32[]{:S(2)}) collective-permute-start(bf16[16,4736]{1,0:T(8,128)(2,1)S(1)} %collective-permute-done.2.rest_3_), channel_id=1, source_target_pairs={{0,1},{1,0},{2,3},{3,2},{4,5},{5,4},{6,7},{7,6},{8,9},{9,8},{10,11... | collective-permute-start | bytes 454664 | tf_op jit(solution)/shard_map/ppermute | solution.py:24
  23.6 2.2 %collective-permute-start.11 = (bf16[16,4736]{1,0:T(8,128)(2,1)S(1)}, bf16[16,4736]{1,0:T(8,128)(2,1)S(1)}, u32[]{:S(2)}, u32[]{:S(2)}) collective-permute-start(bf16[16,4736]{1,0:T(8,128)(2,1)S(1)} %collective-permute-done.3.rest_4_), channel_id=1, source_target_pairs={{0,1},{1,0},{2,3},{3,2},{4,5},{5,4},{6,7},{7,6},{8,9},{9,8},{10,11... | collective-permute-start | bytes 454664 | tf_op jit(solution)/shard_map/ppermute | solution.py:24
  25.2 1.6 %collective-permute-start.13 = (bf16[16,4736]{1,0:T(8,128)(2,1)S(1)}, bf16[16,4736]{1,0:T(8,128)(2,1)S(1)}, u32[]{:S(2)}, u32[]{:S(2)}) collective-permute-start(bf16[16,4736]{1,0:T(8,128)(2,1)S(1)} %collective-permute-done.5.rest_6_), channel_id=1, source_target_pairs={{0,1},{1,0},{2,3},{3,2},{4,5},{5,4},{6,7},{7,6},{8,9},{9,8},{10,11... | collective-permute-start | bytes 454664 | tf_op jit(solution)/shard_map/ppermute | solution.py:24
  32.4 1.6 %collective-permute-start.15 = (bf16[2,288,256]{2,1,0:T(8,128)(2,1)S(1)}, bf16[2,288,256]{2,1,0:T(8,128)(2,1)S(1)}, u32[]{:S(2)}, u32[]{:S(2)}) collective-permute-start(bf16[2,288,256]{2,1,0:T(8,128)(2,1)S(1)} %get-tuple-element.54), channel_id=1, source_target_pairs={{0,1},{1,0},{2,3},{3,2},{4,5},{5,4},{6,7},{7,6},{8,9},{9,8},{10,11... | collective-permute-start | bytes 884744 | tf_op jit(solution)/shard_map/ppermute | solution.py:24
  32.7 3.1 %collective-permute-start.18 = (bf16[2,288,256]{2,1,0:T(8,128)(2,1)S(1)}, bf16[2,288,256]{2,1,0:T(8,128)(2,1)S(1)}, u32[]{:S(2)}, u32[]{:S(2)}) collective-permute-start(bf16[2,288,256]{2,1,0:T(8,128)(2,1)S(1)} %get-tuple-element.56), channel_id=1, source_target_pairs={{0,1},{1,0},{2,3},{3,2},{4,5},{5,4},{6,7},{7,6},{8,9},{9,8},{10,11... | collective-permute-start | bytes 884744 | tf_op jit(solution)/shard_map/ppermute | solution.py:24
  33.0 3.5 %collective-permute-start.21 = (bf16[2,288,256]{2,1,0:T(8,128)(2,1)S(1)}, bf16[2,288,256]{2,1,0:T(8,128)(2,1)S(1)}, u32[]{:S(2)}, u32[]{:S(2)}) collective-permute-start(bf16[2,288,256]{2,1,0:T(8,128)(2,1)S(1)} %get-tuple-element.58), channel_id=1, source_target_pairs={{0,1},{1,0},{2,3},{3,2},{4,5},{5,4},{6,7},{7,6},{8,9},{9,8},{10,11... | collective-permute-start | bytes 884744 | tf_op jit(solution)/shard_map/ppermute | solution.py:24
  33.2 4.9 %collective-permute-start.24 = (bf16[2,288,256]{2,1,0:T(8,128)(2,1)S(1)}, bf16[2,288,256]{2,1,0:T(8,128)(2,1)S(1)}, u32[]{:S(2)}, u32[]{:S(2)}) collective-permute-start(bf16[2,288,256]{2,1,0:T(8,128)(2,1)S(1)} %get-tuple-element.60), channel_id=1, source_target_pairs={{0,1},{1,0},{2,3},{3,2},{4,5},{5,4},{6,7},{7,6},{8,9},{9,8},{10,11... | collective-permute-start | bytes 884744 | tf_op jit(solution)/shard_map/ppermute | solution.py:24
  34.2 6.8 %collective-permute-start.16 = (bf16[288,256]{1,0:T(8,128)(2,1)S(1)}, bf16[288,256]{1,0:T(8,128)(2,1)S(1)}, u32[]{:S(2)}, u32[]{:S(2)}) collective-permute-start(bf16[288,256]{1,0:T(8,128)(2,1)S(1)} %slice_bitcast_fusion.6), channel_id=1, source_target_pairs={{0,2},{1,3},{2,0},{3,1},{4,6},{5,7},{6,4},{7,5},{8,10},{9,11},{10,... | collective-permute-start | bytes 442376 | tf_op jit(solution)/shard_map/ppermute | solution.py:24
  35.9 8.2 %collective-permute-start.19 = (bf16[288,256]{1,0:T(8,128)(2,1)S(1)}, bf16[288,256]{1,0:T(8,128)(2,1)S(1)}, u32[]{:S(2)}, u32[]{:S(2)}) collective-permute-start(bf16[288,256]{1,0:T(8,128)(2,1)S(1)} %slice_bitcast_fusion.4), channel_id=1, source_target_pairs={{0,2},{1,3},{2,0},{3,1},{4,6},{5,7},{6,4},{7,5},{8,10},{9,11},{10,... | collective-permute-start | bytes 442376 | tf_op jit(solution)/shard_map/ppermute | solution.py:24
  36.6 10.7 %collective-permute-start.22 = (bf16[288,256]{1,0:T(8,128)(2,1)S(1)}, bf16[288,256]{1,0:T(8,128)(2,1)S(1)}, u32[]{:S(2)}, u32[]{:S(2)}) collective-permute-start(bf16[288,256]{1,0:T(8,128)(2,1)S(1)} %slice_bitcast_fusion.2), channel_id=1, source_target_pairs={{0,2},{1,3},{2,0},{3,1},{4,6},{5,7},{6,4},{7,5},{8,10},{9,11},{10,... | collective-permute-start | bytes 442376 | tf_op jit(solution)/shard_map/ppermute | solution.py:24
  38.3 11.4 %collective-permute-start.25 = (bf16[288,256]{1,0:T(8,128)(2,1)S(1)}, bf16[288,256]{1,0:T(8,128)(2,1)S(1)}, u32[]{:S(2)}, u32[]{:S(2)}) collective-permute-start(bf16[288,256]{1,0:T(8,128)(2,1)S(1)} %slice_bitcast_fusion), channel_id=1, source_target_pairs={{0,2},{1,3},{2,0},{3,1},{4,6},{5,7},{6,4},{7,5},{8,10},{9,11},{10,... | collective-permute-start | bytes 442376 | tf_op jit(solution)/shard_map/ppermute | solution.py:24
  41.0 8.7 %collective-permute-start.17 = (bf16[288,256]{1,0:T(8,128)(2,1)S(1)}, bf16[288,256]{1,0:T(8,128)(2,1)S(1)}, u32[]{:S(2)}, u32[]{:S(2)}) collective-permute-start(bf16[288,256]{1,0:T(8,128)(2,1)S(1)} %fusion.7), channel_id=1, source_target_pairs={{0,12},{1,13},{2,14},{3,15},{4,8},{5,9},{6,10},{7,11},{8,4},{9,5},... | collective-permute-start | bytes 442376 | tf_op jit(solution)/shard_map/ppermute | solution.py:24
  44.2 11.3 %collective-permute-start.20 = (bf16[288,256]{1,0:T(8,128)(2,1)S(1)}, bf16[288,256]{1,0:T(8,128)(2,1)S(1)}, u32[]{:S(2)}, u32[]{:S(2)}) collective-permute-start(bf16[288,256]{1,0:T(8,128)(2,1)S(1)} %fusion.6), channel_id=1, source_target_pairs={{0,8},{1,9},{2,10},{3,11},{4,12},{5,13},{6,14},{7,15},{8,0},{9,1},... | collective-permute-start | bytes 442376 | tf_op jit(solution)/shard_map/ppermute | solution.py:24
  47.3 8.1 %collective-permute-start.23 = (bf16[288,256]{1,0:T(8,128)(2,1)S(1)}, bf16[288,256]{1,0:T(8,128)(2,1)S(1)}, u32[]{:S(2)}, u32[]{:S(2)}) collective-permute-start(bf16[288,256]{1,0:T(8,128)(2,1)S(1)} %fusion.5), channel_id=1, source_target_pairs={{0,4},{1,5},{2,6},{3,7},{4,0},{5,1},{6,2},{7,3},{8,12},{9,13},{10,... | collective-permute-start | bytes 442376 | tf_op jit(solution)/shard_map/ppermute | solution.py:24
  57.2 1.6 %collective-permute-start.35 = (bf16[2,16,4096]{2,1,0:T(8,128)(2,1)S(1)}, bf16[2,16,4096]{2,1,0:T(8,128)(2,1)S(1)}, u32[]{:S(2)}, u32[]{:S(2)}) collective-permute-start(bf16[2,16,4096]{2,1,0:T(8,128)(2,1)S(1)} %get-tuple-element.68), channel_id=1, source_target_pairs={{0,1},{1,0},{2,3},{3,2},{4,5},{5,4},{6,7},{7,6},{8,9},{9,8},{10,11... | collective-permute-start | bytes 786440 | tf_op jit(solution)/shard_map/ppermute | solution.py:24
  57.3 3.2 %collective-permute-start.32 = (bf16[2,16,4096]{2,1,0:T(8,128)(2,1)S(1)}, bf16[2,16,4096]{2,1,0:T(8,128)(2,1)S(1)}, u32[]{:S(2)}, u32[]{:S(2)}) collective-permute-start(bf16[2,16,4096]{2,1,0:T(8,128)(2,1)S(1)} %get-tuple-element.66), channel_id=1, source_target_pairs={{0,1},{1,0},{2,3},{3,2},{4,5},{5,4},{6,7},{7,6},{8,9},{9,8},{10,11... | collective-permute-start | bytes 786440 | tf_op jit(solution)/shard_map/ppermute | solution.py:24
  57.8 3.4 %collective-permute-start.29 = (bf16[2,16,4096]{2,1,0:T(8,128)(2,1)S(1)}, bf16[2,16,4096]{2,1,0:T(8,128)(2,1)S(1)}, u32[]{:S(2)}, u32[]{:S(2)}) collective-permute-start(bf16[2,16,4096]{2,1,0:T(8,128)(2,1)S(1)} %get-tuple-element.64), channel_id=1, source_target_pairs={{0,1},{1,0},{2,3},{3,2},{4,5},{5,4},{6,7},{7,6},{8,9},{9,8},{10,11... | collective-permute-start | bytes 786440 | tf_op jit(solution)/shard_map/ppermute | solution.py:24
  57.8 4.9 %collective-permute-start.26 = (bf16[2,16,4096]{2,1,0:T(8,128)(2,1)S(1)}, bf16[2,16,4096]{2,1,0:T(8,128)(2,1)S(1)}, u32[]{:S(2)}, u32[]{:S(2)}) collective-permute-start(bf16[2,16,4096]{2,1,0:T(8,128)(2,1)S(1)} %get-tuple-element.62), channel_id=1, source_target_pairs={{0,1},{1,0},{2,3},{3,2},{4,5},{5,4},{6,7},{7,6},{8,9},{9,8},{10,11... | collective-permute-start | bytes 786440 | tf_op jit(solution)/shard_map/ppermute | solution.py:24
  58.9 16.8 %collective-permute-start.36 = (bf16[16,4096]{1,0:T(8,128)(2,1)S(1)}, bf16[16,4096]{1,0:T(8,128)(2,1)S(1)}, u32[]{:S(2)}, u32[]{:S(2)}) collective-permute-start(bf16[16,4096]{1,0:T(8,128)(2,1)S(1)} %slice_bitcast_fusion.8), channel_id=1, source_target_pairs={{0,2},{1,3},{2,0},{3,1},{4,6},{5,7},{6,4},{7,5},{8,10},{9,11},{10,... | collective-permute-start | bytes 393224 | tf_op jit(solution)/shard_map/ppermute | solution.py:24
  60.5 7.6 %collective-permute-start.33 = (bf16[16,4096]{1,0:T(8,128)(2,1)S(1)}, bf16[16,4096]{1,0:T(8,128)(2,1)S(1)}, u32[]{:S(2)}, u32[]{:S(2)}) collective-permute-start(bf16[16,4096]{1,0:T(8,128)(2,1)S(1)} %slice_bitcast_fusion.10), channel_id=1, source_target_pairs={{0,2},{1,3},{2,0},{3,1},{4,6},{5,7},{6,4},{7,5},{8,10},{9,11},{10,... | collective-permute-start | bytes 393224 | tf_op jit(solution)/shard_map/ppermute | solution.py:24
  61.2 9.7 %collective-permute-start.30 = (bf16[16,4096]{1,0:T(8,128)(2,1)S(1)}, bf16[16,4096]{1,0:T(8,128)(2,1)S(1)}, u32[]{:S(2)}, u32[]{:S(2)}) collective-permute-start(bf16[16,4096]{1,0:T(8,128)(2,1)S(1)} %slice_bitcast_fusion.12), channel_id=1, source_target_pairs={{0,2},{1,3},{2,0},{3,1},{4,6},{5,7},{6,4},{7,5},{8,10},{9,11},{10,... | collective-permute-start | bytes 393224 | tf_op jit(solution)/shard_map/ppermute | solution.py:24
  62.9 10.0 %collective-permute-start.27 = (bf16[16,4096]{1,0:T(8,128)(2,1)S(1)}, bf16[16,4096]{1,0:T(8,128)(2,1)S(1)}, u32[]{:S(2)}, u32[]{:S(2)}) collective-permute-start(bf16[16,4096]{1,0:T(8,128)(2,1)S(1)} %slice_bitcast_fusion.14), channel_id=1, source_target_pairs={{0,2},{1,3},{2,0},{3,1},{4,6},{5,7},{6,4},{7,5},{8,10},{9,11},{10,... | collective-permute-start | bytes 393224 | tf_op jit(solution)/shard_map/ppermute | solution.py:24
  68.1 7.6 %collective-permute-start.34 = (bf16[16,4096]{1,0:T(8,128)(2,1)S(1)}, bf16[16,4096]{1,0:T(8,128)(2,1)S(1)}, u32[]{:S(2)}, u32[]{:S(2)}) collective-permute-start(bf16[16,4096]{1,0:T(8,128)(2,1)S(1)} %fusion.9), channel_id=1, source_target_pairs={{0,4},{1,5},{2,6},{3,7},{4,0},{5,1},{6,2},{7,3},{8,12},{9,13},{10,... | collective-permute-start | bytes 393224 | tf_op jit(solution)/shard_map/ppermute | solution.py:24
  70.9 11.4 %collective-permute-start.31 = (bf16[16,4096]{1,0:T(8,128)(2,1)S(1)}, bf16[16,4096]{1,0:T(8,128)(2,1)S(1)}, u32[]{:S(2)}, u32[]{:S(2)}) collective-permute-start(bf16[16,4096]{1,0:T(8,128)(2,1)S(1)} %fusion.10), channel_id=1, source_target_pairs={{0,8},{1,9},{2,10},{3,11},{4,12},{5,13},{6,14},{7,15},{8,0},{9,1},... | collective-permute-start | bytes 393224 | tf_op jit(solution)/shard_map/ppermute | solution.py:24
  72.9 9.4 %collective-permute-start.28 = (bf16[16,4096]{1,0:T(8,128)(2,1)S(1)}, bf16[16,4096]{1,0:T(8,128)(2,1)S(1)}, u32[]{:S(2)}, u32[]{:S(2)}) collective-permute-start(bf16[16,4096]{1,0:T(8,128)(2,1)S(1)} %fusion.11), channel_id=1, source_target_pairs={{0,12},{1,13},{2,14},{3,15},{4,8},{5,9},{6,10},{7,11},{8,4},{9,5},... | collective-permute-start | bytes 393224 | tf_op jit(solution)/shard_map/ppermute | solution.py:24
  82.7 6.5 %collective-permute-start.37 = (bf16[16,4096]{1,0:T(8,128)(2,1)S(1)}, bf16[16,4096]{1,0:T(8,128)(2,1)S(1)}, u32[]{:S(2)}, u32[]{:S(2)}) collective-permute-start(bf16[16,4096]{1,0:T(8,128)(2,1)S(1)} %fusion.2.rest_0_), channel_id=1, source_target_pairs={{0,4},{1,5},{2,6},{3,7},{4,0},{5,1},{6,2},{7,3},{8,12},{9,13},{10,... | collective-permute-start | bytes 393224 | tf_op jit(solution)/shard_map/ppermute | solution.py:24
  85.2 12.1 %collective-permute-start.38 = (bf16[16,4096]{1,0:T(8,128)(2,1)S(1)}, bf16[16,4096]{1,0:T(8,128)(2,1)S(1)}, u32[]{:S(2)}, u32[]{:S(2)}) collective-permute-start(bf16[16,4096]{1,0:T(8,128)(2,1)S(1)} %fusion.2.rest_0_), channel_id=1, source_target_pairs={{0,8},{1,9},{2,10},{3,11},{4,12},{5,13},{6,14},{7,15},{8,0},{9,1},... | collective-permute-start | bytes 393224 | tf_op jit(solution)/shard_map/ppermute | solution.py:24
  85.8 13.0 %collective-permute-start.39 = (bf16[16,4096]{1,0:T(8,128)(2,1)S(1)}, bf16[16,4096]{1,0:T(8,128)(2,1)S(1)}, u32[]{:S(2)}, u32[]{:S(2)}) collective-permute-start(bf16[16,4096]{1,0:T(8,128)(2,1)S(1)} %fusion.2.rest_0_), channel_id=1, source_target_pairs={{0,12},{1,13},{2,14},{3,15},{4,8},{5,9},{6,10},{7,11},{8,4},{9,5},... | collective-permute-start | bytes 393224 | tf_op jit(solution)/shard_map/ppermute | solution.py:24
  87.6 11.7 %collective-permute-start.45 = (bf16[16,4096]{1,0:T(8,128)(2,1)S(1)}, bf16[16,4096]{1,0:T(8,128)(2,1)S(1)}, u32[]{:S(2)}, u32[]{:S(2)}) collective-permute-start(bf16[16,4096]{1,0:T(8,128)(2,1)S(1)} %fusion.2.rest_0_), channel_id=1, source_target_pairs={{0,2},{1,3},{2,0},{3,1},{4,6},{5,7},{6,4},{7,5},{8,10},{9,11},{10,... | collective-permute-start | bytes 393224 | tf_op jit(solution)/shard_map/ppermute | solution.py:24
  89.2 10.1 %collective-permute-start.46 = (bf16[16,4096]{1,0:T(8,128)(2,1)S(1)}, bf16[16,4096]{1,0:T(8,128)(2,1)S(1)}, u32[]{:S(2)}, u32[]{:S(2)}) collective-permute-start(bf16[16,4096]{1,0:T(8,128)(2,1)S(1)} %collective-permute-done.37.rest_1_), channel_id=1, source_target_pairs={{0,2},{1,3},{2,0},{3,1},{4,6},{5,7},{6,4},{7,5},{8,10},{9,11},{10,... | collective-permute-start | bytes 393224 | tf_op jit(solution)/shard_map/ppermute | solution.py:24
  97.3 5.0 %collective-permute-start.47 = (bf16[16,4096]{1,0:T(8,128)(2,1)S(1)}, bf16[16,4096]{1,0:T(8,128)(2,1)S(1)}, u32[]{:S(2)}, u32[]{:S(2)}) collective-permute-start(bf16[16,4096]{1,0:T(8,128)(2,1)S(1)} %collective-permute-done.38.rest_2_), channel_id=1, source_target_pairs={{0,2},{1,3},{2,0},{3,1},{4,6},{5,7},{6,4},{7,5},{8,10},{9,11},{10,... | collective-permute-start | bytes 393224 | tf_op jit(solution)/shard_map/ppermute | solution.py:24
  98.8 5.0 %collective-permute-start.48 = (bf16[16,4096]{1,0:T(8,128)(2,1)S(1)}, bf16[16,4096]{1,0:T(8,128)(2,1)S(1)}, u32[]{:S(2)}, u32[]{:S(2)}) collective-permute-start(bf16[16,4096]{1,0:T(8,128)(2,1)S(1)} %collective-permute-done.39.rest_3_), channel_id=1, source_target_pairs={{0,2},{1,3},{2,0},{3,1},{4,6},{5,7},{6,4},{7,5},{8,10},{9,11},{10,... | collective-permute-start | bytes 393224 | tf_op jit(solution)/shard_map/ppermute | solution.py:24
  99.3 5.0 %collective-permute-start.49 = (bf16[16,4096]{1,0:T(8,128)(2,1)S(1)}, bf16[16,4096]{1,0:T(8,128)(2,1)S(1)}, u32[]{:S(2)}, u32[]{:S(2)}) collective-permute-start(bf16[16,4096]{1,0:T(8,128)(2,1)S(1)} %collective-permute-done.45.rest_0_), channel_id=1, source_target_pairs={{0,1},{1,0},{2,3},{3,2},{4,5},{5,4},{6,7},{7,6},{8,9},{9,8},{10,11... | collective-permute-start | bytes 393224 | tf_op jit(solution)/shard_map/ppermute | solution.py:24
  99.3 5.0 %collective-permute-start.50 = (bf16[16,4096]{1,0:T(8,128)(2,1)S(1)}, bf16[16,4096]{1,0:T(8,128)(2,1)S(1)}, u32[]{:S(2)}, u32[]{:S(2)}) collective-permute-start(bf16[16,4096]{1,0:T(8,128)(2,1)S(1)} %collective-permute-done.46.rest_1_), channel_id=1, source_target_pairs={{0,1},{1,0},{2,3},{3,2},{4,5},{5,4},{6,7},{7,6},{8,9},{9,8},{10,11... | collective-permute-start | bytes 393224 | tf_op jit(solution)/shard_map/ppermute | solution.py:24
  102.2 2.5 %collective-permute-start.51 = (bf16[16,4096]{1,0:T(8,128)(2,1)S(1)}, bf16[16,4096]{1,0:T(8,128)(2,1)S(1)}, u32[]{:S(2)}, u32[]{:S(2)}) collective-permute-start(bf16[16,4096]{1,0:T(8,128)(2,1)S(1)} %collective-permute-done.47.rest_2_), channel_id=1, source_target_pairs={{0,1},{1,0},{2,3},{3,2},{4,5},{5,4},{6,7},{7,6},{8,9},{9,8},{10,11... | collective-permute-start | bytes 393224 | tf_op jit(solution)/shard_map/ppermute | solution.py:24
  103.7 4.5 %collective-permute-start.40 = (bf16[16,4096]{1,0:T(8,128)(2,1)S(1)}, bf16[16,4096]{1,0:T(8,128)(2,1)S(1)}, u32[]{:S(2)}, u32[]{:S(2)}) collective-permute-start(bf16[16,4096]{1,0:T(8,128)(2,1)S(1)} %fusion.2.rest_0_), channel_id=1, source_target_pairs={{0,1},{1,0},{2,3},{3,2},{4,5},{5,4},{6,7},{7,6},{8,9},{9,8},{10,11... | collective-permute-start | bytes 393224 | tf_op jit(solution)/shard_map/ppermute | solution.py:24
  104.2 4.3 %collective-permute-start.41 = (bf16[16,4096]{1,0:T(8,128)(2,1)S(1)}, bf16[16,4096]{1,0:T(8,128)(2,1)S(1)}, u32[]{:S(2)}, u32[]{:S(2)}) collective-permute-start(bf16[16,4096]{1,0:T(8,128)(2,1)S(1)} %collective-permute-done.37.rest_1_), channel_id=1, source_target_pairs={{0,1},{1,0},{2,3},{3,2},{4,5},{5,4},{6,7},{7,6},{8,9},{9,8},{10,11... | collective-permute-start | bytes 393224 | tf_op jit(solution)/shard_map/ppermute | solution.py:24
  104.3 4.5 %collective-permute-start.42 = (bf16[16,4096]{1,0:T(8,128)(2,1)S(1)}, bf16[16,4096]{1,0:T(8,128)(2,1)S(1)}, u32[]{:S(2)}, u32[]{:S(2)}) collective-permute-start(bf16[16,4096]{1,0:T(8,128)(2,1)S(1)} %collective-permute-done.38.rest_2_), channel_id=1, source_target_pairs={{0,1},{1,0},{2,3},{3,2},{4,5},{5,4},{6,7},{7,6},{8,9},{9,8},{10,11... | collective-permute-start | bytes 393224 | tf_op jit(solution)/shard_map/ppermute | solution.py:24
  104.8 4.3 %collective-permute-start.43 = (bf16[16,4096]{1,0:T(8,128)(2,1)S(1)}, bf16[16,4096]{1,0:T(8,128)(2,1)S(1)}, u32[]{:S(2)}, u32[]{:S(2)}) collective-permute-start(bf16[16,4096]{1,0:T(8,128)(2,1)S(1)} %collective-permute-done.39.rest_3_), channel_id=1, source_target_pairs={{0,1},{1,0},{2,3},{3,2},{4,5},{5,4},{6,7},{7,6},{8,9},{9,8},{10,11... | collective-permute-start | bytes 393224 | tf_op jit(solution)/shard_map/ppermute | solution.py:24
  107.9 4.2 %collective-permute-start.61 = (bf16[16,4096]{1,0:T(8,128)(2,1)S(1)}, bf16[16,4096]{1,0:T(8,128)(2,1)S(1)}, u32[]{:S(2)}, u32[]{:S(2)}) collective-permute-start(bf16[16,4096]{1,0:T(8,128)(2,1)S(1)} %get-tuple-element.80), channel_id=1, source_target_pairs={{0,1},{1,0},{2,3},{3,2},{4,5},{5,4},{6,7},{7,6},{8,9},{9,8},{10,11... | collective-permute-start | bytes 393224 | tf_op jit(solution)/shard_map/ppermute | solution.py:24
  108.2 5.4 %collective-permute-start.57 = (bf16[16,4096]{1,0:T(8,128)(2,1)S(1)}, bf16[16,4096]{1,0:T(8,128)(2,1)S(1)}, u32[]{:S(2)}, u32[]{:S(2)}) collective-permute-start(bf16[16,4096]{1,0:T(8,128)(2,1)S(1)} %get-tuple-element.76), channel_id=1, source_target_pairs={{0,1},{1,0},{2,3},{3,2},{4,5},{5,4},{6,7},{7,6},{8,9},{9,8},{10,11... | collective-permute-start | bytes 393224 | tf_op jit(solution)/shard_map/ppermute | solution.py:24
  108.5 5.2 %collective-permute-start.53 = (bf16[16,4096]{1,0:T(8,128)(2,1)S(1)}, bf16[16,4096]{1,0:T(8,128)(2,1)S(1)}, u32[]{:S(2)}, u32[]{:S(2)}) collective-permute-start(bf16[16,4096]{1,0:T(8,128)(2,1)S(1)} %get-tuple-element.72), channel_id=1, source_target_pairs={{0,1},{1,0},{2,3},{3,2},{4,5},{5,4},{6,7},{7,6},{8,9},{9,8},{10,11... | collective-permute-start | bytes 393224 | tf_op jit(solution)/shard_map/ppermute | solution.py:24
  108.7 5.5 %collective-permute-start.65 = (bf16[16,4096]{1,0:T(8,128)(2,1)S(1)}, bf16[16,4096]{1,0:T(8,128)(2,1)S(1)}, u32[]{:S(2)}, u32[]{:S(2)}) collective-permute-start(bf16[16,4096]{1,0:T(8,128)(2,1)S(1)} %get-tuple-element.84), channel_id=1, source_target_pairs={{0,1},{1,0},{2,3},{3,2},{4,5},{5,4},{6,7},{7,6},{8,9},{9,8},{10,11... | collective-permute-start | bytes 393224 | tf_op jit(solution)/shard_map/ppermute | solution.py:24
  111.8 2.6 %collective-permute-start.60 = (bf16[16,4096]{1,0:T(8,128)(2,1)S(1)}, bf16[16,4096]{1,0:T(8,128)(2,1)S(1)}, u32[]{:S(2)}, u32[]{:S(2)}) collective-permute-start(bf16[16,4096]{1,0:T(8,128)(2,1)S(1)} %get-tuple-element.78), channel_id=1, source_target_pairs={{0,1},{1,0},{2,3},{3,2},{4,5},{5,4},{6,7},{7,6},{8,9},{9,8},{10,11... | collective-permute-start | bytes 393224 | tf_op jit(solution)/shard_map/ppermute | solution.py:24
  112.1 6.1 %collective-permute-start.62 = (bf16[16,4096]{1,0:T(8,128)(2,1)S(1)}, bf16[16,4096]{1,0:T(8,128)(2,1)S(1)}, u32[]{:S(2)}, u32[]{:S(2)}) collective-permute-start(bf16[16,4096]{1,0:T(8,128)(2,1)S(1)} %add.145), channel_id=1, source_target_pairs={{0,2},{1,3},{2,0},{3,1},{4,6},{5,7},{6,4},{7,5},{8,10},{9,11},{10,... | collective-permute-start | bytes 393224 | tf_op jit(solution)/shard_map/ppermute | solution.py:24
  113.6 6.4 %collective-permute-start.56 = (bf16[16,4096]{1,0:T(8,128)(2,1)S(1)}, bf16[16,4096]{1,0:T(8,128)(2,1)S(1)}, u32[]{:S(2)}, u32[]{:S(2)}) collective-permute-start(bf16[16,4096]{1,0:T(8,128)(2,1)S(1)} %get-tuple-element.74), channel_id=1, source_target_pairs={{0,1},{1,0},{2,3},{3,2},{4,5},{5,4},{6,7},{7,6},{8,9},{9,8},{10,11... | collective-permute-start | bytes 393224 | tf_op jit(solution)/shard_map/ppermute | solution.py:24
  113.7 7.9 %collective-permute-start.44 = (bf16[16,4096]{1,0:T(8,128)(2,1)S(1)}, bf16[16,4096]{1,0:T(8,128)(2,1)S(1)}, u32[]{:S(2)}, u32[]{:S(2)}) collective-permute-start(bf16[16,4096]{1,0:T(8,128)(2,1)S(1)} %get-tuple-element.70), channel_id=1, source_target_pairs={{0,1},{1,0},{2,3},{3,2},{4,5},{5,4},{6,7},{7,6},{8,9},{9,8},{10,11... | collective-permute-start | bytes 393224 | tf_op jit(solution)/shard_map/ppermute | solution.py:24
  114.3 12.3 %collective-permute-start.64 = (bf16[16,4096]{1,0:T(8,128)(2,1)S(1)}, bf16[16,4096]{1,0:T(8,128)(2,1)S(1)}, u32[]{:S(2)}, u32[]{:S(2)}) collective-permute-start(bf16[16,4096]{1,0:T(8,128)(2,1)S(1)} %get-tuple-element.82), channel_id=1, source_target_pairs={{0,1},{1,0},{2,3},{3,2},{4,5},{5,4},{6,7},{7,6},{8,9},{9,8},{10,11... | collective-permute-start | bytes 393224 | tf_op jit(solution)/shard_map/ppermute | solution.py:24
  114.4 6.6 %collective-permute-start.58 = (bf16[16,4096]{1,0:T(8,128)(2,1)S(1)}, bf16[16,4096]{1,0:T(8,128)(2,1)S(1)}, u32[]{:S(2)}, u32[]{:S(2)}) collective-permute-start(bf16[16,4096]{1,0:T(8,128)(2,1)S(1)} %add.141), channel_id=1, source_target_pairs={{0,2},{1,3},{2,0},{3,1},{4,6},{5,7},{6,4},{7,5},{8,10},{9,11},{10,... | collective-permute-start | bytes 393224 | tf_op jit(solution)/shard_map/ppermute | solution.py:24
  118.2 6.4 %collective-permute-start.54 = (bf16[16,4096]{1,0:T(8,128)(2,1)S(1)}, bf16[16,4096]{1,0:T(8,128)(2,1)S(1)}, u32[]{:S(2)}, u32[]{:S(2)}) collective-permute-start(bf16[16,4096]{1,0:T(8,128)(2,1)S(1)} %add.138), channel_id=1, source_target_pairs={{0,2},{1,3},{2,0},{3,1},{4,6},{5,7},{6,4},{7,5},{8,10},{9,11},{10,... | collective-permute-start | bytes 393224 | tf_op jit(solution)/shard_map/ppermute | solution.py:24
  120.0 6.5 %collective-permute-start.66 = (bf16[16,4096]{1,0:T(8,128)(2,1)S(1)}, bf16[16,4096]{1,0:T(8,128)(2,1)S(1)}, u32[]{:S(2)}, u32[]{:S(2)}) collective-permute-start(bf16[16,4096]{1,0:T(8,128)(2,1)S(1)} %add.149), channel_id=1, source_target_pairs={{0,2},{1,3},{2,0},{3,1},{4,6},{5,7},{6,4},{7,5},{8,10},{9,11},{10,... | collective-permute-start | bytes 393224 | tf_op jit(solution)/shard_map/ppermute | solution.py:24
  121.1 6.6 %collective-permute-start.63 = (bf16[16,4096]{1,0:T(8,128)(2,1)S(1)}, bf16[16,4096]{1,0:T(8,128)(2,1)S(1)}, u32[]{:S(2)}, u32[]{:S(2)}) collective-permute-start(bf16[16,4096]{1,0:T(8,128)(2,1)S(1)} %add_add_fusion), channel_id=1, source_target_pairs={{0,4},{1,5},{2,6},{3,7},{4,0},{5,1},{6,2},{7,3},{8,12},{9,13},{10,... | collective-permute-start | bytes 393224 | tf_op jit(solution)/shard_map/ppermute | solution.py:24
  121.5 12.5 %collective-permute-start.59 = (bf16[16,4096]{1,0:T(8,128)(2,1)S(1)}, bf16[16,4096]{1,0:T(8,128)(2,1)S(1)}, u32[]{:S(2)}, u32[]{:S(2)}) collective-permute-start(bf16[16,4096]{1,0:T(8,128)(2,1)S(1)} %add_add_fusion.1), channel_id=1, source_target_pairs={{0,8},{1,9},{2,10},{3,11},{4,12},{5,13},{6,14},{7,15},{8,0},{9,1},... | collective-permute-start | bytes 393224 | tf_op jit(solution)/shard_map/ppermute | solution.py:24
  124.6 9.4 %collective-permute-start.55 = (bf16[16,4096]{1,0:T(8,128)(2,1)S(1)}, bf16[16,4096]{1,0:T(8,128)(2,1)S(1)}, u32[]{:S(2)}, u32[]{:S(2)}) collective-permute-start(bf16[16,4096]{1,0:T(8,128)(2,1)S(1)} %add_add_fusion.2), channel_id=1, source_target_pairs={{0,12},{1,13},{2,14},{3,15},{4,8},{5,9},{6,10},{7,11},{8,4},{9,5},... | collective-permute-start | bytes 393224 | tf_op jit(solution)/shard_map/ppermute | solution.py:24
  (9 other events, 353.5 us)
